TPU v7x, 256 devices: a whole 4x4x8 slice. The times are simulated.
256 devices in a mesh: slab: 64 (over y, x_lo, z), view: 4 (over x_hi, core).
Axes of the slice: x: 4 (x_hi: 2, x_lo: 2; x = x_hi * 2 + x_lo), y: 4, z: 8, core: 2. Of those that a mesh axis runs over, the one named last changes fastest.
Arguments:
- primal: float32 [5, 256, 32, 128], P(None, 'slab', 'view'), may hold values from -6 to 6
- dual: bfloat16 [64, 256, 128], P('view', 'slab'), may hold values from -6 to 6
- footprints: bfloat16 [8, 128, 128], replicated, may hold values from -0.046875 to 0.046875
- tile_index: int32 [64, 8192, 2], P(None, 'slab'), may hold values from 0 to 3
- footprint_offset: int32 [64, 8192, 2], P(None, 'slab'), may hold values from 0 to 7
- w_first: bfloat16 [3, 3, 3, 32, 6], replicated, may hold values from -0.21875 to 0.21875
- w_middle: bfloat16 [3, 3, 3, 32, 32], replicated, may hold values from -0.21875 to 0.21875
- w_last: bfloat16 [3, 3, 3, 5, 32], replicated, may hold values from -0.5 to 0.5
- cotangent: float32 [5, 256, 32, 128], P(None, 'slab', 'view'), may hold values from -6 to 6
Outputs:
- d_primal: float32 [5, 256, 32, 128], P(None, 'slab', 'view')
- d_dual: float32 [64, 256, 128], P('view', 'slab')
- d_first: float32 [3, 3, 3, 32, 6], replicated
- d_middle: float32 [3, 3, 3, 32, 32], replicated
- d_last: float32 [3, 3, 3, 5, 32], replicated
All inputs are finite; a program needn't handle non-finite values.
Results may differ from a plain program's by a relative error of at most 0.0067.
Values may be sent and summed in bfloat16 or wider, within the bound.
No kernel may reach another device: no remote copies, remote signals or barrier semaphores. Data moves between devices by JAX's collectives and lax.ppermute only.
A program may use at most 64 MiB of HBM per device.

v0:
```python
import math

import jax
import jax.numpy as jnp
from jax import lax
from jax.sharding import PartitionSpec as P


def with_halo(cells, sides, width):
    for axis, dim in sides:
        count = lax.axis_size(axis)
        ends = count - 1
        head = lax.slice_in_dim(cells, 0, width, axis=dim)
        tail = lax.slice_in_dim(cells, cells.shape[dim] - width, cells.shape[dim], axis=dim)
        cells = jnp.concatenate(
            [
                lax.ppermute(tail, axis, [(i, (i + 1) % count) for i in range(ends)]),
                cells,
                lax.ppermute(head, axis, [((i + 1) % count, i) for i in range(ends)]),
            ],
            axis=dim,
        )
    return cells


def silu_slope(value):
    sig = jax.nn.sigmoid(value)
    return sig * (1.0 + value * (1.0 - sig))


def flipped(kernel):
    return kernel[::-1, ::-1, ::-1].transpose(0, 1, 2, 4, 3)


def sideways(padded):
    blank = jnp.zeros(padded.shape[:-1] + (1,), padded.dtype)
    left = jnp.concatenate([blank, padded[..., :-1]], axis=-1)
    right = jnp.concatenate([padded[..., 1:], blank], axis=-1)
    return (left, padded, right)


def rims(field):
    return with_halo(field, (("slab", 1), ("view", 2)), 1)


def convolve(parts, kernel, depth, rows):
    total = None
    for za in range(3):
        for yb in range(3):
            for xc in range(3):
                term = jnp.einsum(
                    "oc,czyx->ozyx",
                    kernel[za, yb, xc],
                    parts[xc][:, za : za + depth, yb : yb + rows, :],
                    preferred_element_type=jnp.float32,
                )
                total = term if total is None else total + term
    return total


def kernel_grad(dout, parts, depth, rows):
    terms = []
    for za in range(3):
        for yb in range(3):
            for xc in range(3):
                terms.append(
                    jnp.einsum(
                        "ozyx,czyx->oc",
                        dout,
                        parts[xc][:, za : za + depth, yb : yb + rows, :],
                        preferred_element_type=jnp.float32,
                    )
                )
    return jnp.stack(terms).reshape(3, 3, 3, dout.shape[0], parts[0].shape[0])


def shards(
    primal, dual, footprints, tile_index, footprint_offset, w_first, w_middle, w_last, cotangent
):
    channels, depth, rows_here, width = primal.shape
    views_here, det_tiles, bins = dual.shape
    all_views = tile_index.shape[0]
    taps = tile_index.shape[2]
    foot_count = footprints.shape[0]
    n_view = lax.axis_size("view")
    full_rows = rows_here * n_view
    x_tiles = width // bins
    view_at = lax.axis_index("view")
    forward_mat = footprints.transpose(1, 0, 2).reshape(bins, foot_count * bins)
    backward_mat = footprints.transpose(2, 0, 1).reshape(bins, foot_count * bins)
    tile_grid = tile_index.reshape(all_views, depth, full_rows, x_tiles, taps)
    foot_grid = footprint_offset.reshape(all_views, depth, full_rows, x_tiles, taps)
    stride = det_tiles * foot_count
    heights = jnp.dot(
        dual.reshape(-1, bins), forward_mat, preferred_element_type=jnp.float32
    ).reshape(-1, bins)
    own_tiles = lax.dynamic_slice_in_dim(tile_grid, view_at * views_here, views_here, 0)
    own_foot = lax.dynamic_slice_in_dim(foot_grid, view_at * views_here, views_here, 0)
    count = rows_here * lax.axis_size("view")

    def strip_add_view(view, total):
        picks = view * stride + own_tiles[view] * foot_count + own_foot[view]
        return total + jnp.take(heights, picks, axis=0).sum(axis=3)

    total = lax.fori_loop(
        0, views_here, strip_add_view, jnp.zeros((depth, count, x_tiles, bins), jnp.float32)
    )
    strips = lax.psum_scatter(
        total.reshape(depth, count, width).transpose(1, 0, 2),
        "view",
        scatter_dimension=0,
        tiled=True,
    )
    back = strips.transpose(1, 0, 2)
    x_zero = jnp.concatenate([primal, back[None]], axis=0).astype(jnp.bfloat16)
    g_low = cotangent.astype(jnp.bfloat16)
    x_parts = sideways(with_halo(x_zero, (("slab", 1), ("view", 2)), 1))
    g_parts = sideways(with_halo(g_low, (("slab", 1), ("view", 2)), 1))
    a_one = convolve(x_parts, w_first, depth, rows_here)
    z_one = jax.nn.silu(a_one).astype(jnp.bfloat16)
    z_one_parts = sideways(rims(z_one))
    a_two = convolve(z_one_parts, w_middle, depth, rows_here)
    z_two = jax.nn.silu(a_two).astype(jnp.bfloat16)
    z_two_parts = sideways(rims(z_two))
    dz_two = convolve(g_parts, flipped(w_last), depth, rows_here)
    d_last = kernel_grad(g_low, z_two_parts, depth, rows_here)
    da_two = (dz_two * silu_slope(a_two)).astype(jnp.bfloat16)
    dz_one = convolve(sideways(rims(da_two)), flipped(w_middle), depth, rows_here)
    d_middle = kernel_grad(da_two, z_one_parts, depth, rows_here)
    da_one = (dz_one * silu_slope(a_one)).astype(jnp.bfloat16)
    dx_zero = convolve(sideways(rims(da_one)), flipped(w_first), depth, rows_here)
    d_first = kernel_grad(da_one, x_parts, depth, rows_here)
    d_primal = cotangent + dx_zero[:channels]
    strip_grad = dx_zero[channels].astype(jnp.bfloat16)
    start_grad = jnp.zeros((views_here * det_tiles, bins), jnp.float32)
    piece = lax.all_gather(strip_grad, "view", axis=1, tiled=True)
    count = piece.shape[1]
    proj = jnp.dot(
        piece.reshape(-1, bins), backward_mat, preferred_element_type=jnp.float32
    ).reshape(-1, bins)
    tile_ids = jnp.arange(depth * count * x_tiles, dtype=jnp.int32).reshape(
        depth, count, x_tiles, 1
    )

    def fold_add_view(view, acc):
        source = tile_ids * foot_count + own_foot[view]
        target = view * det_tiles + own_tiles[view]
        return acc + jax.ops.segment_sum(
            jnp.take(proj, source.reshape(-1), axis=0),
            target.reshape(-1),
            num_segments=views_here * det_tiles,
        )

    d_dual = lax.fori_loop(0, views_here, fold_add_view, start_grad).reshape(
        views_here, det_tiles, bins
    )
    summed = lax.psum((d_first, d_middle, d_last), ("slab", "view"))
    scale = 1.0 / math.sqrt(depth * lax.axis_size("slab") * full_rows * width)
    return (d_primal, d_dual, summed[0] * scale, summed[1] * scale, summed[2] * scale)


def solution(mesh):
    placed = (
        P(None, "slab", "view", None),
        P("view", "slab", None),
        P(),
        P(None, "slab", None),
        P(None, "slab", None),
        P(),
        P(),
        P(),
        P(None, "slab", "view", None),
    )
    return jax.shard_map(
        shards,
        mesh=mesh,
        in_specs=placed,
        out_specs=(P(None, "slab", "view", None), P("view", "slab", None), P(), P(), P()),
        check_vma=False,
    )
```

profile of v0, /device:TPU:1, one launch (start us, length us, event | category | flops | bytes accessed | tf_op | source)
XLA Modules:
  0.0 618.3 jit_solution(12563308730298618970)
XLA Ops:
  7.3 3.5 copy.388
  15.7 21.8 %while.30 = (s32[]{:T(128)}, f32[4,32,1,128]{3,2,1,0:T(1,128)S(1)}, s32[16,4,32,1,2]{4,2,1,3,0:T(8,128)S(1)}, s32[16,4,32,1,2]{4,2,1,3,0:T(8,128)S(1)}, f32[512,...) while((s32[]{:T(128)}, f32[4,32,1,128]{3,2,1,0:T(1,128)S(1)}, ...), condition=%wide.region_2.3_spmd.clone, body=%wide.region_0.2_spmd.clone.sunk | while | flops 86788 | bytes 669307 | solution.py:105
  38.3 4.4 collective-permute-start
  47.3 6.5 %collective-permute-start.2 = (bf16[5,6,1,128]{3,2,1,0:T(2,128)(2,1)S(1)}, bf16[5,6,1,128]{3,2,1,0:T(2,128)(2,1)S(1)}, u32[]{:S(2)}, u32[]{:S(2)}) collective-permute-start(bf16[5,6,1,128]{3,2,1,0:T(2,128)(2,1)S(1)} %get-tuple-element.443), channel_id=1, source_target_pairs={{0,1},{1,2},{2,3},{4,5},{5,6},{6,7},{8,9},{9,10},{10,11},{12,13},{... | collective-permute-start | bytes 23048 | tf_op jit(solution)/shard_map/ppermute | solution.py:17
  55.7 4.6 collective-permute-done.3
  68.7 4.5 reduce-scatter.2.cloned.1.call-done
  73.9 3.2 collective-permute-start.4
  81.6 4.7 collective-permute-start.6
  88.2 4.6 collective-permute-done.7
  106.4 3.2 collective-permute-start.8
  112.3 2.9 collective-permute-done.9
  115.2 3.1 collective-permute-start.10
  120.3 4.9 collective-permute-done.11
  158.0 4.8 collective-permute-start.20
  164.1 4.3 collective-permute-start.12
  169.7 240.3 %all-reduce.15.cloned.1.call-done = f32[3,3,3,32,32]{4,3,2,1,0:T(8,128)} async-done(((f32[3,3,3,32,32]{4,3,2,1,0:T(8,128)}), f32[3,3,3,32,32]{4,3,2,1,0:T(8,128)}) %all-reduce.15.cloned.1.call-update) | async-done | bytes 110608 | tf_op jit(solution)/shard_map/psum | solution.py:157
  411.8 5.5 collective-permute-start.22
  419.3 5.1 collective-permute-start.14
  426.6 4.8 collective-permute-done.15
  453.8 80.9 %all-reduce.12 = (f32[3,3,3,32,6]{3,4,2,1,0:T(8,128)S(1)}, f32[3,3,3,5,32]{4,2,3,1,0:T(4,128)S(1)}) all-reduce(f32[3,3,3,32,6]{3,4,2,1,0:T(8,128)} %bitcast.1969, f32[3,3,3,5,32]{4,2,3,1,0:T(4,128)S(1)} %copy.582), channel_id=1, replica_groups=mesh['slab'=64,'view'=4] {'slab','view'}, use_global_device_ids=true, to_apply=%region_7.8 | all-reduce | flops 9504 | bytes 76032 | tf_op jit(solution)/shard_map/psum | solution.py:157
  535.4 3.8 collective-permute-start.18
  542.0 4.1 collective-permute-done.19
  551.5 5.6 all-gather
  557.5 53.1 %while.29 = (s32[]{:T(128)}, f32[64,128]{1,0:T(8,128)S(1)}, s32[16,4,32,1,2]{4,2,1,3,0:T(8,128)S(1)}, s32[16,4,32,1,2]{4,2,1,3,0:T(8,128)S(1)}, f32[1024,128]{1,...) while((s32[]{:T(128)}, f32[64,128]{1,0:T(8,128)S(1)}, ...), condition=%wide.region_6.7_spmd.clone.clone, body=%wide.region_4.6_spmd.clone.clone.sunk | while | flops 70019 | bytes 588653 | solution.py:154
  (751 shorter events, 190.8 us)
Async XLA Ops:
  7.2 66.0 %reduce-scatter.2.cloned.1.call-start = ((), (), s32[]{:S(2)}) async-start(), calls=%async_computation.1 | async-start | bytes 81920 | tf_op jit(solution)/shard_map/reduce_scatter | solution.py:108
  38.2 371.8 %all-reduce.15.cloned.1.call-start = ((), (), s32[]{:S(2)}) async-start(), calls=%async_computation.2 | async-start | bytes 884736 | tf_op jit(solution)/shard_map/psum | solution.py:157
  38.3 6.6 %collective-permute-start = (bf16[5,1,8,128]{3,2,1,0:T(8,128)(2,1)S(1)}, bf16[5,1,8,128]{3,2,1,0:T(8,128)(2,1)S(1)}, u32[]{:S(2)}, u32[]{:S(2)}) collective-permute-start(bf16[5,1,8,128]{3,2,1,0:T(8,128)(2,1)S(1)} %get-tuple-element.452), channel_id=1, source_target_pairs={{0,4},{4,8},{8,12},{12,16},{16,20},{20,24},{24,28},{28,32},{32,36}... | collective-permute-start | bytes 30728 | tf_op jit(solution)/shard_map/ppermute | solution.py:17
  47.3 8.4 %collective-permute-start.2 = (bf16[5,6,1,128]{3,2,1,0:T(2,128)(2,1)S(1)}, bf16[5,6,1,128]{3,2,1,0:T(2,128)(2,1)S(1)}, u32[]{:S(2)}, u32[]{:S(2)}) collective-permute-start(bf16[5,6,1,128]{3,2,1,0:T(2,128)(2,1)S(1)} %get-tuple-element.443), channel_id=1, source_target_pairs={{0,1},{1,2},{2,3},{4,5},{5,6},{6,7},{8,9},{9,10},{10,11},{12,13},{... | collective-permute-start | bytes 23048 | tf_op jit(solution)/shard_map/ppermute | solution.py:17
  53.7 6.6 %collective-permute-start.3 = (bf16[5,6,1,128]{3,2,1,0:T(2,128)(2,1)S(1)}, bf16[5,6,1,128]{3,2,1,0:T(2,128)(2,1)S(1)}, u32[]{:S(2)}, u32[]{:S(2)}) collective-permute-start(bf16[5,6,1,128]{3,2,1,0:T(2,128)(2,1)S(1)} %get-tuple-element.444), channel_id=1, source_target_pairs={{1,0},{2,1},{3,2},{5,4},{6,5},{7,6},{9,8},{10,9},{11,10},{13,12},{... | collective-permute-start | bytes 23048 | tf_op jit(solution)/shard_map/ppermute | solution.py:19
  73.9 5.5 collective-permute-start.4
  81.6 6.7 %collective-permute-start.6 = (bf16[6,6,1,128]{3,2,1,0:T(2,128)(2,1)S(1)}, bf16[6,6,1,128]{3,2,1,0:T(2,128)(2,1)S(1)}, u32[]{:S(2)}, u32[]{:S(2)}) collective-permute-start(bf16[6,6,1,128]{3,2,1,0:T(2,128)(2,1)S(1)} %get-tuple-element.440), channel_id=1, source_target_pairs={{0,1},{1,2},{2,3},{4,5},{5,6},{6,7},{8,9},{9,10},{10,11},{12,13},{... | collective-permute-start | bytes 27656 | tf_op jit(solution)/shard_map/ppermute | solution.py:17
  86.3 6.6 %collective-permute-start.7 = (bf16[6,6,1,128]{3,2,1,0:T(2,128)(2,1)S(1)}, bf16[6,6,1,128]{3,2,1,0:T(2,128)(2,1)S(1)}, u32[]{:S(2)}, u32[]{:S(2)}) collective-permute-start(bf16[6,6,1,128]{3,2,1,0:T(2,128)(2,1)S(1)} %get-tuple-element.439), channel_id=1, source_target_pairs={{1,0},{2,1},{3,2},{5,4},{6,5},{7,6},{9,8},{10,9},{11,10},{13,12},{... | collective-permute-start | bytes 27656 | tf_op jit(solution)/shard_map/ppermute | solution.py:19
  106.4 5.9 collective-permute-start.8
  109.6 5.6 collective-permute-start.9
  115.2 5.1 collective-permute-start.10
  118.3 6.9 %collective-permute-start.11 = (bf16[32,6,1,128]{3,0,2,1:T(8,128)(2,1)S(1)}, bf16[32,6,1,128]{3,0,2,1:T(8,128)(2,1)S(1)}, u32[]{:S(2)}, u32[]{:S(2)}) collective-permute-start(bf16[32,6,1,128]{3,0,2,1:T(8,128)(2,1)S(1)} %get-tuple-element.372), channel_id=1, source_target_pairs={{1,0},{2,1},{3,2},{5,4},{6,5},{7,6},{9,8},{10,9},{11,10},{13,12},{... | collective-permute-start | bytes 147464 | tf_op jit(solution)/shard_map/ppermute | solution.py:19
  158.0 253.8 %collective-permute-start.20 = (bf16[32,1,8,128]{3,0,2,1:T(8,128)(2,1)}, bf16[32,1,8,128]{3,0,2,1:T(8,128)(2,1)S(1)}, u32[]{:S(2)}, u32[]{:S(2)}) collective-permute-start(bf16[32,1,8,128]{3,0,2,1:T(8,128)(2,1)} %get-tuple-element.375), channel_id=1, source_target_pairs={{0,4},{4,8},{8,12},{12,16},{16,20},{20,24},{24,28},{28,32},{32,36}... | collective-permute-start | bytes 196616 | tf_op jit(solution)/shard_map/ppermute | solution.py:17
  162.8 249.0 %collective-permute-start.21 = (bf16[32,1,8,128]{3,0,2,1:T(8,128)(2,1)}, bf16[32,1,8,128]{3,0,2,1:T(8,128)(2,1)S(1)}, u32[]{:S(2)}, u32[]{:S(2)}) collective-permute-start(bf16[32,1,8,128]{3,0,2,1:T(8,128)(2,1)} %get-tuple-element.376), channel_id=1, source_target_pairs={{4,0},{8,4},{12,8},{16,12},{20,16},{24,20},{28,24},{32,28},{36,32}... | collective-permute-start | bytes 196616 | tf_op jit(solution)/shard_map/ppermute | solution.py:19
  164.1 255.2 %collective-permute-start.12 = (bf16[32,1,8,128]{3,0,2,1:T(8,128)(2,1)}, bf16[32,1,8,128]{3,0,2,1:T(8,128)(2,1)S(1)}, u32[]{:S(2)}, u32[]{:S(2)}) collective-permute-start(bf16[32,1,8,128]{3,0,2,1:T(8,128)(2,1)} %get-tuple-element.379), channel_id=1, source_target_pairs={{0,4},{4,8},{8,12},{12,16},{16,20},{20,24},{24,28},{28,32},{32,36}... | collective-permute-start | bytes 196616 | tf_op jit(solution)/shard_map/ppermute | solution.py:17
  168.4 250.9 %collective-permute-start.13 = (bf16[32,1,8,128]{3,0,2,1:T(8,128)(2,1)}, bf16[32,1,8,128]{3,0,2,1:T(8,128)(2,1)S(1)}, u32[]{:S(2)}, u32[]{:S(2)}) collective-permute-start(bf16[32,1,8,128]{3,0,2,1:T(8,128)(2,1)} %get-tuple-element.380), channel_id=1, source_target_pairs={{4,0},{8,4},{12,8},{16,12},{20,16},{24,20},{28,24},{32,28},{36,32}... | collective-permute-start | bytes 196616 | tf_op jit(solution)/shard_map/ppermute | solution.py:19
  411.8 27.3 %collective-permute-start.22 = (bf16[32,6,1,128]{3,0,2,1:T(8,128)(2,1)S(1)}, bf16[32,6,1,128]{3,0,2,1:T(8,128)(2,1)S(1)}, u32[]{:S(2)}, u32[]{:S(2)}) collective-permute-start(bf16[32,6,1,128]{3,0,2,1:T(8,128)(2,1)S(1)} %get-tuple-element.361), channel_id=1, source_target_pairs={{0,1},{1,2},{2,3},{4,5},{5,6},{6,7},{8,9},{9,10},{10,11},{12,13},{... | collective-permute-start | bytes 147464 | tf_op jit(solution)/shard_map/ppermute | solution.py:17
  417.3 21.8 %collective-permute-start.23 = (bf16[32,6,1,128]{3,0,2,1:T(8,128)(2,1)S(1)}, bf16[32,6,1,128]{3,0,2,1:T(8,128)(2,1)S(1)}, u32[]{:S(2)}, u32[]{:S(2)}) collective-permute-start(bf16[32,6,1,128]{3,0,2,1:T(8,128)(2,1)S(1)} %get-tuple-element.362), channel_id=1, source_target_pairs={{1,0},{2,1},{3,2},{5,4},{6,5},{7,6},{9,8},{10,9},{11,10},{13,12},{... | collective-permute-start | bytes 147464 | tf_op jit(solution)/shard_map/ppermute | solution.py:19
  419.3 7.3 %collective-permute-start.14 = (bf16[32,6,1,128]{3,0,2,1:T(8,128)(2,1)S(1)}, bf16[32,6,1,128]{3,0,2,1:T(8,128)(2,1)S(1)}, u32[]{:S(2)}, u32[]{:S(2)}) collective-permute-start(bf16[32,6,1,128]{3,0,2,1:T(8,128)(2,1)S(1)} %get-tuple-element.367), channel_id=1, source_target_pairs={{0,1},{1,2},{2,3},{4,5},{5,6},{6,7},{8,9},{9,10},{10,11},{12,13},{... | collective-permute-start | bytes 147464 | tf_op jit(solution)/shard_map/ppermute | solution.py:17
  424.5 6.9 %collective-permute-start.15 = (bf16[32,6,1,128]{3,0,2,1:T(8,128)(2,1)S(1)}, bf16[32,6,1,128]{3,0,2,1:T(8,128)(2,1)S(1)}, u32[]{:S(2)}, u32[]{:S(2)}) collective-permute-start(bf16[32,6,1,128]{3,0,2,1:T(8,128)(2,1)S(1)} %get-tuple-element.368), channel_id=1, source_target_pairs={{1,0},{2,1},{3,2},{5,4},{6,5},{7,6},{9,8},{10,9},{11,10},{13,12},{... | collective-permute-start | bytes 147464 | tf_op jit(solution)/shard_map/ppermute | solution.py:19
  450.9 84.5 %collective-permute-start.16 = (bf16[32,1,8,128]{3,0,2,1:T(8,128)(2,1)}, bf16[32,1,8,128]{3,0,2,1:T(8,128)(2,1)S(1)}, u32[]{:S(2)}, u32[]{:S(2)}) collective-permute-start(bf16[32,1,8,128]{3,0,2,1:T(8,128)(2,1)} %get-tuple-element.377), channel_id=1, source_target_pairs={{0,4},{4,8},{8,12},{12,16},{16,20},{20,24},{24,28},{28,32},{32,36}... | collective-permute-start | bytes 196616 | tf_op jit(solution)/shard_map/ppermute | solution.py:17
  452.3 83.0 %collective-permute-start.17 = (bf16[32,1,8,128]{3,0,2,1:T(8,128)(2,1)}, bf16[32,1,8,128]{3,0,2,1:T(8,128)(2,1)S(1)}, u32[]{:S(2)}, u32[]{:S(2)}) collective-permute-start(bf16[32,1,8,128]{3,0,2,1:T(8,128)(2,1)} %get-tuple-element.378), channel_id=1, source_target_pairs={{4,0},{8,4},{12,8},{16,12},{20,16},{24,20},{28,24},{32,28},{36,32}... | collective-permute-start | bytes 196616 | tf_op jit(solution)/shard_map/ppermute | solution.py:19
  535.4 6.6 %collective-permute-start.18 = (bf16[32,6,1,128]{3,0,2,1:T(8,128)(2,1)S(1)}, bf16[32,6,1,128]{3,0,2,1:T(8,128)(2,1)S(1)}, u32[]{:S(2)}, u32[]{:S(2)}) collective-permute-start(bf16[32,6,1,128]{3,0,2,1:T(8,128)(2,1)S(1)} %get-tuple-element.363), channel_id=1, source_target_pairs={{0,1},{1,2},{2,3},{4,5},{5,6},{6,7},{8,9},{9,10},{10,11},{12,13},{... | collective-permute-start | bytes 147464 | tf_op jit(solution)/shard_map/ppermute | solution.py:17
  539.2 6.9 %collective-permute-start.19 = (bf16[32,6,1,128]{3,0,2,1:T(8,128)(2,1)S(1)}, bf16[32,6,1,128]{3,0,2,1:T(8,128)(2,1)S(1)}, u32[]{:S(2)}, u32[]{:S(2)}) collective-permute-start(bf16[32,6,1,128]{3,0,2,1:T(8,128)(2,1)S(1)} %get-tuple-element.364), channel_id=1, source_target_pairs={{1,0},{2,1},{3,2},{5,4},{6,5},{7,6},{9,8},{10,9},{11,10},{13,12},{... | collective-permute-start | bytes 147464 | tf_op jit(solution)/shard_map/ppermute | solution.py:19
  (64 other events, 520.1 us)
Sparse Core Ops, SparseCore 0:
  38.3 34.8 reduce-scatter.1
  157.4 252.5 all-reduce.14
where the time goes:
time: 628 us; the launch traced here: 618 us
  waiting for transfers between devices  275 us (44%)
  blocking collectives  86.5 us (14%)
  matrix products  72.4 us (12%)
  starting transfers between devices  70.2 us (11%)
  other arithmetic  51.7 us (8%)
  local copies, waits for them, and re-layouts  44 us (7%)
  between operations  16.3 us (3%)
    psum x1, waiting for transfers between devices, shards(): summed = lax.psum((d_first, d_middle, d_last), ('slab', 'view'))  240 us
    psum x1, blocking collectives, shards(): summed = lax.psum((d_first, d_middle, d_last), ('slab', 'view'))  80.9 us
    ppermute x12, starting transfers between devices, with_halo(): lax.ppermute(tail, axis, [(i, (i + 1) % count) for i in range(ends)])  50 us
    dot_general x135, matrix products, convolve(): jnp.einsum('oc,czyx->ozyx', kernel[za, yb, xc], parts[xc][:, za:za + dept...  40 us
    scatter-add x16, other arithmetic, fold_add_view(): jax.ops.segment_sum(jnp.take(proj, source.reshape(-1), axis=0), target.re...  38.8 us
    dot_general x81, matrix products, kernel_grad(): jnp.einsum('ozyx,czyx->oc', dout, parts[xc][:, za:za + depth, yb:yb + row...  31.9 us
    ppermute x12, waiting for transfers between devices, with_halo(): lax.ppermute(head, axis, [((i + 1) % count, i) for i in range(ends)])  30.4 us
    ppermute x12, starting transfers between devices, with_halo(): lax.ppermute(head, axis, [((i + 1) % count, i) for i in range(ends)])  20.1 us
  transfers between devices with their start and end apart: 26, of which 10 were waited for; matrix products, arithmetic and copies ran while one was open for 4% of the time, Pallas kernels for 0%

commit v1 on v0

v1 whole, which is shorter than its diff:
```python
import math

import jax
import jax.numpy as jnp
from jax import lax
from jax.experimental import pallas as pl
from jax.experimental.pallas import tpu as pltpu
from jax.sharding import PartitionSpec as P

F32 = jnp.float32
BF16 = jnp.bfloat16
INTERPRET = False
PARAMS = pltpu.CompilerParams(vmem_limit_bytes=48 << 20)

CZ = 4
RY = 8
REACH = 4
WY = RY + 2 * REACH
LANES = 128
HID = 32
SLOT = 16
DTL = 4


def smem_spec():
    return pl.BlockSpec(memory_space=pltpu.SMEM)


def vmem_spec():
    return pl.BlockSpec(memory_space=pltpu.VMEM)


def gather_kernel(meta, packed, tiles, foots, prints, out, codes, duals, field, rows):
    view_at = meta[0]
    foot_count = prints.shape[0]
    views = tiles.shape[0] // 2
    codes[...] = (tiles[...] * foot_count + foots[...]).astype(F32)
    by_tap = jnp.concatenate(
        [codes[pl.ds(0, views, stride=2), :], codes[pl.ds(1, views, stride=2), :]], axis=0
    )
    by_tile = by_tap.T
    ranks = packed.shape[0]
    local = views // ranks * DTL
    for d in range(ranks):
        duals[d * local : (d + 1) * local, :] = packed[d, 320 : 320 + local, :].astype(F32)
    stack = []
    for g in range(DTL):
        one = duals[pl.ds(g, views, stride=DTL), :].astype(BF16)
        stack += [one, one]
    dual_rows = jnp.concatenate(stack, axis=0)
    back = jnp.zeros((by_tile.shape[0], LANES), F32)
    for o in range(foot_count):
        counts = jnp.concatenate(
            [
                jnp.where(by_tile == float(g * foot_count + o), 1.0, 0.0).astype(BF16)
                for g in range(DTL)
            ],
            axis=1,
        )
        part = jnp.dot(counts, dual_rows, preferred_element_type=F32)
        high = part.astype(BF16)
        low = (part - high.astype(F32)).astype(BF16)
        back = back + jnp.dot(high, prints[o], preferred_element_type=F32)
        back = back + jnp.dot(low, prints[o], preferred_element_type=F32)
    field[...] = back

    rows[...] = jnp.zeros(rows.shape, F32)
    before = jnp.maximum(view_at - 1, 0)
    after = jnp.minimum(view_at + 1, ranks - 1)
    has_before = view_at > 0
    has_after = view_at < ranks - 1
    full_y = RY * ranks

    def place(z, slot, mid, low_side, high_side):
        base = z * WY * SLOT + slot
        rows[pl.ds(base, REACH, stride=SLOT), :] = jnp.where(has_before, low_side[RY - REACH :], 0.0)
        rows[pl.ds(base + REACH * SLOT, RY, stride=SLOT), :] = mid
        rows[pl.ds(base + (REACH + RY) * SLOT, REACH, stride=SLOT), :] = jnp.where(
            has_after, high_side[:REACH], 0.0
        )

    for c in range(10):
        slot = c if c < 5 else c + 3
        mid = packed[view_at, c * 32 : c * 32 + 32, :].astype(F32)
        low_side = packed[before, c * 32 : c * 32 + 32, :].astype(F32)
        high_side = packed[after, c * 32 : c * 32 + 32, :].astype(F32)
        for z in range(CZ):
            cut = slice(z * RY, z * RY + RY)
            place(z, slot, mid[cut], low_side[cut], high_side[cut])
    for z in range(CZ):
        at = lambda rank: field[pl.ds(pl.multiple_of(z * full_y + rank * RY, RY), RY), :]
        place(z, 5, at(view_at), at(before), at(after))
    out[...] = rows[...].reshape(out.shape).astype(BF16)


def lane_masks(shape):
    lane = lax.broadcasted_iota(jnp.int32, shape, 1)
    return lane == 0, lane == LANES - 1


def shifted(value, first, last):
    left = jnp.where(first, 0.0, pltpu.roll(value, 1, 1))
    right = jnp.where(last, 0.0, pltpu.roll(value, LANES - 1, 1))
    return left, value, right


def shift_sum(taps, first, last):
    step = taps.shape[0] // 3
    left = jnp.where(first, 0.0, pltpu.roll(taps[:step], 1, 1))
    right = jnp.where(last, 0.0, pltpu.roll(taps[2 * step :], LANES - 1, 1))
    return taps[step : 2 * step] + left + right


def window(ref, width, z, y):
    sides = []
    for ahead in range(2):
        sides.append(
            jnp.concatenate(
                [ref[(z + a) * width + y + ahead + b] for a in range(3) for b in range(3)], axis=0
            )
        )
    return jnp.concatenate(sides, axis=1)


def net_kernel(
    meta, prev, here, following, cot, w_in, w_mid, w_mid_flip, w_first_flip,
    d_primal, strip, grads,
    box, slope, dz_two, z_one, z_two, da_two, da_one, dx,
):
    slab_at, view_at, slabs, ranks = meta[0], meta[1], meta[2], meta[3]
    per = CZ * WY
    box[0:per] = jnp.where(slab_at > 0, prev[...], jnp.zeros_like(prev[...]))
    box[per : 2 * per] = here[...]
    box[2 * per : 3 * per] = jnp.where(
        slab_at < slabs - 1, following[...], jnp.zeros_like(following[...])
    )
    first, last = lane_masks((HID, LANES))
    z_start, y_start = slab_at * CZ, view_at * RY
    z_end, y_end = slabs * CZ, ranks * RY

    def inside(z, y, reach):
        zz, yy = z_start - reach + z, y_start - reach + y
        return (zz >= 0) & (zz < z_end) & (yy >= 0) & (yy < y_end)

    def sigmoid(value):
        return 0.5 * jnp.tanh(0.5 * value) + 0.5

    depth3, rows3 = CZ + 6, RY + 6
    depth2, rows2 = CZ + 4, RY + 4
    depth1, rows1 = CZ + 2, RY + 2

    def layer_one(z, carry):
        for y in range(0, rows3, 2):
            taps = jnp.dot(w_in[...], window(box, WY, z, y), preferred_element_type=F32)
            for s in range(2):
                half = taps[:, s * LANES : (s + 1) * LANES]
                value = shift_sum(half[: 3 * HID], first, last)
                sig = sigmoid(value)
                at = z * rows3 + y + s
                z_one[at] = jnp.where(inside(z, y + s, 3), value * sig, 0.0).astype(BF16)
                slope[at] = sig * (1.0 + value * (1.0 - sig))
                dz_two[at] = shift_sum(half[3 * HID :], first, last)
        return carry

    lax.fori_loop(0, depth3, layer_one, 0)

    def layer_two(z, carry):
        for y in range(0, rows2, 2):
            taps = jnp.dot(w_mid[...], window(z_one, rows3, z, y), preferred_element_type=F32)
            for s in range(2):
                value = shift_sum(taps[:, s * LANES : (s + 1) * LANES], first, last)
                sig = sigmoid(value)
                at = z * rows2 + y + s
                z_two[at] = (value * sig).astype(BF16)
                grad = dz_two[(z + 1) * rows3 + y + s + 1] * (sig * (1.0 + value * (1.0 - sig)))
                da_two[at] = jnp.where(inside(z, y + s, 2), grad, 0.0).astype(BF16)
        return carry

    lax.fori_loop(0, depth2, layer_two, 0)

    def layer_back(z, carry):
        for y in range(0, rows1, 2):
            taps = jnp.dot(w_mid_flip[...], window(da_two, rows2, z, y), preferred_element_type=F32)
            for s in range(2):
                value = shift_sum(taps[:, s * LANES : (s + 1) * LANES], first, last)
                grad = value * slope[(z + 2) * rows3 + y + s + 2]
                da_one[z * rows1 + y + s] = jnp.where(inside(z, y + s, 1), grad, 0.0).astype(BF16)
        return carry

    lax.fori_loop(0, depth1, layer_back, 0)

    first8, last8 = lane_masks((8, LANES))
    grads[...] = jnp.zeros(grads.shape, F32)

    def layer_out(z, carry):
        for y in range(0, RY, 2):
            taps = jnp.dot(w_first_flip[...], window(da_one, rows1, z, y), preferred_element_type=F32)
            for s in range(2):
                at = pl.multiple_of((z * RY + y + s) * 8, 8)
                dx[pl.ds(at, 8), :] = shift_sum(taps[:, s * LANES : (s + 1) * LANES], first8, last8)
        blank = jnp.zeros((HID, LANES), BF16)
        ends, mids, low, mid = [], [], [], []
        for y in range(0, RY, 2):
            low.append(window(box, WY, z + 3, y + 3))
            mid.append(window(da_two, rows2, z + 1, y + 1))
            for s in range(2):
                one = da_one[(z + 1) * rows1 + y + s + 1].astype(F32)
                two = z_two[(z + 2) * rows2 + y + s + 2].astype(F32)
                inner = z_one[(z + 3) * rows3 + y + s + 3].astype(F32)
                back = lambda v: [p.astype(BF16) for p in shifted(v, first, last)[::-1]]
                ends.append(jnp.concatenate(back(one) + [blank] + back(two) + [blank], axis=0))
                mids.append(jnp.concatenate(back(inner) + [blank], axis=0))
        contract = (((1,), (1,)), ((), ()))
        out = lax.dot_general(
            jnp.concatenate(low, axis=1), jnp.concatenate(ends, axis=1), contract,
            preferred_element_type=F32,
        )
        for tap in range(9):
            x_rows = slice(tap * SLOT, tap * SLOT + 8)
            g_rows = slice(tap * SLOT + 8, tap * SLOT + 16)
            grads[288 + tap * SLOT : 288 + tap * SLOT + 8, :] += out[x_rows, :LANES]
            grads[288 + tap * SLOT + 8 : 288 + tap * SLOT + 16, :] += out[g_rows, LANES:]
        grads[0:288, :] += lax.dot_general(
            jnp.concatenate(mid, axis=1), jnp.concatenate(mids, axis=1), contract,
            preferred_element_type=F32,
        )
        return carry

    lax.fori_loop(0, CZ, layer_out, 0)

    for z in range(CZ):
        for c in range(5):
            d_primal[c, z] = cot[c, z] + dx[pl.ds(z * RY * 8 + c, RY, stride=8), :]
        strip[z * RY : (z + 1) * RY, :] = dx[pl.ds(z * RY * 8 + 5, RY, stride=8), :]


def dual_kernel(meta, strips, tiles, foots, prints, out, codes):
    view_at = meta[0]
    foot_count = prints.shape[0]
    ranks = strips.shape[0]
    views = tiles.shape[0] // 2 // ranks
    own = pl.ds(pl.multiple_of(view_at * views * 2, views * 2), views * 2)
    codes[...] = (tiles[own, :] * foot_count + foots[own, :]).astype(F32)
    taps = [codes[pl.ds(k, views, stride=2), :] for k in range(2)]
    pieces = [strips[d].astype(F32) for d in range(ranks)]
    field = jnp.concatenate(
        [pieces[d][z * RY : (z + 1) * RY] for z in range(CZ) for d in range(ranks)], axis=0
    ).astype(BF16)
    total = jnp.zeros((DTL * views, LANES), F32)
    contract = (((1,), (1,)), ((), ()))
    for o in range(foot_count):
        counts = jnp.concatenate(
            [
                sum(jnp.where(tap == float(g * foot_count + o), 1.0, 0.0) for tap in taps)
                for g in range(DTL)
            ],
            axis=0,
        ).astype(BF16)
        part = jnp.dot(counts, field, preferred_element_type=F32)
        high = part.astype(BF16)
        low = (part - high.astype(F32)).astype(BF16)
        both = lax.dot_general(
            jnp.concatenate([high, low], axis=0), prints[o], contract, preferred_element_type=F32
        )
        total = total + both[: DTL * views] + both[DTL * views :]
    for g in range(DTL):
        out[pl.ds(g, views, stride=DTL), :] = total[g * views : (g + 1) * views]


def split_kernel(scale, packed, d_first, d_middle, d_last):
    values = packed[0:432, :] * scale
    for shift in range(3):
        moved = values if shift == 0 else pltpu.roll(values, LANES - shift * HID, 1)
        for a in range(3):
            for b in range(3):
                tap = a * 3 + b
                d_middle[2 - a, 2 - b, 2 - shift] = moved[tap * HID : (tap + 1) * HID, :HID]
                at = 288 + tap * SLOT
                d_first[a, b, shift] = moved[at : at + 6, :HID]
                d_last[2 - a, 2 - b, 2 - shift] = moved[at + 8 : at + 13, :HID]


def split_call(scale):
    def kernel(*refs):
        split_kernel(scale, *refs)

    return kernel


def flipped(kernel):
    return kernel[::-1, ::-1, ::-1].transpose(0, 1, 2, 4, 3)


def by_rows(kernel, inputs_to, outputs_to, shift=0):
    o, i = kernel.shape[3], kernel.shape[4]
    kernel = jnp.pad(
        kernel, ((0, 0), (0, 0), (0, 0), (0, outputs_to - o), (shift, inputs_to - i - shift))
    )
    return kernel.transpose(2, 3, 0, 1, 4).reshape(3 * outputs_to, 9 * inputs_to)


def shards(
    primal, dual, footprints, tile_index, footprint_offset, w_first, w_middle, w_last, cotangent
):
    views_here, det_tiles, bins = dual.shape
    all_views, tiles_here, taps = tile_index.shape
    ranks = lax.axis_size("view")
    slabs = lax.axis_size("slab")
    devices = ranks * slabs
    view_at = lax.axis_index("view")
    slab_at = lax.axis_index("slab")
    meta = jnp.stack([view_at]).astype(jnp.int32)
    meta_net = jnp.stack([slab_at, view_at, slabs, ranks]).astype(jnp.int32)
    flat = lambda idx: idx.transpose(0, 2, 1).reshape(all_views * taps, tiles_here)
    tiles, foots = flat(tile_index), flat(footprint_offset)

    packed = jnp.concatenate(
        [
            primal.astype(BF16).reshape(160, LANES),
            cotangent.astype(BF16).reshape(160, LANES),
            dual.reshape(views_here * det_tiles, LANES),
        ],
        axis=0,
    )
    packed = lax.all_gather(packed, "view", axis=0, tiled=False)

    here = pl.pallas_call(
        gather_kernel,
        out_shape=jax.ShapeDtypeStruct((CZ * WY, SLOT, LANES), BF16),
        in_specs=[smem_spec()] + [vmem_spec()] * 4,
        out_specs=vmem_spec(),
        scratch_shapes=[
            pltpu.VMEM((all_views * taps, tiles_here), F32),
            pltpu.VMEM((all_views * det_tiles, LANES), F32),
            pltpu.VMEM((tiles_here, LANES), F32),
            pltpu.VMEM((CZ * WY * SLOT, LANES), F32),
        ],
        compiler_params=PARAMS,
        interpret=INTERPRET,
        name="box_rows",
    )(meta, packed, tiles, foots, footprints)

    prev = lax.ppermute(here, "slab", [(i, (i + 1) % slabs) for i in range(slabs)])
    following = lax.ppermute(here, "slab", [((i + 1) % slabs, i) for i in range(slabs)])

    w_in = jnp.concatenate(
        [by_rows(w_first, SLOT, HID), by_rows(flipped(w_last), SLOT, HID, 8)], axis=0
    )
    w_mid = by_rows(w_middle, HID, HID)
    w_mid_flip = by_rows(flipped(w_middle), HID, HID)
    w_first_flip = by_rows(flipped(w_first), HID, 8)

    rows3, rows2, rows1 = 140, 96, 60
    d_primal, strip, grads = pl.pallas_call(
        net_kernel,
        out_shape=(
            jax.ShapeDtypeStruct(primal.shape, F32),
            jax.ShapeDtypeStruct((CZ * RY, LANES), F32),
            jax.ShapeDtypeStruct((2 * devices if devices >= 216 else 32 * devices, LANES), F32),
        ),
        in_specs=[smem_spec()] + [vmem_spec()] * 8,
        out_specs=(vmem_spec(),) * 3,
        scratch_shapes=[
            pltpu.VMEM((3 * CZ * WY, SLOT, LANES), BF16),
            pltpu.VMEM((rows3, HID, LANES), F32),
            pltpu.VMEM((rows3, HID, LANES), F32),
            pltpu.VMEM((rows3, HID, LANES), BF16),
            pltpu.VMEM((rows2, HID, LANES), BF16),
            pltpu.VMEM((rows2, HID, LANES), BF16),
            pltpu.VMEM((rows1, HID, LANES), BF16),
            pltpu.VMEM((CZ * RY * 8, LANES), F32),
        ],
        compiler_params=PARAMS,
        interpret=INTERPRET,
        name="net_box",
    )(meta_net, prev, here, following, cotangent, w_in, w_mid, w_mid_flip, w_first_flip)

    strip = strip.astype(BF16)
    ring = lambda step: [(i, (i + step) % ranks) for i in range(ranks)]
    others = [lax.ppermute(strip, "view", ring(step)) for step in range(1, ranks)]

    both = ("slab", "view")
    per = grads.shape[0] // devices
    shares = lax.all_to_all(grads.reshape(devices, per, LANES), both, 0, 0, tiled=True)
    summed = shares.sum(axis=0)
    whole = lax.all_to_all(
        jnp.broadcast_to(summed[None], shares.shape), both, 0, 0, tiled=True
    ).reshape(grads.shape)

    arrived = jnp.stack([strip] + others)
    order = (view_at - jnp.arange(ranks)) % ranks
    strips = jnp.take(arrived, order, axis=0)
    d_dual = pl.pallas_call(
        dual_kernel,
        out_shape=jax.ShapeDtypeStruct((views_here * det_tiles, LANES), F32),
        in_specs=[smem_spec()] + [vmem_spec()] * 4,
        out_specs=vmem_spec(),
        scratch_shapes=[pltpu.VMEM((views_here * taps, tiles_here), F32)],
        compiler_params=PARAMS,
        interpret=INTERPRET,
        name="dual_views",
    )(meta, strips, tiles, foots, footprints)

    full = slabs * CZ * ranks * RY * LANES
    d_first, d_middle, d_last = pl.pallas_call(
        split_call(1.0 / math.sqrt(full)),
        out_shape=(
            jax.ShapeDtypeStruct((3, 3, 3, 6, HID), F32),
            jax.ShapeDtypeStruct((3, 3, 3, HID, HID), F32),
            jax.ShapeDtypeStruct((3, 3, 3, 5, HID), F32),
        ),
        in_specs=[vmem_spec()],
        out_specs=(vmem_spec(),) * 3,
        compiler_params=PARAMS,
        interpret=INTERPRET,
        name="split_grads",
    )(whole)
    return (
        d_primal,
        d_dual.reshape(dual.shape),
        d_first.transpose(0, 1, 2, 4, 3),
        d_middle,
        d_last,
    )


def solution(mesh):
    placed = (
        P(None, "slab", "view", None),
        P("view", "slab", None),
        P(),
        P(None, "slab", None),
        P(None, "slab", None),
        P(),
        P(),
        P(),
        P(None, "slab", "view", None),
    )
    return jax.shard_map(
        shards,
        mesh=mesh,
        in_specs=placed,
        out_specs=(P(None, "slab", "view", None), P("view", "slab", None), P(), P(), P()),
        check_vma=False,
    )
```

time: 628 us -> 92 us (0.15); the launches traced: 618 us -> 91.7 us
  waiting for transfers between devices: 275 us -> 27.9 us
  blocking collectives: 86.5 us -> 10.8 us
  matrix products: 72.4 us -> 0 us
  other arithmetic: 51.7 us -> 1.44 us
  starting transfers between devices: 70.2 us -> 27.7 us
  local copies, waits for them, and re-layouts: 44 us -> 5.05 us
  Pallas kernels: 0 us -> 17.9 us
  between operations: 16.3 us -> 0.9 us
    psum x1 -> x0, waiting for transfers between devices: 240 us -> none  [shards(): summed = lax.psum((d_first, d_middle, d_last), ('slab', 'view'))]
    psum x1 -> x0, blocking collectives: 80.9 us -> none  [shards(): summed = lax.psum((d_first, d_middle, d_last), ('slab', 'view'))]
    dot_general x218 -> x0, matrix products: 72.4 us -> none  [the longest x135 40 us: convolve(): jnp.einsum('oc,czyx->ozyx', kernel[za, yb, xc], parts[xc][:, za:za + dept...]
    ppermute x24 -> x5, starting transfers between devices: 70.1 us -> 12.5 us  [the longest x1 7.06 us: shards(): lax.ppermute(here, 'slab', [((i + 1) % slabs, i) for i in range(slabs)])]
    scatter-add x16 -> x0, other arithmetic: 38.8 us -> none  [fold_add_view(): jax.ops.segment_sum(jnp.take(proj, source.reshape(-1), axis=0), target.re...]
    ppermute x24 -> x5, waiting for transfers between devices: 30.4 us -> 3.91 us  [the longest x1 3.9 us: shards(): lax.ppermute(here, 'slab', [(i, (i + 1) % slabs) for i in range(slabs)])]
    all_to_all x0 -> x2, waiting for transfers between devices: none -> 24 us  [the longest x1 13.6 us: shards(): lax.all_to_all(jnp.broadcast_to(summed[None], shares.shape), both, 0, 0,...]
    pallas_call x0 -> x4, Pallas kernels: none -> 17.9 us  [the longest x1 14.3 us: shards(): pl.pallas_call(net_kernel, out_shape=(jax.ShapeDtypeStruct(primal.shape,...]
  transfers between devices with their start and end apart: 26 -> 7, of which waited for: 10 -> 3; matrix products, arithmetic and copies ran while one was open for 4% -> 4% of each run, Pallas kernels for 0% -> 1%
where the time goes in v1:
time: 92 us; the launch traced here: 91.7 us
  waiting for transfers between devices  27.9 us (30%)
  starting transfers between devices  27.7 us (30%)
  Pallas kernels  17.9 us (19%)
  blocking collectives  10.8 us (12%)
  local copies, waits for them, and re-layouts  5.05 us (5%)
  other arithmetic  1.44 us (2%)
    pallas_call x1, Pallas kernels, shards(): pl.pallas_call(net_kernel, out_shape=(jax.ShapeDtypeStruct(primal.shape,...  14.3 us
    all_to_all x1, waiting for transfers between devices, shards(): lax.all_to_all(jnp.broadcast_to(summed[None], shares.shape), both, 0, 0,...  13.6 us
    all_gather x1, blocking collectives, shards(): packed = lax.all_gather(packed, 'view', axis=0, tiled=False)  10.8 us
    all_to_all x1, waiting for transfers between devices, shards(): lax.all_to_all(grads.reshape(devices, per, LANES), both, 0, 0, tiled=True)  10.4 us
    all_to_all x1, starting transfers between devices, shards(): lax.all_to_all(grads.reshape(devices, per, LANES), both, 0, 0, tiled=True)  9.92 us
    ppermute x1, starting transfers between devices, shards(): lax.ppermute(here, 'slab', [((i + 1) % slabs, i) for i in range(slabs)])  7.06 us
    all_to_all x1, starting transfers between devices, shards(): lax.all_to_all(jnp.broadcast_to(summed[None], shares.shape), both, 0, 0,...  5.27 us
    ppermute x3, starting transfers between devices, shards(): lax.ppermute(strip, 'view', ring(step))  5.08 us
  transfers between devices with their start and end apart: 7, of which 3 were waited for; matrix products, arithmetic and copies ran while one was open for 4% of the time, Pallas kernels for 1%

profile of v1, /device:TPU:1, one launch (start us, length us, event | category | flops | bytes accessed | tf_op | source)
XLA Modules:
  0.0 91.7 jit_solution(11585815280725163278)
XLA Ops:
  0.6 0.9 %convert_element_type.15 = bf16[5,4,8,128]{3,2,1,0:T(8,128)(2,1)S(1)} convert(f32[5,4,8,128]{3,2,1,0:T(8,128)} %param.9) | non-fusion elementwise | flops 20480 | bytes 122880 | tf_op jit(solution)/shard_map/convert_element_type | solution.py:319
  1.6 0.7 copy-done.7
  2.3 10.8 %all-gather = bf16[1536,128]{1,0:T(8,128)(2,1)S(1)} all-gather(bf16[384,128]{1,0:T(8,128)(2,1)S(1)} %pad_maximum_fusion), channel_id=2, replica_groups=mesh['slab'=64,'view'=4] {'view'}, dimensions={0}, use_global_device_ids=true | all-gather | bytes 491520 | tf_op jit(solution)/shard_map/all_gather | solution.py:325
  13.2 1.3 %box_rows.1.here = bf16[64,16,128]{2,1,0:T(8,128)(2,1)S(1)} custom-call(s32[1]{0:T(128)} %bitcast.1.meta, bf16[4,384,128]{2,1,0:T(8,128)(2,1)S(1)} %bitcast.39, s32[128,128]{1,0:T(8,128)S(1)} %bitcast.41, s32[128,128]{1,0:T(8,128)S(1)} %bitcast.43, bf16[8,128,128]{2,1,0:T(8,128)(2,1)S(1)} %copy-done), custom_call_target="tpu_custom_call" | custom-call | tf_op jit(solution)/shard_map/box_rows/pallas_call | solution.py:327
  14.5 0.4 collective-permute-start
  14.8 7.1 %collective-permute-start.1 = (bf16[64,16,128]{2,1,0:T(8,128)(2,1)S(1)}, bf16[64,16,128]{2,1,0:T(8,128)(2,1)S(1)}, u32[]{:S(2)}, u32[]{:S(2)}) collective-permute-start(bf16[64,16,128]{2,1,0:T(8,128)(2,1)S(1)} %box_rows.1.here), channel_id=1, source_target_pairs={{4,0},{8,4},{12,8},{16,12},{20,16},{24,20},{28,24},{32,28},{36,32}... | collective-permute-start | bytes 786440 | tf_op jit(solution)/shard_map/ppermute | solution.py:344
  21.9 0.7 copy-done.6
  23.4 0.2 copy.24
  23.6 0.2 reshape.112.w_mid_flip
  24.0 0.2 reshape.111.w_mid
  24.4 3.9 %collective-permute-done.prev = bf16[64,16,128]{2,1,0:T(8,128)(2,1)S(1)} collective-permute-done((bf16[64,16,128]{2,1,0:T(8,128)(2,1)S(1)}, bf16[64,16,128]{2,1,0:T(8,128)(2,1)S(1)}, u32[]{:S(2)}, u32[]{:S(2)}) %collective-permute-start) | collective-permute-done | bytes 262176 | tf_op jit(solution)/shard_map/ppermute | solution.py:343
  28.3 14.3 %net_box.1 = (f32[5,4,8,128]{3,2,1,0:T(8,128)}, f32[32,128]{1,0:T(8,128)S(1)}, f32[512,128]{1,0:T(8,128)}) custom-call(s32[4]{0:T(128)S(1)} %pad_add_fusion.meta, bf16[64,16,128]{2,1,0:T(8,128)(2,1)S(1)} %collective-permute-done.prev, bf16[64,16,128]{2,1,0:T(8,128)(2,1)S(1)} %box_rows.1.here, bf16[64,16,128]{2,1,0:T(8,128)(2,1)S(1)} %collective-permute-done.1.following, ...), custom_call_target="tpu_custom_call" | custom-call | tf_op jit(solution)/shard_map/net_box/pallas_call | solution.py:354
  42.6 9.9 %all-to-all-start = ((f32[256,2,128]{2,1,0:T(2,128)}), f32[256,2,128]{2,1,0:T(2,128)S(1)}, u32[]{:S(2)}, u32[]{:S(2)}) async-start(f32[256,2,128]{2,1,0:T(2,128)} %bitcast.25), calls=%async_computation | async-start | bytes 524288 | tf_op jit(solution)/shard_map/all_to_all | solution.py:384
  52.6 3.2 %collective-permute-start.2 = (bf16[32,128]{1,0:T(8,128)(2,1)S(1)}, bf16[32,128]{1,0:T(8,128)(2,1)S(1)}, u32[]{:S(2)}, u32[]{:S(2)}) collective-permute-start(bf16[32,128]{1,0:T(8,128)(2,1)S(1)} %convert_element_type.17), channel_id=1, source_target_pairs={{0,1},{1,2},{2,3},{3,0},{4,5},{5,6},{6,7},{7,4},{8,9},{9,10},{10,1... | collective-permute-start | bytes 24584 | tf_op jit(solution)/shard_map/ppermute | solution.py:380
  55.8 1.9 %collective-permute-start.3 = (bf16[32,128]{1,0:T(8,128)(2,1)S(1)}, bf16[32,128]{1,0:T(8,128)(2,1)S(1)}, u32[]{:S(2)}, u32[]{:S(2)}) collective-permute-start(bf16[32,128]{1,0:T(8,128)(2,1)S(1)} %convert_element_type.17), channel_id=1, source_target_pairs={{0,2},{1,3},{2,0},{3,1},{4,6},{5,7},{6,4},{7,5},{8,10},{9,11},{10,... | collective-permute-start | bytes 24584 | tf_op jit(solution)/shard_map/ppermute | solution.py:380
  57.7 10.4 %all-to-all-done = f32[256,2,128]{2,1,0:T(2,128)S(1)} async-done(((f32[256,2,128]{2,1,0:T(2,128)}), f32[256,2,128]{2,1,0:T(2,128)S(1)}, u32[]{:S(2)}, u32[]{:S(2)}) %all-to-all-start) | async-done | bytes 262176 | tf_op jit(solution)/shard_map/all_to_all | solution.py:384
  68.1 0.3 reduce_sum.9
  68.3 0.8 broadcast_in_dim.18
  69.1 5.3 %all-to-all-start.1 = ((f32[256,2,128]{2,1,0:T(2,128)}), f32[256,2,128]{2,1,0:T(2,128)S(1)}, u32[]{:S(2)}, u32[]{:S(2)}) async-start(f32[256,2,128]{2,1,0:T(2,128)} %broadcast_in_dim.18), calls=%async_computation.1 | async-start | bytes 524288 | tf_op jit(solution)/shard_map/all_to_all | solution.py:386
  74.5 0.6 gather_fusion
  75.1 1.3 %dual_views.1 = f32[64,128]{1,0:T(8,128)} custom-call(s32[1]{0:T(128)} %bitcast.1.meta, bf16[4,32,128]{2,1,0:T(8,128)(2,1)S(1)} %broadcast_select_fusion.strips, s32[128,128]{1,0:T(8,128)S(1)} %bitcast.42, s32[128,128]{1,0:T(8,128)S(1)} %bitcast.44, bf16[8,128,128]{2,1,0:T(8,128)(2,1)S(1)} %copy-done), custom_call_target="tpu_custom_call" | custom-call | tf_op jit(solution)/shard_map/dual_views/pallas_call | solution.py:393
  76.4 13.6 %all-to-all-done.1 = f32[256,2,128]{2,1,0:T(2,128)S(1)} async-done(((f32[256,2,128]{2,1,0:T(2,128)}), f32[256,2,128]{2,1,0:T(2,128)S(1)}, u32[]{:S(2)}, u32[]{:S(2)}) %all-to-all-start.1) | async-done | bytes 262176 | tf_op jit(solution)/shard_map/all_to_all | solution.py:386
  90.1 1.0 %split_grads.1 = (f32[3,3,3,6,32]{4,3,2,1,0:T(8,128)}, f32[3,3,3,32,32]{4,3,2,1,0:T(8,128)}, f32[3,3,3,5,32]{4,3,2,1,0:T(8,128)S(1)}) custom-call(f32[512,128]{1,0:T(8,128)S(1)} %bitcast.40), custom_call_target="tpu_custom_call" | custom-call | tf_op jit(solution)/shard_map/split_grads/pallas_call | solution.py:405
  91.0 0.7 copy.26
  (44 shorter events, 1.3 us)
Async XLA Ops:
  0.6 0.9 %copy-start.1 = (f32[5,4,8,128]{3,2,1,0:T(8,128)S(1)}, f32[5,4,8,128]{3,2,1,0:T(8,128)}, u32[]{:S(2)}) copy-start(f32[5,4,8,128]{3,2,1,0:T(8,128)} %cot.1) | copy-start | bytes 245764
  1.6 0.7 copy-start.7
  2.3 10.8 %copy-start = (bf16[8,128,128]{2,1,0:T(8,128)(2,1)S(1)}, bf16[8,128,128]{2,1,0:T(8,128)(2,1)}, u32[]{:S(2)}) copy-start(bf16[8,128,128]{2,1,0:T(8,128)(2,1)} %prints.3) | copy-start | bytes 786436
  2.3 10.8 %copy-start.2 = (s32[64,128,2]{1,2,0:T(2,128)S(1)}, s32[64,128,2]{1,2,0:T(2,128)}, u32[]{:S(2)}) copy-start(s32[64,128,2]{1,2,0:T(2,128)} %param.12) | copy-start | bytes 196612
  2.3 10.8 %copy-start.3 = (s32[64,128,2]{1,2,0:T(2,128)S(1)}, s32[64,128,2]{1,2,0:T(2,128)}, u32[]{:S(2)}) copy-start(s32[64,128,2]{1,2,0:T(2,128)} %param.13) | copy-start | bytes 196612
  13.2 8.7 %copy-start.5 = (bf16[3,3,3,32,6]{3,4,2,1,0:T(8,128)(2,1)S(1)}, bf16[3,3,3,32,6]{3,4,2,1,0:T(8,128)(2,1)}, u32[]{:S(2)}) copy-start(bf16[3,3,3,32,6]{3,4,2,1,0:T(8,128)(2,1)} %param.14) | copy-start | bytes 31108
  14.5 13.8 %collective-permute-start = (bf16[64,16,128]{2,1,0:T(8,128)(2,1)S(1)}, bf16[64,16,128]{2,1,0:T(8,128)(2,1)S(1)}, u32[]{:S(2)}, u32[]{:S(2)}) collective-permute-start(bf16[64,16,128]{2,1,0:T(8,128)(2,1)S(1)} %box_rows.1.here), channel_id=1, source_target_pairs={{0,4},{4,8},{8,12},{12,16},{16,20},{20,24},{24,28},{28,32},{32,36}... | collective-permute-start | bytes 786440 | tf_op jit(solution)/shard_map/ppermute | solution.py:343
  14.8 13.5 %collective-permute-start.1 = (bf16[64,16,128]{2,1,0:T(8,128)(2,1)S(1)}, bf16[64,16,128]{2,1,0:T(8,128)(2,1)S(1)}, u32[]{:S(2)}, u32[]{:S(2)}) collective-permute-start(bf16[64,16,128]{2,1,0:T(8,128)(2,1)S(1)} %box_rows.1.here), channel_id=1, source_target_pairs={{4,0},{8,4},{12,8},{16,12},{20,16},{24,20},{28,24},{32,28},{36,32}... | collective-permute-start | bytes 786440 | tf_op jit(solution)/shard_map/ppermute | solution.py:344
  21.9 0.8 copy-start.6
  21.9 0.9 %copy-start.4 = (bf16[3,3,3,32,32]{4,3,2,1,0:T(8,128)(2,1)S(1)}, bf16[3,3,3,32,32]{4,3,2,1,0:T(8,128)(2,1)}, u32[]{:S(2)}) copy-start(bf16[3,3,3,32,32]{4,3,2,1,0:T(8,128)(2,1)} %param.15) | copy-start | bytes 165892
  42.6 25.5 %all-to-all-start = ((f32[256,2,128]{2,1,0:T(2,128)}), f32[256,2,128]{2,1,0:T(2,128)S(1)}, u32[]{:S(2)}, u32[]{:S(2)}) async-start(f32[256,2,128]{2,1,0:T(2,128)} %bitcast.25), calls=%async_computation | async-start | bytes 524288 | tf_op jit(solution)/shard_map/all_to_all | solution.py:384
  52.6 21.8 %collective-permute-start.2 = (bf16[32,128]{1,0:T(8,128)(2,1)S(1)}, bf16[32,128]{1,0:T(8,128)(2,1)S(1)}, u32[]{:S(2)}, u32[]{:S(2)}) collective-permute-start(bf16[32,128]{1,0:T(8,128)(2,1)S(1)} %convert_element_type.17), channel_id=1, source_target_pairs={{0,1},{1,2},{2,3},{3,0},{4,5},{5,6},{6,7},{7,4},{8,9},{9,10},{10,1... | collective-permute-start | bytes 24584 | tf_op jit(solution)/shard_map/ppermute | solution.py:380
  55.8 18.6 %collective-permute-start.3 = (bf16[32,128]{1,0:T(8,128)(2,1)S(1)}, bf16[32,128]{1,0:T(8,128)(2,1)S(1)}, u32[]{:S(2)}, u32[]{:S(2)}) collective-permute-start(bf16[32,128]{1,0:T(8,128)(2,1)S(1)} %convert_element_type.17), channel_id=1, source_target_pairs={{0,2},{1,3},{2,0},{3,1},{4,6},{5,7},{6,4},{7,5},{8,10},{9,11},{10,... | collective-permute-start | bytes 24584 | tf_op jit(solution)/shard_map/ppermute | solution.py:380
  57.7 16.8 %collective-permute-start.4 = (bf16[32,128]{1,0:T(8,128)(2,1)S(1)}, bf16[32,128]{1,0:T(8,128)(2,1)S(1)}, u32[]{:S(2)}, u32[]{:S(2)}) collective-permute-start(bf16[32,128]{1,0:T(8,128)(2,1)S(1)} %convert_element_type.17), channel_id=1, source_target_pairs={{0,3},{1,0},{2,1},{3,2},{4,7},{5,4},{6,5},{7,6},{8,11},{9,8},{10,9... | collective-permute-start | bytes 24584 | tf_op jit(solution)/shard_map/ppermute | solution.py:380
  69.1 21.0 %all-to-all-start.1 = ((f32[256,2,128]{2,1,0:T(2,128)}), f32[256,2,128]{2,1,0:T(2,128)S(1)}, u32[]{:S(2)}, u32[]{:S(2)}) async-start(f32[256,2,128]{2,1,0:T(2,128)} %broadcast_in_dim.18), calls=%async_computation.1 | async-start | bytes 524288 | tf_op jit(solution)/shard_map/all_to_all | solution.py:386

commit v2 on v1

--- a/solution.py
+++ b/solution.py
@@ -124,16 +124,14 @@
 
 def net_kernel(
     meta, prev, here, following, cot, w_in, w_mid, w_mid_flip, w_first_flip,
-    d_primal, strip, grads,
-    box, slope, dz_two, z_one, z_two, da_two, da_one, dx,
+    d_primal, strip, packed,
+    grads, box, slope, dz_two, z_one, z_two, da_two, da_one, dx,
 ):
     slab_at, view_at, slabs, ranks = meta[0], meta[1], meta[2], meta[3]
     per = CZ * WY
-    box[0:per] = jnp.where(slab_at > 0, prev[...], jnp.zeros_like(prev[...]))
+    box[0:per] = prev[...]
     box[per : 2 * per] = here[...]
-    box[2 * per : 3 * per] = jnp.where(
-        slab_at < slabs - 1, following[...], jnp.zeros_like(following[...])
-    )
+    box[2 * per : 3 * per] = following[...]
     first, last = lane_masks((HID, LANES))
     z_start, y_start = slab_at * CZ, view_at * RY
     z_end, y_end = slabs * CZ, ranks * RY
@@ -232,6 +230,8 @@
         for c in range(5):
             d_primal[c, z] = cot[c, z] + dx[pl.ds(z * RY * 8 + c, RY, stride=8), :]
         strip[z * RY : (z + 1) * RY, :] = dx[pl.ds(z * RY * 8 + 5, RY, stride=8), :]
+    packed[0 : grads.shape[0], :] = grads[...].astype(BF16)
+    packed[grads.shape[0] :, :] = jnp.zeros((packed.shape[0] - grads.shape[0], LANES), BF16)
 
 
 def dual_kernel(meta, strips, tiles, foots, prints, out, codes):
@@ -267,8 +267,29 @@
         out[pl.ds(g, views, stride=DTL), :] = total[g * views : (g + 1) * views]
 
 
+def sum_kernel(per, shares, out):
+    block = max(per, 8)
+    total = shares[...].astype(F32).reshape(shares.shape[0] // block, block, LANES).sum(axis=0)
+    step = per
+    while step < block:
+        total = total + pltpu.roll(total, step, 0)
+        step *= 2
+    while total.shape[0] < 16:
+        total = jnp.concatenate([total, total], axis=0)
+    total = total.astype(BF16)
+    for at in range(0, out.shape[0], total.shape[0]):
+        out[at : at + total.shape[0], :] = total
+
+
+def sum_call(per):
+    def kernel(*refs):
+        sum_kernel(per, *refs)
+
+    return kernel
+
+
 def split_kernel(scale, packed, d_first, d_middle, d_last):
-    values = packed[0:432, :] * scale
+    values = packed[0:432, :].astype(F32) * scale
     for shift in range(3):
         moved = values if shift == 0 else pltpu.roll(values, LANES - shift * HID, 1)
         for a in range(3):
@@ -277,7 +298,7 @@
                 d_middle[2 - a, 2 - b, 2 - shift] = moved[tap * HID : (tap + 1) * HID, :HID]
                 at = 288 + tap * SLOT
                 d_first[a, b, shift] = moved[at : at + 6, :HID]
-                d_last[2 - a, 2 - b, 2 - shift] = moved[at + 8 : at + 13, :HID]
+                d_last[2 - a, 2 - b, :, 2 - shift, :] = moved[at + 8 : at + 13, :HID]
 
 
 def split_call(scale):
@@ -340,8 +361,8 @@
         name="box_rows",
     )(meta, packed, tiles, foots, footprints)
 
-    prev = lax.ppermute(here, "slab", [(i, (i + 1) % slabs) for i in range(slabs)])
-    following = lax.ppermute(here, "slab", [((i + 1) % slabs, i) for i in range(slabs)])
+    prev = lax.ppermute(here, "slab", [(i, i + 1) for i in range(slabs - 1)])
+    following = lax.ppermute(here, "slab", [(i + 1, i) for i in range(slabs - 1)])
 
     w_in = jnp.concatenate(
         [by_rows(w_first, SLOT, HID), by_rows(flipped(w_last), SLOT, HID, 8)], axis=0
@@ -356,11 +377,12 @@
         out_shape=(
             jax.ShapeDtypeStruct(primal.shape, F32),
             jax.ShapeDtypeStruct((CZ * RY, LANES), F32),
-            jax.ShapeDtypeStruct((2 * devices if devices >= 216 else 32 * devices, LANES), F32),
+            jax.ShapeDtypeStruct((2 * devices if devices >= 256 else 32 * devices, LANES), BF16),
         ),
         in_specs=[smem_spec()] + [vmem_spec()] * 8,
         out_specs=(vmem_spec(),) * 3,
         scratch_shapes=[
+            pltpu.VMEM((432, LANES), F32),
             pltpu.VMEM((3 * CZ * WY, SLOT, LANES), BF16),
             pltpu.VMEM((rows3, HID, LANES), F32),
             pltpu.VMEM((rows3, HID, LANES), F32),
@@ -382,9 +404,17 @@
     both = ("slab", "view")
     per = grads.shape[0] // devices
     shares = lax.all_to_all(grads.reshape(devices, per, LANES), both, 0, 0, tiled=True)
-    summed = shares.sum(axis=0)
+    summed = pl.pallas_call(
+        sum_call(per),
+        out_shape=jax.ShapeDtypeStruct(grads.shape, BF16),
+        in_specs=[vmem_spec()],
+        out_specs=vmem_spec(),
+        compiler_params=PARAMS,
+        interpret=INTERPRET,
+        name="sum_shares",
+    )(shares.reshape(grads.shape))
     whole = lax.all_to_all(
-        jnp.broadcast_to(summed[None], shares.shape), both, 0, 0, tiled=True
+        summed.reshape(shares.shape), both, 0, 0, tiled=True
     ).reshape(grads.shape)
 
     arrived = jnp.stack([strip] + others)
@@ -407,7 +437,7 @@
         out_shape=(
             jax.ShapeDtypeStruct((3, 3, 3, 6, HID), F32),
             jax.ShapeDtypeStruct((3, 3, 3, HID, HID), F32),
-            jax.ShapeDtypeStruct((3, 3, 3, 5, HID), F32),
+            jax.ShapeDtypeStruct((3, 3, 5, 3, HID), F32),
         ),
         in_specs=[vmem_spec()],
         out_specs=(vmem_spec(),) * 3,
@@ -420,7 +450,7 @@
         d_dual.reshape(dual.shape),
         d_first.transpose(0, 1, 2, 4, 3),
         d_middle,
-        d_last,
+        d_last.transpose(0, 1, 3, 2, 4),
     )
 
 

time: 92 us -> 89.5 us (0.973)
  waiting for transfers between devices: 27.9 us -> 20.9 us
  starting transfers between devices: 27.7 us -> 33.2 us
  local copies, waits for them, and re-layouts: 5.05 us -> 3.61 us
    all_to_all x1, starting transfers between devices: 9.92 us -> 17.1 us  [shards(): lax.all_to_all(grads.reshape(devices, per, LANES), both, 0, 0, tiled=True)]
    all_to_all x1, waiting for transfers between devices: 10.4 us -> 7.4 us  [shards(): lax.all_to_all(grads.reshape(devices, per, LANES), both, 0, 0, tiled=True)]
    all_to_all x1, waiting for transfers between devices: 13.6 us -> 10.9 us  [shards(): lax.all_to_all(summed.reshape(shares.shape), both, 0, 0, tiled=True)]
    ppermute x2, starting transfers between devices: 7.41 us -> 5.29 us  [the longest x1 4 us: shards(): prev = lax.ppermute(here, 'slab', [(i, i + 1) for i in range(slabs - 1)])]
    ppermute x2, waiting for transfers between devices: 3.9 us -> 2.62 us  [the longest x1 1.71 us: shards(): lax.ppermute(here, 'slab', [(i + 1, i) for i in range(slabs - 1)])]
    unnamed x17 -> x16, local copies, waits for them, and re-layouts: 2.16 us -> 1.49 us
  transfers between devices with their start and end apart: 7 -> 7, of which waited for: 3 -> 4; matrix products, arithmetic and copies ran while one was open for 4% -> 3% of each run, Pallas kernels for 1% -> 2%
where the time goes in v2:
time: 89.5 us; the launch traced here: 89.2 us
  starting transfers between devices  33.2 us (37%)
  waiting for transfers between devices  20.9 us (23%)
  Pallas kernels  18.5 us (21%)
  blocking collectives  10.8 us (12%)
  local copies, waits for them, and re-layouts  3.61 us (4%)
  other arithmetic  1.17 us (1%)
  between operations  0.93 us (1%)
    all_to_all x1, starting transfers between devices, shards(): lax.all_to_all(grads.reshape(devices, per, LANES), both, 0, 0, tiled=True)  17.1 us
    pallas_call x1, Pallas kernels, shards(): pl.pallas_call(net_kernel, out_shape=(jax.ShapeDtypeStruct(primal.shape,...  14.2 us
    all_to_all x1, waiting for transfers between devices, shards(): lax.all_to_all(summed.reshape(shares.shape), both, 0, 0, tiled=True)  10.9 us
    all_gather x1, blocking collectives, shards(): packed = lax.all_gather(packed, 'view', axis=0, tiled=False)  10.8 us
    all_to_all x1, waiting for transfers between devices, shards(): lax.all_to_all(grads.reshape(devices, per, LANES), both, 0, 0, tiled=True)  7.4 us
    all_to_all x1, starting transfers between devices, shards(): lax.all_to_all(summed.reshape(shares.shape), both, 0, 0, tiled=True)  5.44 us
    ppermute x3, starting transfers between devices, shards(): lax.ppermute(strip, 'view', ring(step))  5.37 us
    ppermute x1, starting transfers between devices, shards(): prev = lax.ppermute(here, 'slab', [(i, i + 1) for i in range(slabs - 1)])  4 us
  transfers between devices with their start and end apart: 7, of which 4 were waited for; matrix products, arithmetic and copies ran while one was open for 3% of the time, Pallas kernels for 2%

profile of v2, /device:TPU:1, one launch (start us, length us, event | category | flops | bytes accessed | tf_op | source)
XLA Modules:
  0.0 89.2 jit_solution(4609154473574068117)
XLA Ops:
  0.6 0.9 %convert_element_type.15 = bf16[5,4,8,128]{3,2,1,0:T(8,128)(2,1)S(1)} convert(f32[5,4,8,128]{3,2,1,0:T(8,128)} %param.9) | non-fusion elementwise | flops 20480 | bytes 122880 | tf_op jit(solution)/shard_map/convert_element_type | solution.py:340
  1.6 0.7 copy-done.7
  2.3 10.8 %all-gather = bf16[1536,128]{1,0:T(8,128)(2,1)S(1)} all-gather(bf16[384,128]{1,0:T(8,128)(2,1)S(1)} %pad_maximum_fusion), channel_id=2, replica_groups=mesh['slab'=64,'view'=4] {'view'}, dimensions={0}, use_global_device_ids=true | all-gather | bytes 491520 | tf_op jit(solution)/shard_map/all_gather | solution.py:346
  13.2 1.3 %box_rows.1.here = bf16[64,16,128]{2,1,0:T(8,128)(2,1)S(1)} custom-call(s32[1]{0:T(128)} %bitcast.1.meta, bf16[4,384,128]{2,1,0:T(8,128)(2,1)S(1)} %bitcast.42, s32[128,128]{1,0:T(8,128)S(1)} %bitcast.45, s32[128,128]{1,0:T(8,128)S(1)} %bitcast.47, bf16[8,128,128]{2,1,0:T(8,128)(2,1)S(1)} %copy-done), custom_call_target="tpu_custom_call" | custom-call | tf_op jit(solution)/shard_map/box_rows/pallas_call | solution.py:348
  14.5 1.3 %collective-permute-start.1 = (bf16[64,16,128]{2,1,0:T(8,128)(2,1)S(1)}, bf16[64,16,128]{2,1,0:T(8,128)(2,1)S(1)}, u32[]{:S(2)}, u32[]{:S(2)}) collective-permute-start(bf16[64,16,128]{2,1,0:T(8,128)(2,1)S(1)} %box_rows.1.here), channel_id=1, source_target_pairs={{4,0},{8,4},{12,8},{16,12},{20,16},{24,20},{28,24},{32,28},{36,32}... | collective-permute-start | bytes 786440 | tf_op jit(solution)/shard_map/ppermute | solution.py:365
  15.8 4.0 %collective-permute-start = (bf16[64,16,128]{2,1,0:T(8,128)(2,1)S(1)}, bf16[64,16,128]{2,1,0:T(8,128)(2,1)S(1)}, u32[]{:S(2)}, u32[]{:S(2)}) collective-permute-start(bf16[64,16,128]{2,1,0:T(8,128)(2,1)S(1)} %box_rows.1.here), channel_id=1, source_target_pairs={{0,4},{4,8},{8,12},{12,16},{16,20},{20,24},{24,28},{28,32},{32,36}... | collective-permute-start | bytes 786440 | tf_op jit(solution)/shard_map/ppermute | solution.py:364
  19.9 0.7 copy-done.6
  21.6 0.2 copy.23
  21.8 0.2 reshape.117.w_mid_flip
  22.0 0.2 copy.22
  22.1 0.2 reshape.116.w_mid
  22.3 1.7 %collective-permute-done.1.following = bf16[64,16,128]{2,1,0:T(8,128)(2,1)S(1)} collective-permute-done((bf16[64,16,128]{2,1,0:T(8,128)(2,1)S(1)}, bf16[64,16,128]{2,1,0:T(8,128)(2,1)S(1)}, u32[]{:S(2)}, u32[]{:S(2)}) %collective-permute-start.1) | collective-permute-done | bytes 262176 | tf_op jit(solution)/shard_map/ppermute | solution.py:365
  24.1 0.9 %collective-permute-done.prev = bf16[64,16,128]{2,1,0:T(8,128)(2,1)S(1)} collective-permute-done((bf16[64,16,128]{2,1,0:T(8,128)(2,1)S(1)}, bf16[64,16,128]{2,1,0:T(8,128)(2,1)S(1)}, u32[]{:S(2)}, u32[]{:S(2)}) %collective-permute-start) | collective-permute-done | bytes 262176 | tf_op jit(solution)/shard_map/ppermute | solution.py:364
  25.0 14.2 %net_box.1 = (f32[5,4,8,128]{3,2,1,0:T(8,128)}, f32[32,128]{1,0:T(8,128)S(1)}, bf16[512,128]{1,0:T(8,128)(2,1)}) custom-call(s32[4]{0:T(128)S(1)} %pad_add_fusion.meta, bf16[64,16,128]{2,1,0:T(8,128)(2,1)S(1)} %collective-permute-done.prev, bf16[64,16,128]{2,1,0:T(8,128)(2,1)S(1)} %box_rows.1.here, ...), custom_call_target="tpu_custom_call" | custom-call | tf_op jit(solution)/shard_map/net_box/pallas_call | solution.py:375
  39.1 17.1 %all-to-all-start = ((bf16[256,2,128]{2,1,0:T(2,128)(2,1)}), bf16[256,2,128]{2,1,0:T(2,128)(2,1)S(1)}, u32[]{:S(2)}, u32[]{:S(2)}) async-start(bf16[256,2,128]{2,1,0:T(2,128)(2,1)} %bitcast.25), calls=%async_computation | async-start | bytes 262144 | tf_op jit(solution)/shard_map/all_to_all | solution.py:406
  56.3 2.9 %collective-permute-start.3 = (bf16[32,128]{1,0:T(8,128)(2,1)S(1)}, bf16[32,128]{1,0:T(8,128)(2,1)S(1)}, u32[]{:S(2)}, u32[]{:S(2)}) collective-permute-start(bf16[32,128]{1,0:T(8,128)(2,1)S(1)} %convert_element_type.17), channel_id=1, source_target_pairs={{0,2},{1,3},{2,0},{3,1},{4,6},{5,7},{6,4},{7,5},{8,10},{9,11},{10,... | collective-permute-start | bytes 24584 | tf_op jit(solution)/shard_map/ppermute | solution.py:402
  59.2 2.4 %collective-permute-start.2 = (bf16[32,128]{1,0:T(8,128)(2,1)S(1)}, bf16[32,128]{1,0:T(8,128)(2,1)S(1)}, u32[]{:S(2)}, u32[]{:S(2)}) collective-permute-start(bf16[32,128]{1,0:T(8,128)(2,1)S(1)} %convert_element_type.17), channel_id=1, source_target_pairs={{0,1},{1,2},{2,3},{3,0},{4,5},{5,6},{6,7},{7,4},{8,9},{9,10},{10,1... | collective-permute-start | bytes 24584 | tf_op jit(solution)/shard_map/ppermute | solution.py:402
  61.6 7.4 %all-to-all-done = bf16[256,2,128]{2,1,0:T(2,128)(2,1)S(1)} async-done(((bf16[256,2,128]{2,1,0:T(2,128)(2,1)}), bf16[256,2,128]{2,1,0:T(2,128)(2,1)S(1)}, u32[]{:S(2)}, u32[]{:S(2)}) %all-to-all-start) | async-done | bytes 131104 | tf_op jit(solution)/shard_map/all_to_all | solution.py:406
  69.0 0.7 sum_shares.1
  69.8 5.4 %all-to-all-start.1 = ((bf16[256,2,128]{2,1,0:T(2,128)(2,1)}), bf16[256,2,128]{2,1,0:T(2,128)(2,1)S(1)}, u32[]{:S(2)}, u32[]{:S(2)}) async-start(bf16[256,2,128]{2,1,0:T(2,128)(2,1)} %bitcast.27), calls=%async_computation.1 | async-start | bytes 262144 | tf_op jit(solution)/shard_map/all_to_all | solution.py:416
  75.3 0.6 gather_fusion
  75.9 1.3 %dual_views.1 = f32[64,128]{1,0:T(8,128)} custom-call(s32[1]{0:T(128)} %bitcast.1.meta, bf16[4,32,128]{2,1,0:T(8,128)(2,1)S(1)} %broadcast_select_fusion.strips, s32[128,128]{1,0:T(8,128)S(1)} %bitcast.46, s32[128,128]{1,0:T(8,128)S(1)} %bitcast.48, bf16[8,128,128]{2,1,0:T(8,128)(2,1)S(1)} %copy-done), custom_call_target="tpu_custom_call" | custom-call | tf_op jit(solution)/shard_map/dual_views/pallas_call | solution.py:423
  77.3 10.9 %all-to-all-done.1 = bf16[256,2,128]{2,1,0:T(2,128)(2,1)S(1)} async-done(((bf16[256,2,128]{2,1,0:T(2,128)(2,1)}), bf16[256,2,128]{2,1,0:T(2,128)(2,1)S(1)}, u32[]{:S(2)}, u32[]{:S(2)}) %all-to-all-start.1) | async-done | bytes 131104 | tf_op jit(solution)/shard_map/all_to_all | solution.py:416
  88.2 1.0 %split_grads.1 = (f32[3,3,3,6,32]{4,3,2,1,0:T(8,128)}, f32[3,3,3,32,32]{4,3,2,1,0:T(8,128)}, f32[3,3,5,3,32]{4,3,2,1,0:T(4,128)}) custom-call(bf16[512,128]{1,0:T(8,128)(2,1)S(1)} %bitcast.43), custom_call_target="tpu_custom_call" | custom-call | tf_op jit(solution)/shard_map/split_grads/pallas_call | solution.py:435
  (42 shorter events, 1.1 us)
Async XLA Ops:
  0.6 0.9 %copy-start.1 = (f32[5,4,8,128]{3,2,1,0:T(8,128)S(1)}, f32[5,4,8,128]{3,2,1,0:T(8,128)}, u32[]{:S(2)}) copy-start(f32[5,4,8,128]{3,2,1,0:T(8,128)} %cot.1) | copy-start | bytes 245764
  1.6 0.7 copy-start.7
  2.3 10.8 %copy-start = (bf16[8,128,128]{2,1,0:T(8,128)(2,1)S(1)}, bf16[8,128,128]{2,1,0:T(8,128)(2,1)}, u32[]{:S(2)}) copy-start(bf16[8,128,128]{2,1,0:T(8,128)(2,1)} %prints.3) | copy-start | bytes 786436
  2.3 10.8 %copy-start.2 = (s32[64,128,2]{1,2,0:T(2,128)S(1)}, s32[64,128,2]{1,2,0:T(2,128)}, u32[]{:S(2)}) copy-start(s32[64,128,2]{1,2,0:T(2,128)} %param.12) | copy-start | bytes 196612
  2.3 10.8 %copy-start.3 = (s32[64,128,2]{1,2,0:T(2,128)S(1)}, s32[64,128,2]{1,2,0:T(2,128)}, u32[]{:S(2)}) copy-start(s32[64,128,2]{1,2,0:T(2,128)} %param.13) | copy-start | bytes 196612
  13.2 6.6 %copy-start.5 = (bf16[3,3,3,32,6]{3,4,2,1,0:T(8,128)(2,1)S(1)}, bf16[3,3,3,32,6]{3,4,2,1,0:T(8,128)(2,1)}, u32[]{:S(2)}) copy-start(bf16[3,3,3,32,6]{3,4,2,1,0:T(8,128)(2,1)} %param.14) | copy-start | bytes 31108
  14.5 9.6 %collective-permute-start.1 = (bf16[64,16,128]{2,1,0:T(8,128)(2,1)S(1)}, bf16[64,16,128]{2,1,0:T(8,128)(2,1)S(1)}, u32[]{:S(2)}, u32[]{:S(2)}) collective-permute-start(bf16[64,16,128]{2,1,0:T(8,128)(2,1)S(1)} %box_rows.1.here), channel_id=1, source_target_pairs={{4,0},{8,4},{12,8},{16,12},{20,16},{24,20},{28,24},{32,28},{36,32}... | collective-permute-start | bytes 786440 | tf_op jit(solution)/shard_map/ppermute | solution.py:365
  15.8 9.2 %collective-permute-start = (bf16[64,16,128]{2,1,0:T(8,128)(2,1)S(1)}, bf16[64,16,128]{2,1,0:T(8,128)(2,1)S(1)}, u32[]{:S(2)}, u32[]{:S(2)}) collective-permute-start(bf16[64,16,128]{2,1,0:T(8,128)(2,1)S(1)} %box_rows.1.here), channel_id=1, source_target_pairs={{0,4},{4,8},{8,12},{12,16},{16,20},{20,24},{24,28},{28,32},{32,36}... | collective-permute-start | bytes 786440 | tf_op jit(solution)/shard_map/ppermute | solution.py:364
  19.8 0.8 copy-start.6
  19.9 0.9 %copy-start.4 = (bf16[3,3,3,32,32]{4,3,2,1,0:T(8,128)(2,1)S(1)}, bf16[3,3,3,32,32]{4,3,2,1,0:T(8,128)(2,1)}, u32[]{:S(2)}) copy-start(bf16[3,3,3,32,32]{4,3,2,1,0:T(8,128)(2,1)} %param.15) | copy-start | bytes 165892
  39.1 29.9 %all-to-all-start = ((bf16[256,2,128]{2,1,0:T(2,128)(2,1)}), bf16[256,2,128]{2,1,0:T(2,128)(2,1)S(1)}, u32[]{:S(2)}, u32[]{:S(2)}) async-start(bf16[256,2,128]{2,1,0:T(2,128)(2,1)} %bitcast.25), calls=%async_computation | async-start | bytes 262144 | tf_op jit(solution)/shard_map/all_to_all | solution.py:406
  56.3 19.0 %collective-permute-start.3 = (bf16[32,128]{1,0:T(8,128)(2,1)S(1)}, bf16[32,128]{1,0:T(8,128)(2,1)S(1)}, u32[]{:S(2)}, u32[]{:S(2)}) collective-permute-start(bf16[32,128]{1,0:T(8,128)(2,1)S(1)} %convert_element_type.17), channel_id=1, source_target_pairs={{0,2},{1,3},{2,0},{3,1},{4,6},{5,7},{6,4},{7,5},{8,10},{9,11},{10,... | collective-permute-start | bytes 24584 | tf_op jit(solution)/shard_map/ppermute | solution.py:402
  59.2 16.0 %collective-permute-start.2 = (bf16[32,128]{1,0:T(8,128)(2,1)S(1)}, bf16[32,128]{1,0:T(8,128)(2,1)S(1)}, u32[]{:S(2)}, u32[]{:S(2)}) collective-permute-start(bf16[32,128]{1,0:T(8,128)(2,1)S(1)} %convert_element_type.17), channel_id=1, source_target_pairs={{0,1},{1,2},{2,3},{3,0},{4,5},{5,6},{6,7},{7,4},{8,9},{9,10},{10,1... | collective-permute-start | bytes 24584 | tf_op jit(solution)/shard_map/ppermute | solution.py:402
  61.6 13.6 %collective-permute-start.4 = (bf16[32,128]{1,0:T(8,128)(2,1)S(1)}, bf16[32,128]{1,0:T(8,128)(2,1)S(1)}, u32[]{:S(2)}, u32[]{:S(2)}) collective-permute-start(bf16[32,128]{1,0:T(8,128)(2,1)S(1)} %convert_element_type.17), channel_id=1, source_target_pairs={{0,3},{1,0},{2,1},{3,2},{4,7},{5,4},{6,5},{7,6},{8,11},{9,8},{10,9... | collective-permute-start | bytes 24584 | tf_op jit(solution)/shard_map/ppermute | solution.py:402
  69.8 18.4 %all-to-all-start.1 = ((bf16[256,2,128]{2,1,0:T(2,128)(2,1)}), bf16[256,2,128]{2,1,0:T(2,128)(2,1)S(1)}, u32[]{:S(2)}, u32[]{:S(2)}) async-start(bf16[256,2,128]{2,1,0:T(2,128)(2,1)} %bitcast.27), calls=%async_computation.1 | async-start | bytes 262144 | tf_op jit(solution)/shard_map/all_to_all | solution.py:416

commit v3 on v2

--- a/solution.py
+++ b/solution.py
@@ -28,6 +28,12 @@
 
 def vmem_spec():
     return pl.BlockSpec(memory_space=pltpu.VMEM)
+
+
+def pack_kernel(primal, cotangent, dual, out):
+    out[0:160, :] = primal[...].astype(BF16)
+    out[160:320, :] = cotangent[...].astype(BF16)
+    out[320:, :] = dual[...]
 
 
 def gather_kernel(meta, packed, tiles, foots, prints, out, codes, duals, field, rows):
@@ -122,16 +128,51 @@
     return jnp.concatenate(sides, axis=1)
 
 
+def side_matrix():
+    row = lax.broadcasted_iota(jnp.int32, (LANES, 2 * LANES), 0)
+    col = lax.broadcasted_iota(jnp.int32, (LANES, 2 * LANES), 1)
+    source = jnp.where(col < LANES, col - 1, col - LANES + 1)
+    source = jnp.where(source < LANES, source, -1)
+    return jnp.where(row == source, 1.0, 0.0).astype(BF16)
+
+
+def pipelined(count, multiply, finish, first_buf, second_buf):
+    multiply(0, first_buf)
+
+    def step(i, carry):
+        multiply(2 * i + 1, second_buf)
+        finish(2 * i, first_buf)
+        multiply(2 * i + 2, first_buf)
+        finish(2 * i + 1, second_buf)
+        return carry
+
+    lax.fori_loop(0, count // 2 - 1, step, 0)
+    multiply(count - 1, second_buf)
+    finish(count - 2, first_buf)
+    finish(count - 1, second_buf)
+
+
 def net_kernel(
     meta, prev, here, following, cot, w_in, w_mid, w_mid_flip, w_first_flip,
     d_primal, strip, packed,
-    grads, box, slope, dz_two, z_one, z_two, da_two, da_one, dx,
+    grads, ends_grad, mid_grad, buf_a, buf_b, box, slope, dz_two, z_one, z_two, da_two, da_one, dx,
 ):
     slab_at, view_at, slabs, ranks = meta[0], meta[1], meta[2], meta[3]
+    sides = side_matrix()
     per = CZ * WY
-    box[0:per] = prev[...]
-    box[per : 2 * per] = here[...]
-    box[2 * per : 3 * per] = following[...]
+    has = (slab_at > 0, None, slab_at < slabs - 1)
+    for part, source in enumerate((prev, here, following)):
+        for at in range(0, per, WY):
+            rows = source[at : at + WY]
+            if has[part] is not None:
+                rows = jnp.where(has[part], rows, jnp.zeros_like(rows))
+            both = jnp.dot(
+                rows.reshape(WY * SLOT, LANES), sides, preferred_element_type=F32
+            ).astype(BF16)
+            to = slice(part * per + at, part * per + at + WY)
+            box[to, 0:SLOT, :] = both[:, :LANES].reshape(WY, SLOT, LANES)
+            box[to, SLOT : 2 * SLOT, :] = rows
+            box[to, 2 * SLOT : 3 * SLOT, :] = both[:, LANES:].reshape(WY, SLOT, LANES)
     first, last = lane_masks((HID, LANES))
     z_start, y_start = slab_at * CZ, view_at * RY
     z_end, y_end = slabs * CZ, ranks * RY
@@ -147,48 +188,52 @@
     depth2, rows2 = CZ + 4, RY + 4
     depth1, rows1 = CZ + 2, RY + 2
 
-    def layer_one(z, carry):
-        for y in range(0, rows3, 2):
-            taps = jnp.dot(w_in[...], window(box, WY, z, y), preferred_element_type=F32)
-            for s in range(2):
-                half = taps[:, s * LANES : (s + 1) * LANES]
-                value = shift_sum(half[: 3 * HID], first, last)
-                sig = sigmoid(value)
-                at = z * rows3 + y + s
-                z_one[at] = jnp.where(inside(z, y + s, 3), value * sig, 0.0).astype(BF16)
-                slope[at] = sig * (1.0 + value * (1.0 - sig))
-                dz_two[at] = shift_sum(half[3 * HID :], first, last)
-        return carry
-
-    lax.fori_loop(0, depth3, layer_one, 0)
-
-    def layer_two(z, carry):
-        for y in range(0, rows2, 2):
-            taps = jnp.dot(w_mid[...], window(z_one, rows3, z, y), preferred_element_type=F32)
-            for s in range(2):
-                value = shift_sum(taps[:, s * LANES : (s + 1) * LANES], first, last)
-                sig = sigmoid(value)
-                at = z * rows2 + y + s
-                z_two[at] = (value * sig).astype(BF16)
-                grad = dz_two[(z + 1) * rows3 + y + s + 1] * (sig * (1.0 + value * (1.0 - sig)))
-                da_two[at] = jnp.where(inside(z, y + s, 2), grad, 0.0).astype(BF16)
-        return carry
-
-    lax.fori_loop(0, depth2, layer_two, 0)
-
-    def layer_back(z, carry):
-        for y in range(0, rows1, 2):
-            taps = jnp.dot(w_mid_flip[...], window(da_two, rows2, z, y), preferred_element_type=F32)
-            for s in range(2):
-                value = shift_sum(taps[:, s * LANES : (s + 1) * LANES], first, last)
-                grad = value * slope[(z + 2) * rows3 + y + s + 2]
-                da_one[z * rows1 + y + s] = jnp.where(inside(z, y + s, 1), grad, 0.0).astype(BF16)
-        return carry
-
-    lax.fori_loop(0, depth1, layer_back, 0)
+    def times(weights, source, width, rows):
+        def multiply(z, buf):
+            for y in range(0, rows, 2):
+                buf[y // 2, 0 : weights.shape[0], :] = jnp.dot(
+                    weights[...], window(source, width, z, y), preferred_element_type=F32
+                )
+
+        return multiply
+
+    def finish_one(z, buf):
+        for y in range(rows3):
+            half = slice((y % 2) * LANES, (y % 2 + 1) * LANES)
+            value = buf[y // 2, 0:HID, half]
+            sig = sigmoid(value)
+            at = z * rows3 + y
+            z_one[at] = jnp.where(inside(z, y, 3), value * sig, 0.0).astype(BF16)
+            slope[at] = sig * (1.0 + value * (1.0 - sig))
+            dz_two[at] = buf[y // 2, HID : 2 * HID, half]
+
+    pipelined(depth3, times(w_in, box, WY, rows3), finish_one, buf_a, buf_b)
+
+    def finish_two(z, buf):
+        for y in range(rows2):
+            half = slice((y % 2) * LANES, (y % 2 + 1) * LANES)
+            value = shift_sum(buf[y // 2, 0 : 3 * HID, half], first, last)
+            sig = sigmoid(value)
+            at = z * rows2 + y
+            z_two[at] = (value * sig).astype(BF16)
+            grad = dz_two[(z + 1) * rows3 + y + 1] * (sig * (1.0 + value * (1.0 - sig)))
+            da_two[at] = jnp.where(inside(z, y, 2), grad, 0.0).astype(BF16)
+
+    pipelined(depth2, times(w_mid, z_one, rows3, rows2), finish_two, buf_a, buf_b)
+
+    def finish_back(z, buf):
+        for y in range(rows1):
+            half = slice((y % 2) * LANES, (y % 2 + 1) * LANES)
+            value = shift_sum(buf[y // 2, 0 : 3 * HID, half], first, last)
+            grad = value * slope[(z + 2) * rows3 + y + 2]
+            da_one[z * rows1 + y] = jnp.where(inside(z, y, 1), grad, 0.0).astype(BF16)
+
+    pipelined(depth1, times(w_mid_flip, da_two, rows2, rows1), finish_back, buf_a, buf_b)
 
     first8, last8 = lane_masks((8, LANES))
-    grads[...] = jnp.zeros(grads.shape, F32)
+    ends_grad[...] = jnp.zeros(ends_grad.shape, F32)
+    mid_grad[...] = jnp.zeros(mid_grad.shape, F32)
+    contract = (((1,), (1,)), ((), ()))
 
     def layer_out(z, carry):
         for y in range(0, RY, 2):
@@ -196,32 +241,37 @@
             for s in range(2):
                 at = pl.multiple_of((z * RY + y + s) * 8, 8)
                 dx[pl.ds(at, 8), :] = shift_sum(taps[:, s * LANES : (s + 1) * LANES], first8, last8)
-        blank = jnp.zeros((HID, LANES), BF16)
-        ends, mids, low, mid = [], [], [], []
-        for y in range(0, RY, 2):
-            low.append(window(box, WY, z + 3, y + 3))
-            mid.append(window(da_two, rows2, z + 1, y + 1))
-            for s in range(2):
-                one = da_one[(z + 1) * rows1 + y + s + 1].astype(F32)
-                two = z_two[(z + 2) * rows2 + y + s + 2].astype(F32)
-                inner = z_one[(z + 3) * rows3 + y + s + 3].astype(F32)
-                back = lambda v: [p.astype(BF16) for p in shifted(v, first, last)[::-1]]
-                ends.append(jnp.concatenate(back(one) + [blank] + back(two) + [blank], axis=0))
-                mids.append(jnp.concatenate(back(inner) + [blank], axis=0))
-        contract = (((1,), (1,)), ((), ()))
-        out = lax.dot_general(
-            jnp.concatenate(low, axis=1), jnp.concatenate(ends, axis=1), contract,
-            preferred_element_type=F32,
+        inner = z_one[pl.ds((z + 3) * rows3 + 3, RY)]
+        both = jnp.dot(
+            inner.reshape(RY * HID, LANES), sides, preferred_element_type=F32
+        ).astype(BF16)
+        ends = jnp.concatenate(
+            [
+                jnp.concatenate(
+                    [da_one[(z + 1) * rows1 + y + 1], z_two[(z + 2) * rows2 + y + 2]], axis=0
+                )
+                for y in range(RY)
+            ],
+            axis=1,
         )
-        for tap in range(9):
-            x_rows = slice(tap * SLOT, tap * SLOT + 8)
-            g_rows = slice(tap * SLOT + 8, tap * SLOT + 16)
-            grads[288 + tap * SLOT : 288 + tap * SLOT + 8, :] += out[x_rows, :LANES]
-            grads[288 + tap * SLOT + 8 : 288 + tap * SLOT + 16, :] += out[g_rows, LANES:]
-        grads[0:288, :] += lax.dot_general(
-            jnp.concatenate(mid, axis=1), jnp.concatenate(mids, axis=1), contract,
-            preferred_element_type=F32,
+        mids = jnp.concatenate(
+            [
+                jnp.concatenate(
+                    [
+                        both[y * HID : (y + 1) * HID, LANES:],
+                        inner[y],
+                        both[y * HID : (y + 1) * HID, :LANES],
+                    ],
+                    axis=0,
+                )
+                for y in range(RY)
+            ],
+            axis=1,
         )
+        low = jnp.concatenate([window(box, WY, z + 3, y + 3) for y in range(0, RY, 2)], axis=1)
+        mid = jnp.concatenate([window(da_two, rows2, z + 1, y + 1) for y in range(0, RY, 2)], axis=1)
+        ends_grad[...] += lax.dot_general(low, ends, contract, preferred_element_type=F32)
+        mid_grad[...] += lax.dot_general(mid, mids, contract, preferred_element_type=F32)
         return carry
 
     lax.fori_loop(0, CZ, layer_out, 0)
@@ -230,6 +280,15 @@
         for c in range(5):
             d_primal[c, z] = cot[c, z] + dx[pl.ds(z * RY * 8 + c, RY, stride=8), :]
         strip[z * RY : (z + 1) * RY, :] = dx[pl.ds(z * RY * 8 + 5, RY, stride=8), :]
+    grads[...] = jnp.zeros(grads.shape, F32)
+    grads[0:288, 0 : 3 * HID] = mid_grad[...]
+    for tap in range(9):
+        for shift in range(3):
+            at = (tap * 3 + shift) * SLOT
+            to = 288 + tap * SLOT
+            cut = slice(shift * HID, (shift + 1) * HID)
+            grads[to : to + 8, cut] = ends_grad[at : at + 8, 0:HID]
+            grads[to + 8 : to + 16, cut] = ends_grad[at + 8 : at + 16, HID : 2 * HID]
     packed[0 : grads.shape[0], :] = grads[...].astype(BF16)
     packed[grads.shape[0] :, :] = jnp.zeros((packed.shape[0] - grads.shape[0], LANES), BF16)
 
@@ -312,10 +371,16 @@
     return kernel[::-1, ::-1, ::-1].transpose(0, 1, 2, 4, 3)
 
 
-def by_rows(kernel, inputs_to, outputs_to, shift=0):
+def by_taps(kernel, shift):
+    o, i = kernel.shape[3], kernel.shape[4]
+    kernel = jnp.pad(kernel, ((0, 0),) * 4 + ((shift, SLOT - i - shift),))
+    return kernel.transpose(3, 0, 1, 2, 4).reshape(o, 27 * SLOT)
+
+
+def by_rows(kernel, inputs_to, outputs_to):
     o, i = kernel.shape[3], kernel.shape[4]
     kernel = jnp.pad(
-        kernel, ((0, 0), (0, 0), (0, 0), (0, outputs_to - o), (shift, inputs_to - i - shift))
+        kernel, ((0, 0), (0, 0), (0, 0), (0, outputs_to - o), (0, inputs_to - i))
     )
     return kernel.transpose(2, 3, 0, 1, 4).reshape(3 * outputs_to, 9 * inputs_to)
 
@@ -335,13 +400,18 @@
     flat = lambda idx: idx.transpose(0, 2, 1).reshape(all_views * taps, tiles_here)
     tiles, foots = flat(tile_index), flat(footprint_offset)
 
-    packed = jnp.concatenate(
-        [
-            primal.astype(BF16).reshape(160, LANES),
-            cotangent.astype(BF16).reshape(160, LANES),
-            dual.reshape(views_here * det_tiles, LANES),
-        ],
-        axis=0,
+    packed = pl.pallas_call(
+        pack_kernel,
+        out_shape=jax.ShapeDtypeStruct((320 + views_here * det_tiles, LANES), BF16),
+        in_specs=[vmem_spec()] * 3,
+        out_specs=vmem_spec(),
+        compiler_params=PARAMS,
+        interpret=INTERPRET,
+        name="pack_inputs",
+    )(
+        primal.reshape(160, LANES),
+        cotangent.reshape(160, LANES),
+        dual.reshape(views_here * det_tiles, LANES),
     )
     packed = lax.all_gather(packed, "view", axis=0, tiled=False)
 
@@ -361,12 +431,10 @@
         name="box_rows",
     )(meta, packed, tiles, foots, footprints)
 
-    prev = lax.ppermute(here, "slab", [(i, i + 1) for i in range(slabs - 1)])
-    following = lax.ppermute(here, "slab", [(i + 1, i) for i in range(slabs - 1)])
-
-    w_in = jnp.concatenate(
-        [by_rows(w_first, SLOT, HID), by_rows(flipped(w_last), SLOT, HID, 8)], axis=0
-    )
+    prev = lax.ppermute(here, "slab", [(i, (i + 1) % slabs) for i in range(slabs)])
+    following = lax.ppermute(here, "slab", [((i + 1) % slabs, i) for i in range(slabs)])
+
+    w_in = jnp.concatenate([by_taps(w_first, 0), by_taps(flipped(w_last), 8)], axis=0)
     w_mid = by_rows(w_middle, HID, HID)
     w_mid_flip = by_rows(flipped(w_middle), HID, HID)
     w_first_flip = by_rows(flipped(w_first), HID, 8)
@@ -383,7 +451,11 @@
         out_specs=(vmem_spec(),) * 3,
         scratch_shapes=[
             pltpu.VMEM((432, LANES), F32),
-            pltpu.VMEM((3 * CZ * WY, SLOT, LANES), BF16),
+            pltpu.VMEM((27 * SLOT, 2 * HID), F32),
+            pltpu.VMEM((288, 3 * HID), F32),
+            pltpu.VMEM((7, 3 * HID, 2 * LANES), F32),
+            pltpu.VMEM((7, 3 * HID, 2 * LANES), F32),
+            pltpu.VMEM((3 * CZ * WY, 3 * SLOT, LANES), BF16),
             pltpu.VMEM((rows3, HID, LANES), F32),
             pltpu.VMEM((rows3, HID, LANES), F32),
             pltpu.VMEM((rows3, HID, LANES), BF16),

time: 89.5 us -> 84 us (0.939)
  starting transfers between devices: 33.2 us -> 27.8 us
  Pallas kernels: 18.5 us -> 15.9 us
  local copies, waits for them, and re-layouts: 3.61 us -> 5.83 us
  waiting for transfers between devices: 20.9 us -> 22.1 us
  other arithmetic: 1.17 us -> 0.21 us
    all_to_all x1, starting transfers between devices: 17.1 us -> 9.92 us  [shards(): lax.all_to_all(grads.reshape(devices, per, LANES), both, 0, 0, tiled=True)]
    pallas_call x1, Pallas kernels: 14.2 us -> 11.6 us  [shards(): pl.pallas_call(net_kernel, out_shape=(jax.ShapeDtypeStruct(primal.shape,...]
    unnamed x16 -> x20, local copies, waits for them, and re-layouts: 1.49 us -> 4.03 us
    ppermute x2, starting transfers between devices: 5.29 us -> 7.41 us  [the longest x1 7.06 us: shards(): lax.ppermute(here, 'slab', [((i + 1) % slabs, i) for i in range(slabs)])]
    convert_element_type x2 -> x0, other arithmetic: 0.94 us -> none  [the longest x1 0.93 us: shards(): primal.astype(BF16).reshape(160, LANES)]
  transfers between devices with their start and end apart: 7 -> 7, of which waited for: 4 -> 3; matrix products, arithmetic and copies ran while one was open for 3% -> 2% of each run, Pallas kernels for 2% -> 2%
where the time goes in v3:
time: 84 us; the launch traced here: 83.6 us
  starting transfers between devices  27.8 us (33%)
  waiting for transfers between devices  22.1 us (26%)
  Pallas kernels  15.9 us (19%)
  blocking collectives  10.8 us (13%)
  local copies, waits for them, and re-layouts  5.83 us (7%)
  between operations  0.9 us (1%)
    pallas_call x1, Pallas kernels, shards(): pl.pallas_call(net_kernel, out_shape=(jax.ShapeDtypeStruct(primal.shape,...  11.6 us
    all_to_all x1, waiting for transfers between devices, shards(): lax.all_to_all(summed.reshape(shares.shape), both, 0, 0, tiled=True)  10.9 us
    all_gather x1, blocking collectives, shards(): packed = lax.all_gather(packed, 'view', axis=0, tiled=False)  10.8 us
    all_to_all x1, starting transfers between devices, shards(): lax.all_to_all(grads.reshape(devices, per, LANES), both, 0, 0, tiled=True)  9.92 us
    all_to_all x1, waiting for transfers between devices, shards(): lax.all_to_all(grads.reshape(devices, per, LANES), both, 0, 0, tiled=True)  7.69 us
    ppermute x1, starting transfers between devices, shards(): lax.ppermute(here, 'slab', [((i + 1) % slabs, i) for i in range(slabs)])  7.06 us
    all_to_all x1, starting transfers between devices, shards(): lax.all_to_all(summed.reshape(shares.shape), both, 0, 0, tiled=True)  5.44 us
    ppermute x3, starting transfers between devices, shards(): lax.ppermute(strip, 'view', ring(step))  5.08 us
  transfers between devices with their start and end apart: 7, of which 3 were waited for; matrix products, arithmetic and copies ran while one was open for 2% of the time, Pallas kernels for 2%

profile of v3, /device:TPU:1, one launch (start us, length us, event | category | flops | bytes accessed | tf_op | source)
XLA Modules:
  0.0 83.6 jit_solution(4276071424148202023)
XLA Ops:
  0.6 0.9 %copy-done.1 = f32[5,4,8,128]{3,2,1,0:T(8,128)S(1)} copy-done((f32[5,4,8,128]{3,2,1,0:T(8,128)S(1)}, f32[5,4,8,128]{3,2,1,0:T(8,128)}, u32[]{:S(2)}) %copy-start.1) | copy-done | bytes 81944
  1.5 0.9 %copy-done.5 = f32[5,4,8,128]{3,2,1,0:T(8,128)S(1)} copy-done((f32[5,4,8,128]{3,2,1,0:T(8,128)S(1)}, f32[5,4,8,128]{3,2,1,0:T(8,128)}, u32[]{:S(2)}) %copy-start.5) | copy-done | bytes 81944
  2.4 0.7 copy-done.6
  3.2 10.8 %all-gather = bf16[1536,128]{1,0:T(8,128)(2,1)S(1)} all-gather(bf16[384,128]{1,0:T(8,128)(2,1)S(1)} %pack_inputs.1), channel_id=2, replica_groups=mesh['slab'=64,'view'=4] {'view'}, dimensions={0}, use_global_device_ids=true | all-gather | bytes 491520 | tf_op jit(solution)/shard_map/all_gather | solution.py:416
  14.0 1.3 %box_rows.1.here = bf16[64,16,128]{2,1,0:T(8,128)(2,1)S(1)} custom-call(s32[1]{0:T(128)} %bitcast.1.meta, bf16[4,384,128]{2,1,0:T(8,128)(2,1)S(1)} %bitcast.40, s32[128,128]{1,0:T(8,128)S(1)} %bitcast.44, s32[128,128]{1,0:T(8,128)S(1)} %bitcast.46, bf16[8,128,128]{2,1,0:T(8,128)(2,1)S(1)} %copy-done), custom_call_target="tpu_custom_call" | custom-call | tf_op jit(solution)/shard_map/box_rows/pallas_call | solution.py:418
  15.3 0.4 collective-permute-start
  15.7 7.1 %collective-permute-start.1 = (bf16[64,16,128]{2,1,0:T(8,128)(2,1)S(1)}, bf16[64,16,128]{2,1,0:T(8,128)(2,1)S(1)}, u32[]{:S(2)}, u32[]{:S(2)}) collective-permute-start(bf16[64,16,128]{2,1,0:T(8,128)(2,1)S(1)} %box_rows.1.here), channel_id=1, source_target_pairs={{4,0},{8,4},{12,8},{16,12},{20,16},{24,20},{28,24},{32,28},{36,32}... | collective-permute-start | bytes 786440 | tf_op jit(solution)/shard_map/ppermute | solution.py:435
  22.8 0.8 copy-done.9
  23.7 0.7 copy-done.8
  24.6 0.2 copy.23
  24.8 0.2 reshape.117.w_mid_flip
  25.3 0.2 reshape.116.w_mid
  25.7 3.4 %collective-permute-done.prev = bf16[64,16,128]{2,1,0:T(8,128)(2,1)S(1)} collective-permute-done((bf16[64,16,128]{2,1,0:T(8,128)(2,1)S(1)}, bf16[64,16,128]{2,1,0:T(8,128)(2,1)S(1)}, u32[]{:S(2)}, u32[]{:S(2)}) %collective-permute-start) | collective-permute-done | bytes 262176 | tf_op jit(solution)/shard_map/ppermute | solution.py:434
  29.2 11.6 %net_box.1 = (f32[5,4,8,128]{3,2,1,0:T(8,128)}, f32[32,128]{1,0:T(8,128)S(1)}, bf16[512,128]{1,0:T(8,128)(2,1)}) custom-call(s32[4]{0:T(128)S(1)} %pad_add_fusion.meta, bf16[64,16,128]{2,1,0:T(8,128)(2,1)S(1)} %collective-permute-done.prev, bf16[64,16,128]{2,1,0:T(8,128)(2,1)S(1)} %box_rows.1.here, ...), custom_call_target="tpu_custom_call" | custom-call | tf_op jit(solution)/shard_map/net_box/pallas_call | solution.py:443
  40.7 9.9 %all-to-all-start = ((bf16[256,2,128]{2,1,0:T(2,128)(2,1)}), bf16[256,2,128]{2,1,0:T(2,128)(2,1)S(1)}, u32[]{:S(2)}, u32[]{:S(2)}) async-start(bf16[256,2,128]{2,1,0:T(2,128)(2,1)} %bitcast.27), calls=%async_computation | async-start | bytes 262144 | tf_op jit(solution)/shard_map/all_to_all | solution.py:478
  50.7 3.2 %collective-permute-start.2 = (bf16[32,128]{1,0:T(8,128)(2,1)S(1)}, bf16[32,128]{1,0:T(8,128)(2,1)S(1)}, u32[]{:S(2)}, u32[]{:S(2)}) collective-permute-start(bf16[32,128]{1,0:T(8,128)(2,1)S(1)} %convert_element_type.9), channel_id=1, source_target_pairs={{0,1},{1,2},{2,3},{3,0},{4,5},{5,6},{6,7},{7,4},{8,9},{9,10},{10,1... | collective-permute-start | bytes 24584 | tf_op jit(solution)/shard_map/ppermute | solution.py:474
  53.9 1.9 %collective-permute-start.3 = (bf16[32,128]{1,0:T(8,128)(2,1)S(1)}, bf16[32,128]{1,0:T(8,128)(2,1)S(1)}, u32[]{:S(2)}, u32[]{:S(2)}) collective-permute-start(bf16[32,128]{1,0:T(8,128)(2,1)S(1)} %convert_element_type.9), channel_id=1, source_target_pairs={{0,2},{1,3},{2,0},{3,1},{4,6},{5,7},{6,4},{7,5},{8,10},{9,11},{10,... | collective-permute-start | bytes 24584 | tf_op jit(solution)/shard_map/ppermute | solution.py:474
  55.8 7.7 %all-to-all-done = bf16[256,2,128]{2,1,0:T(2,128)(2,1)S(1)} async-done(((bf16[256,2,128]{2,1,0:T(2,128)(2,1)}), bf16[256,2,128]{2,1,0:T(2,128)(2,1)S(1)}, u32[]{:S(2)}, u32[]{:S(2)}) %all-to-all-start) | async-done | bytes 131104 | tf_op jit(solution)/shard_map/all_to_all | solution.py:478
  63.5 0.7 sum_shares.1
  64.2 5.4 %all-to-all-start.1 = ((bf16[256,2,128]{2,1,0:T(2,128)(2,1)}), bf16[256,2,128]{2,1,0:T(2,128)(2,1)S(1)}, u32[]{:S(2)}, u32[]{:S(2)}) async-start(bf16[256,2,128]{2,1,0:T(2,128)(2,1)} %bitcast.29), calls=%async_computation.1 | async-start | bytes 262144 | tf_op jit(solution)/shard_map/all_to_all | solution.py:488
  69.7 0.6 gather_fusion
  70.3 1.3 %dual_views.1 = f32[64,128]{1,0:T(8,128)} custom-call(s32[1]{0:T(128)} %bitcast.1.meta, bf16[4,32,128]{2,1,0:T(8,128)(2,1)S(1)} %broadcast_select_fusion.strips, s32[128,128]{1,0:T(8,128)S(1)} %bitcast.45, s32[128,128]{1,0:T(8,128)S(1)} %bitcast.47, bf16[8,128,128]{2,1,0:T(8,128)(2,1)S(1)} %copy-done), custom_call_target="tpu_custom_call" | custom-call | tf_op jit(solution)/shard_map/dual_views/pallas_call | solution.py:495
  71.7 10.9 %all-to-all-done.1 = bf16[256,2,128]{2,1,0:T(2,128)(2,1)S(1)} async-done(((bf16[256,2,128]{2,1,0:T(2,128)(2,1)}), bf16[256,2,128]{2,1,0:T(2,128)(2,1)S(1)}, u32[]{:S(2)}, u32[]{:S(2)}) %all-to-all-start.1) | async-done | bytes 131104 | tf_op jit(solution)/shard_map/all_to_all | solution.py:488
  82.6 1.0 %split_grads.1 = (f32[3,3,3,6,32]{4,3,2,1,0:T(8,128)}, f32[3,3,3,32,32]{4,3,2,1,0:T(8,128)}, f32[3,3,5,3,32]{4,3,2,1,0:T(4,128)}) custom-call(bf16[512,128]{1,0:T(8,128)(2,1)S(1)} %bitcast.41), custom_call_target="tpu_custom_call" | custom-call | tf_op jit(solution)/shard_map/split_grads/pallas_call | solution.py:507
  (42 shorter events, 1.0 us)
Async XLA Ops:
  0.6 0.9 %copy-start.1 = (f32[5,4,8,128]{3,2,1,0:T(8,128)S(1)}, f32[5,4,8,128]{3,2,1,0:T(8,128)}, u32[]{:S(2)}) copy-start(f32[5,4,8,128]{3,2,1,0:T(8,128)} %cot.1) | copy-start | bytes 245764
  1.5 0.9 %copy-start.5 = (f32[5,4,8,128]{3,2,1,0:T(8,128)S(1)}, f32[5,4,8,128]{3,2,1,0:T(8,128)}, u32[]{:S(2)}) copy-start(f32[5,4,8,128]{3,2,1,0:T(8,128)} %param.9) | copy-start | bytes 245764
  2.4 0.7 copy-start.6
  3.1 10.9 %copy-start = (bf16[8,128,128]{2,1,0:T(8,128)(2,1)S(1)}, bf16[8,128,128]{2,1,0:T(8,128)(2,1)}, u32[]{:S(2)}) copy-start(bf16[8,128,128]{2,1,0:T(8,128)(2,1)} %prints.3) | copy-start | bytes 786436
  3.2 10.8 %copy-start.3 = (s32[64,128,2]{1,2,0:T(2,128)S(1)}, s32[64,128,2]{1,2,0:T(2,128)}, u32[]{:S(2)}) copy-start(s32[64,128,2]{1,2,0:T(2,128)} %param.12) | copy-start | bytes 196612
  3.2 10.8 %copy-start.4 = (s32[64,128,2]{1,2,0:T(2,128)S(1)}, s32[64,128,2]{1,2,0:T(2,128)}, u32[]{:S(2)}) copy-start(s32[64,128,2]{1,2,0:T(2,128)} %param.13) | copy-start | bytes 196612
  14.0 8.7 %copy-start.7 = (bf16[3,3,3,32,32]{4,3,2,1,0:T(8,128)(2,1)S(1)}, bf16[3,3,3,32,32]{4,3,2,1,0:T(8,128)(2,1)}, u32[]{:S(2)}) copy-start(bf16[3,3,3,32,32]{4,3,2,1,0:T(8,128)(2,1)} %param.15) | copy-start | bytes 165892
  15.3 13.8 %collective-permute-start = (bf16[64,16,128]{2,1,0:T(8,128)(2,1)S(1)}, bf16[64,16,128]{2,1,0:T(8,128)(2,1)S(1)}, u32[]{:S(2)}, u32[]{:S(2)}) collective-permute-start(bf16[64,16,128]{2,1,0:T(8,128)(2,1)S(1)} %box_rows.1.here), channel_id=1, source_target_pairs={{0,4},{4,8},{8,12},{12,16},{16,20},{20,24},{24,28},{28,32},{32,36}... | collective-permute-start | bytes 786440 | tf_op jit(solution)/shard_map/ppermute | solution.py:434
  15.7 13.5 %collective-permute-start.1 = (bf16[64,16,128]{2,1,0:T(8,128)(2,1)S(1)}, bf16[64,16,128]{2,1,0:T(8,128)(2,1)S(1)}, u32[]{:S(2)}, u32[]{:S(2)}) collective-permute-start(bf16[64,16,128]{2,1,0:T(8,128)(2,1)S(1)} %box_rows.1.here), channel_id=1, source_target_pairs={{4,0},{8,4},{12,8},{16,12},{20,16},{24,20},{28,24},{32,28},{36,32}... | collective-permute-start | bytes 786440 | tf_op jit(solution)/shard_map/ppermute | solution.py:435
  22.7 0.8 copy-start.9
  23.6 0.8 copy-start.8
  25.7 3.5 %copy-start.2 = (f32[5,4,8,128]{3,2,1,0:T(8,128)S(1)}, f32[5,4,8,128]{3,2,1,0:T(8,128)}, u32[]{:S(2)}) copy-start(f32[5,4,8,128]{3,2,1,0:T(8,128)} %cot.1) | copy-start | bytes 245764
  40.7 22.7 %all-to-all-start = ((bf16[256,2,128]{2,1,0:T(2,128)(2,1)}), bf16[256,2,128]{2,1,0:T(2,128)(2,1)S(1)}, u32[]{:S(2)}, u32[]{:S(2)}) async-start(bf16[256,2,128]{2,1,0:T(2,128)(2,1)} %bitcast.27), calls=%async_computation | async-start | bytes 262144 | tf_op jit(solution)/shard_map/all_to_all | solution.py:478
  50.7 19.0 %collective-permute-start.2 = (bf16[32,128]{1,0:T(8,128)(2,1)S(1)}, bf16[32,128]{1,0:T(8,128)(2,1)S(1)}, u32[]{:S(2)}, u32[]{:S(2)}) collective-permute-start(bf16[32,128]{1,0:T(8,128)(2,1)S(1)} %convert_element_type.9), channel_id=1, source_target_pairs={{0,1},{1,2},{2,3},{3,0},{4,5},{5,6},{6,7},{7,4},{8,9},{9,10},{10,1... | collective-permute-start | bytes 24584 | tf_op jit(solution)/shard_map/ppermute | solution.py:474
  53.9 15.8 %collective-permute-start.3 = (bf16[32,128]{1,0:T(8,128)(2,1)S(1)}, bf16[32,128]{1,0:T(8,128)(2,1)S(1)}, u32[]{:S(2)}, u32[]{:S(2)}) collective-permute-start(bf16[32,128]{1,0:T(8,128)(2,1)S(1)} %convert_element_type.9), channel_id=1, source_target_pairs={{0,2},{1,3},{2,0},{3,1},{4,6},{5,7},{6,4},{7,5},{8,10},{9,11},{10,... | collective-permute-start | bytes 24584 | tf_op jit(solution)/shard_map/ppermute | solution.py:474
  55.8 13.9 %collective-permute-start.4 = (bf16[32,128]{1,0:T(8,128)(2,1)S(1)}, bf16[32,128]{1,0:T(8,128)(2,1)S(1)}, u32[]{:S(2)}, u32[]{:S(2)}) collective-permute-start(bf16[32,128]{1,0:T(8,128)(2,1)S(1)} %convert_element_type.9), channel_id=1, source_target_pairs={{0,3},{1,0},{2,1},{3,2},{4,7},{5,4},{6,5},{7,6},{8,11},{9,8},{10,9... | collective-permute-start | bytes 24584 | tf_op jit(solution)/shard_map/ppermute | solution.py:474
  64.2 18.4 %all-to-all-start.1 = ((bf16[256,2,128]{2,1,0:T(2,128)(2,1)}), bf16[256,2,128]{2,1,0:T(2,128)(2,1)S(1)}, u32[]{:S(2)}, u32[]{:S(2)}) async-start(bf16[256,2,128]{2,1,0:T(2,128)(2,1)} %bitcast.29), calls=%async_computation.1 | async-start | bytes 262144 | tf_op jit(solution)/shard_map/all_to_all | solution.py:488

commit v4 on v3

--- a/solution.py
+++ b/solution.py
@@ -20,6 +20,7 @@
 HID = 32
 SLOT = 16
 DTL = 4
+SENT = 11
 
 
 def smem_spec():
@@ -30,10 +31,19 @@
     return pl.BlockSpec(memory_space=pltpu.VMEM)
 
 
-def pack_kernel(primal, cotangent, dual, out):
-    out[0:160, :] = primal[...].astype(BF16)
-    out[160:320, :] = cotangent[...].astype(BF16)
-    out[320:, :] = dual[...]
+def pack_kernel(primal, cotangent, dual, out, primal_in, cotangent_in, dual_in, sems):
+    copies = [
+        pltpu.make_async_copy(primal, primal_in, sems.at[0]),
+        pltpu.make_async_copy(cotangent, cotangent_in, sems.at[1]),
+        pltpu.make_async_copy(dual, dual_in, sems.at[2]),
+    ]
+    for copy in copies:
+        copy.start()
+    for copy in copies:
+        copy.wait()
+    out[0:160, :] = primal_in[...].astype(BF16)
+    out[160:320, :] = cotangent_in[...].astype(BF16)
+    out[320:, :] = dual_in[...]
 
 
 def gather_kernel(meta, packed, tiles, foots, prints, out, codes, duals, field, rows):
@@ -70,7 +80,6 @@
         back = back + jnp.dot(low, prints[o], preferred_element_type=F32)
     field[...] = back
 
-    rows[...] = jnp.zeros(rows.shape, F32)
     before = jnp.maximum(view_at - 1, 0)
     after = jnp.minimum(view_at + 1, ranks - 1)
     has_before = view_at > 0
@@ -78,15 +87,15 @@
     full_y = RY * ranks
 
     def place(z, slot, mid, low_side, high_side):
-        base = z * WY * SLOT + slot
-        rows[pl.ds(base, REACH, stride=SLOT), :] = jnp.where(has_before, low_side[RY - REACH :], 0.0)
-        rows[pl.ds(base + REACH * SLOT, RY, stride=SLOT), :] = mid
-        rows[pl.ds(base + (REACH + RY) * SLOT, REACH, stride=SLOT), :] = jnp.where(
+        base = z * WY * SENT + slot
+        rows[pl.ds(base, REACH, stride=SENT), :] = jnp.where(has_before, low_side[RY - REACH :], 0.0)
+        rows[pl.ds(base + REACH * SENT, RY, stride=SENT), :] = mid
+        rows[pl.ds(base + (REACH + RY) * SENT, REACH, stride=SENT), :] = jnp.where(
             has_after, high_side[:REACH], 0.0
         )
 
     for c in range(10):
-        slot = c if c < 5 else c + 3
+        slot = c if c < 5 else c + 1
         mid = packed[view_at, c * 32 : c * 32 + 32, :].astype(F32)
         low_side = packed[before, c * 32 : c * 32 + 32, :].astype(F32)
         high_side = packed[after, c * 32 : c * 32 + 32, :].astype(F32)
@@ -96,7 +105,7 @@
     for z in range(CZ):
         at = lambda rank: field[pl.ds(pl.multiple_of(z * full_y + rank * RY, RY), RY), :]
         place(z, 5, at(view_at), at(before), at(after))
-    out[...] = rows[...].reshape(out.shape).astype(BF16)
+    out[...] = rows[...].astype(BF16)
 
 
 def lane_masks(shape):
@@ -136,42 +145,50 @@
     return jnp.where(row == source, 1.0, 0.0).astype(BF16)
 
 
+def spread_matrix():
+    shape = (WY * SLOT, WY * SENT)
+    row = lax.broadcasted_iota(jnp.int32, shape, 0)
+    col = lax.broadcasted_iota(jnp.int32, shape, 1)
+    slot = row & (SLOT - 1)
+    channel = jnp.where(slot < 6, slot, jnp.where((slot >= 8) & (slot < 13), slot - 2, -WY * SENT))
+    return jnp.where(col == (row >> 4) * SENT + channel, 1.0, 0.0).astype(BF16)
+
+
 def pipelined(count, multiply, finish, first_buf, second_buf):
     multiply(0, first_buf)
 
-    def step(i, carry):
-        multiply(2 * i + 1, second_buf)
-        finish(2 * i, first_buf)
-        multiply(2 * i + 2, first_buf)
-        finish(2 * i + 1, second_buf)
-        return carry
-
-    lax.fori_loop(0, count // 2 - 1, step, 0)
-    multiply(count - 1, second_buf)
-    finish(count - 2, first_buf)
-    finish(count - 1, second_buf)
+    bufs = (first_buf, second_buf)
+    for z in range(1, count):
+        multiply(z, bufs[z % 2])
+        finish(z - 1, bufs[1 - z % 2])
+    finish(count - 1, bufs[1 - count % 2])
 
 
 def net_kernel(
-    meta, prev, here, following, cot, w_in, w_mid, w_mid_flip, w_first_flip,
-    d_primal, strip, packed,
-    grads, ends_grad, mid_grad, buf_a, buf_b, box, slope, dz_two, z_one, z_two, da_two, da_one, dx,
+    meta, paired, here, crossed, w_in, w_mid, w_mid_flip,
+    da_one, packed,
+    grads, ends_grad, mid_grad, buf_a, buf_b, box, slope, dz_two, z_one, z_two, da_two,
 ):
     slab_at, view_at, slabs, ranks = meta[0], meta[1], meta[2], meta[3]
     sides = side_matrix()
+    spread = spread_matrix()
     per = CZ * WY
-    has = (slab_at > 0, None, slab_at < slabs - 1)
-    for part, source in enumerate((prev, here, following)):
-        for at in range(0, per, WY):
-            rows = source[at : at + WY]
-            if has[part] is not None:
-                rows = jnp.where(has[part], rows, jnp.zeros_like(rows))
-            both = jnp.dot(
-                rows.reshape(WY * SLOT, LANES), sides, preferred_element_type=F32
-            ).astype(BF16)
-            to = slice(part * per + at, part * per + at + WY)
+    odd = slab_at % 2 == 1
+    has_prev, has_next = slab_at > 0, slab_at < slabs - 1
+    for part in range(3):
+        for z in range(CZ):
+            cut = slice(z * WY * SENT, (z + 1) * WY * SENT)
+            if part == 1:
+                rows = here[cut]
+            else:
+                towards, away = paired[cut], crossed[cut]
+                rows = jnp.where(odd, towards, away) if part == 0 else jnp.where(odd, away, towards)
+                rows = jnp.where(has_next if part else has_prev, rows, jnp.zeros_like(rows))
+            rows = jnp.dot(spread, rows, preferred_element_type=F32).astype(BF16)
+            both = jnp.dot(rows, sides, preferred_element_type=F32).astype(BF16)
+            to = slice(part * per + z * WY, part * per + (z + 1) * WY)
             box[to, 0:SLOT, :] = both[:, :LANES].reshape(WY, SLOT, LANES)
-            box[to, SLOT : 2 * SLOT, :] = rows
+            box[to, SLOT : 2 * SLOT, :] = rows.reshape(WY, SLOT, LANES)
             box[to, 2 * SLOT : 3 * SLOT, :] = both[:, LANES:].reshape(WY, SLOT, LANES)
     first, last = lane_masks((HID, LANES))
     z_start, y_start = slab_at * CZ, view_at * RY
@@ -230,17 +247,11 @@
 
     pipelined(depth1, times(w_mid_flip, da_two, rows2, rows1), finish_back, buf_a, buf_b)
 
-    first8, last8 = lane_masks((8, LANES))
     ends_grad[...] = jnp.zeros(ends_grad.shape, F32)
     mid_grad[...] = jnp.zeros(mid_grad.shape, F32)
     contract = (((1,), (1,)), ((), ()))
 
     def layer_out(z, carry):
-        for y in range(0, RY, 2):
-            taps = jnp.dot(w_first_flip[...], window(da_one, rows1, z, y), preferred_element_type=F32)
-            for s in range(2):
-                at = pl.multiple_of((z * RY + y + s) * 8, 8)
-                dx[pl.ds(at, 8), :] = shift_sum(taps[:, s * LANES : (s + 1) * LANES], first8, last8)
         inner = z_one[pl.ds((z + 3) * rows3 + 3, RY)]
         both = jnp.dot(
             inner.reshape(RY * HID, LANES), sides, preferred_element_type=F32
@@ -276,10 +287,6 @@
 
     lax.fori_loop(0, CZ, layer_out, 0)
 
-    for z in range(CZ):
-        for c in range(5):
-            d_primal[c, z] = cot[c, z] + dx[pl.ds(z * RY * 8 + c, RY, stride=8), :]
-        strip[z * RY : (z + 1) * RY, :] = dx[pl.ds(z * RY * 8 + 5, RY, stride=8), :]
     grads[...] = jnp.zeros(grads.shape, F32)
     grads[0:288, 0 : 3 * HID] = mid_grad[...]
     for tap in range(9):
@@ -291,6 +298,23 @@
             grads[to + 8 : to + 16, cut] = ends_grad[at + 8 : at + 16, HID : 2 * HID]
     packed[0 : grads.shape[0], :] = grads[...].astype(BF16)
     packed[grads.shape[0] :, :] = jnp.zeros((packed.shape[0] - grads.shape[0], LANES), BF16)
+
+
+def last_kernel(da_one, cot, w_first_flip, d_primal, strip, dx):
+    rows1 = RY + 2
+    first, last = lane_masks((8, LANES))
+    for z in range(CZ):
+        for y in range(0, RY, 2):
+            taps = jnp.dot(w_first_flip[...], window(da_one, rows1, z, y), preferred_element_type=F32)
+            for s in range(2):
+                at = (z * RY + y + s) * 8
+                dx[at : at + 8, :] = shift_sum(taps[:, s * LANES : (s + 1) * LANES], first, last)
+    fields = []
+    for z in range(CZ):
+        for c in range(5):
+            d_primal[c, z] = cot[c, z] + dx[pl.ds(z * RY * 8 + c, RY, stride=8), :]
+        fields.append(dx[pl.ds(z * RY * 8 + 5, RY, stride=8), :])
+    strip[...] = jnp.concatenate(fields, axis=0).astype(BF16)
 
 
 def dual_kernel(meta, strips, tiles, foots, prints, out, codes):
@@ -403,8 +427,14 @@
     packed = pl.pallas_call(
         pack_kernel,
         out_shape=jax.ShapeDtypeStruct((320 + views_here * det_tiles, LANES), BF16),
-        in_specs=[vmem_spec()] * 3,
+        in_specs=[pl.BlockSpec(memory_space=pl.ANY)] * 3,
         out_specs=vmem_spec(),
+        scratch_shapes=[
+            pltpu.VMEM((160, LANES), F32),
+            pltpu.VMEM((160, LANES), F32),
+            pltpu.VMEM((views_here * det_tiles, LANES), BF16),
+            pltpu.SemaphoreType.DMA((3,)),
+        ],
         compiler_params=PARAMS,
         interpret=INTERPRET,
         name="pack_inputs",
@@ -417,22 +447,23 @@
 
     here = pl.pallas_call(
         gather_kernel,
-        out_shape=jax.ShapeDtypeStruct((CZ * WY, SLOT, LANES), BF16),
+        out_shape=jax.ShapeDtypeStruct((CZ * WY * SENT, LANES), BF16),
         in_specs=[smem_spec()] + [vmem_spec()] * 4,
         out_specs=vmem_spec(),
         scratch_shapes=[
             pltpu.VMEM((all_views * taps, tiles_here), F32),
             pltpu.VMEM((all_views * det_tiles, LANES), F32),
             pltpu.VMEM((tiles_here, LANES), F32),
-            pltpu.VMEM((CZ * WY * SLOT, LANES), F32),
+            pltpu.VMEM((CZ * WY * SENT, LANES), F32),
         ],
         compiler_params=PARAMS,
         interpret=INTERPRET,
         name="box_rows",
     )(meta, packed, tiles, foots, footprints)
 
-    prev = lax.ppermute(here, "slab", [(i, (i + 1) % slabs) for i in range(slabs)])
-    following = lax.ppermute(here, "slab", [((i + 1) % slabs, i) for i in range(slabs)])
+    inner = lambda i: i if i == 0 or i == slabs - 1 else ((i - 1) ^ 1) + 1
+    paired = lax.ppermute(here, "slab", [(i, i ^ 1) for i in range(slabs)])
+    crossed = lax.ppermute(here, "slab", [(i, inner(i)) for i in range(slabs)])
 
     w_in = jnp.concatenate([by_taps(w_first, 0), by_taps(flipped(w_last), 8)], axis=0)
     w_mid = by_rows(w_middle, HID, HID)
@@ -440,15 +471,14 @@
     w_first_flip = by_rows(flipped(w_first), HID, 8)
 
     rows3, rows2, rows1 = 140, 96, 60
-    d_primal, strip, grads = pl.pallas_call(
+    da_one, grads = pl.pallas_call(
         net_kernel,
         out_shape=(
-            jax.ShapeDtypeStruct(primal.shape, F32),
-            jax.ShapeDtypeStruct((CZ * RY, LANES), F32),
+            jax.ShapeDtypeStruct((rows1, HID, LANES), BF16),
             jax.ShapeDtypeStruct((2 * devices if devices >= 256 else 32 * devices, LANES), BF16),
         ),
-        in_specs=[smem_spec()] + [vmem_spec()] * 8,
-        out_specs=(vmem_spec(),) * 3,
+        in_specs=[smem_spec()] + [vmem_spec()] * 6,
+        out_specs=(vmem_spec(),) * 2,
         scratch_shapes=[
             pltpu.VMEM((432, LANES), F32),
             pltpu.VMEM((27 * SLOT, 2 * HID), F32),
@@ -461,21 +491,33 @@
             pltpu.VMEM((rows3, HID, LANES), BF16),
             pltpu.VMEM((rows2, HID, LANES), BF16),
             pltpu.VMEM((rows2, HID, LANES), BF16),
-            pltpu.VMEM((rows1, HID, LANES), BF16),
-            pltpu.VMEM((CZ * RY * 8, LANES), F32),
         ],
         compiler_params=PARAMS,
         interpret=INTERPRET,
         name="net_box",
-    )(meta_net, prev, here, following, cotangent, w_in, w_mid, w_mid_flip, w_first_flip)
-
-    strip = strip.astype(BF16)
-    ring = lambda step: [(i, (i + step) % ranks) for i in range(ranks)]
-    others = [lax.ppermute(strip, "view", ring(step)) for step in range(1, ranks)]
+    )(meta_net, paired, here, crossed, w_in, w_mid, w_mid_flip)
 
     both = ("slab", "view")
     per = grads.shape[0] // devices
     shares = lax.all_to_all(grads.reshape(devices, per, LANES), both, 0, 0, tiled=True)
+
+    d_primal, strip = pl.pallas_call(
+        last_kernel,
+        out_shape=(
+            jax.ShapeDtypeStruct(primal.shape, F32),
+            jax.ShapeDtypeStruct((CZ * RY, LANES), BF16),
+        ),
+        in_specs=[vmem_spec()] * 3,
+        out_specs=(vmem_spec(),) * 2,
+        scratch_shapes=[pltpu.VMEM((CZ * RY * 8, LANES), F32)],
+        compiler_params=PARAMS,
+        interpret=INTERPRET,
+        name="last_layer",
+    )(da_one, cotangent, w_first_flip)
+
+    ring = lambda step: [(i, (i + step) % ranks) for i in range(ranks)]
+    others = [lax.ppermute(strip, "view", ring(step)) for step in range(1, ranks)]
+
     summed = pl.pallas_call(
         sum_call(per),
         out_shape=jax.ShapeDtypeStruct(grads.shape, BF16),

time: 84 us -> 84.5 us (level)
  waiting for transfers between devices: 22.1 us -> 18.8 us
  starting transfers between devices: 27.8 us -> 30.7 us
    all_to_all x1, starting transfers between devices: 9.92 us -> 17.5 us  [shards(): lax.all_to_all(grads.reshape(devices, per, LANES), both, 0, 0, tiled=True)]
    ppermute x2, starting transfers between devices: 7.41 us -> 1.02 us  [the longest x1 0.66 us: shards(): crossed = lax.ppermute(here, 'slab', [(i, inner(i)) for i in range(slabs)])]
    all_to_all x1, waiting for transfers between devices: 7.69 us -> 5.6 us  [shards(): lax.all_to_all(grads.reshape(devices, per, LANES), both, 0, 0, tiled=True)]
    all_to_all x1, starting transfers between devices: 5.44 us -> 7.24 us  [shards(): lax.all_to_all(summed.reshape(shares.shape), both, 0, 0, tiled=True)]
    ppermute x2, waiting for transfers between devices: 3.44 us -> 2.38 us  [the longest x1 2.38 us: shards(): paired = lax.ppermute(here, 'slab', [(i, i ^ 1) for i in range(slabs)])]
    pallas_call x2 -> x3, Pallas kernels: 12.9 us -> 12.9 us  [the longest x1 10.4 us: shards(): pl.pallas_call(net_kernel, out_shape=(jax.ShapeDtypeStruct((rows1, HID, L...]
  transfers between devices with their start and end apart: 7 -> 7, of which waited for: 3 -> 3; matrix products, arithmetic and copies ran while one was open for 2% -> 2% of each run, Pallas kernels for 2% -> 4%
where the time goes in v4:
time: 84.5 us; the launch traced here: 84 us
  starting transfers between devices  30.7 us (36%)
  waiting for transfers between devices  18.8 us (22%)
  Pallas kernels  16.2 us (19%)
  blocking collectives  10.8 us (13%)
  local copies, waits for them, and re-layouts  6.35 us (8%)
  between operations  0.9 us (1%)
    all_to_all x1, starting transfers between devices, shards(): lax.all_to_all(grads.reshape(devices, per, LANES), both, 0, 0, tiled=True)  17.5 us
    all_gather x1, blocking collectives, shards(): packed = lax.all_gather(packed, 'view', axis=0, tiled=False)  10.8 us
    all_to_all x1, waiting for transfers between devices, shards(): lax.all_to_all(summed.reshape(shares.shape), both, 0, 0, tiled=True)  10.8 us
    pallas_call x1, Pallas kernels, shards(): pl.pallas_call(net_kernel, out_shape=(jax.ShapeDtypeStruct((rows1, HID, L...  10.4 us
    all_to_all x1, starting transfers between devices, shards(): lax.all_to_all(summed.reshape(shares.shape), both, 0, 0, tiled=True)  7.24 us
    all_to_all x1, waiting for transfers between devices, shards(): lax.all_to_all(grads.reshape(devices, per, LANES), both, 0, 0, tiled=True)  5.6 us
    ppermute x3, starting transfers between devices, shards(): lax.ppermute(strip, 'view', ring(step))  5 us
    unnamed x20, local copies, waits for them, and re-layouts  4.55 us
  transfers between devices with their start and end apart: 7, of which 3 were waited for; matrix products, arithmetic and copies ran while one was open for 2% of the time, Pallas kernels for 4%

profile of v4, /device:TPU:1, one launch (start us, length us, event | category | flops | bytes accessed | tf_op | source)
XLA Modules:
  0.0 84.0 jit_solution(15300123588495890124)
XLA Ops:
  0.6 0.9 %copy-done.1 = f32[5,4,8,128]{3,2,1,0:T(8,128)S(1)} copy-done((f32[5,4,8,128]{3,2,1,0:T(8,128)S(1)}, f32[5,4,8,128]{3,2,1,0:T(8,128)}, u32[]{:S(2)}) %copy-start.1) | copy-done | bytes 81944
  1.5 0.9 %copy-done.5 = f32[5,4,8,128]{3,2,1,0:T(8,128)S(1)} copy-done((f32[5,4,8,128]{3,2,1,0:T(8,128)S(1)}, f32[5,4,8,128]{3,2,1,0:T(8,128)}, u32[]{:S(2)}) %copy-start.5) | copy-done | bytes 81944
  2.4 0.7 copy-done.6
  3.1 0.2 pack_inputs.1
  3.4 10.8 %all-gather = bf16[1536,128]{1,0:T(8,128)(2,1)S(1)} all-gather(bf16[384,128]{1,0:T(8,128)(2,1)S(1)} %pack_inputs.1), channel_id=2, replica_groups=mesh['slab'=64,'view'=4] {'view'}, dimensions={0}, use_global_device_ids=true | all-gather | bytes 491520 | tf_op jit(solution)/shard_map/all_gather | solution.py:446
  14.2 1.2 %box_rows.1.here = bf16[704,128]{1,0:T(8,128)(2,1)S(1)} custom-call(s32[1]{0:T(128)} %bitcast.1.meta, bf16[4,384,128]{2,1,0:T(8,128)(2,1)S(1)} %bitcast.39, s32[128,128]{1,0:T(8,128)S(1)} %bitcast.43, s32[128,128]{1,0:T(8,128)S(1)} %bitcast.45, bf16[8,128,128]{2,1,0:T(8,128)(2,1)S(1)} %copy-done), custom_call_target="tpu_custom_call" | custom-call | tf_op jit(solution)/shard_map/box_rows/pallas_call | solution.py:448
  15.5 0.4 collective-permute-start
  15.8 0.7 collective-permute-start.1
  16.9 0.6 copy-done.9
  17.8 0.7 copy-done.8
  19.1 2.4 %collective-permute-done.paired = bf16[704,128]{1,0:T(8,128)(2,1)S(1)} collective-permute-done((bf16[704,128]{1,0:T(8,128)(2,1)S(1)}, bf16[704,128]{1,0:T(8,128)(2,1)S(1)}, u32[]{:S(2)}, u32[]{:S(2)}) %collective-permute-start) | collective-permute-done | bytes 180256 | tf_op jit(solution)/shard_map/ppermute | solution.py:465
  21.5 10.4 %net_box.1 = (bf16[60,32,128]{2,1,0:T(8,128)(2,1)S(1)}, bf16[512,128]{1,0:T(8,128)(2,1)}) custom-call(s32[4]{0:T(128)S(1)} %pad_add_fusion.meta, bf16[704,128]{1,0:T(8,128)(2,1)S(1)} %collective-permute-done.paired, bf16[704,128]{1,0:T(8,128)(2,1)S(1)} %box_rows.1.here, bf16[704,128]{1,0:T(8,128)(2,1)S(1)} %collective-permute-done.1.crossed, ...), custom_call_target="tpu_custom_call" | custom-call | tf_op jit(solution)/shard_map/net_box/pallas_call | solution.py:474
  31.9 17.5 %all-to-all-start = ((bf16[256,2,128]{2,1,0:T(2,128)(2,1)}), bf16[256,2,128]{2,1,0:T(2,128)(2,1)S(1)}, u32[]{:S(2)}, u32[]{:S(2)}) async-start(bf16[256,2,128]{2,1,0:T(2,128)(2,1)} %bitcast.27), calls=%async_computation | async-start | bytes 262144 | tf_op jit(solution)/shard_map/all_to_all | solution.py:502
  49.6 0.7 copy-done.2
  50.3 1.3 %last_layer.1 = (f32[5,4,8,128]{3,2,1,0:T(8,128)}, bf16[32,128]{1,0:T(8,128)(2,1)S(1)}) custom-call(bf16[60,32,128]{2,1,0:T(8,128)(2,1)S(1)} %get-tuple-element.12.da_one, f32[5,4,8,128]{3,2,1,0:T(8,128)S(1)} %copy-done.2, bf16[24,288]{1,0:T(8,128)(2,1)S(1)} %reshape.118.w_first_flip), custom_call_target="tpu_custom_call" | custom-call | tf_op jit(solution)/shard_map/last_layer/pallas_call | solution.py:504
  51.6 3.1 %collective-permute-start.2 = (bf16[32,128]{1,0:T(8,128)(2,1)S(1)}, bf16[32,128]{1,0:T(8,128)(2,1)S(1)}, u32[]{:S(2)}, u32[]{:S(2)}) collective-permute-start(bf16[32,128]{1,0:T(8,128)(2,1)S(1)} %get-tuple-element.14), channel_id=1, source_target_pairs={{0,1},{1,2},{2,3},{3,0},{4,5},{5,6},{6,7},{7,4},{8,9},{9,10},{10,1... | collective-permute-start | bytes 24584 | tf_op jit(solution)/shard_map/ppermute | solution.py:519
  54.7 1.9 %collective-permute-start.3 = (bf16[32,128]{1,0:T(8,128)(2,1)S(1)}, bf16[32,128]{1,0:T(8,128)(2,1)S(1)}, u32[]{:S(2)}, u32[]{:S(2)}) collective-permute-start(bf16[32,128]{1,0:T(8,128)(2,1)S(1)} %get-tuple-element.14), channel_id=1, source_target_pairs={{0,2},{1,3},{2,0},{3,1},{4,6},{5,7},{6,4},{7,5},{8,10},{9,11},{10,... | collective-permute-start | bytes 24584 | tf_op jit(solution)/shard_map/ppermute | solution.py:519
  56.6 5.6 %all-to-all-done = bf16[256,2,128]{2,1,0:T(2,128)(2,1)S(1)} async-done(((bf16[256,2,128]{2,1,0:T(2,128)(2,1)}), bf16[256,2,128]{2,1,0:T(2,128)(2,1)S(1)}, u32[]{:S(2)}, u32[]{:S(2)}) %all-to-all-start) | async-done | bytes 131104 | tf_op jit(solution)/shard_map/all_to_all | solution.py:502
  62.2 0.7 sum_shares.1
  62.9 7.2 %all-to-all-start.1 = ((bf16[256,2,128]{2,1,0:T(2,128)(2,1)}), bf16[256,2,128]{2,1,0:T(2,128)(2,1)S(1)}, u32[]{:S(2)}, u32[]{:S(2)}) async-start(bf16[256,2,128]{2,1,0:T(2,128)(2,1)} %bitcast.29), calls=%async_computation.1 | async-start | bytes 262144 | tf_op jit(solution)/shard_map/all_to_all | solution.py:530
  70.2 0.6 gather_fusion
  70.9 1.3 %dual_views.1 = f32[64,128]{1,0:T(8,128)} custom-call(s32[1]{0:T(128)} %bitcast.1.meta, bf16[4,32,128]{2,1,0:T(8,128)(2,1)S(1)} %broadcast_select_fusion.strips, s32[128,128]{1,0:T(8,128)S(1)} %bitcast.44, s32[128,128]{1,0:T(8,128)S(1)} %bitcast.46, bf16[8,128,128]{2,1,0:T(8,128)(2,1)S(1)} %copy-done), custom_call_target="tpu_custom_call" | custom-call | tf_op jit(solution)/shard_map/dual_views/pallas_call | solution.py:537
  72.2 10.8 %all-to-all-done.1 = bf16[256,2,128]{2,1,0:T(2,128)(2,1)S(1)} async-done(((bf16[256,2,128]{2,1,0:T(2,128)(2,1)}), bf16[256,2,128]{2,1,0:T(2,128)(2,1)S(1)}, u32[]{:S(2)}, u32[]{:S(2)}) %all-to-all-start.1) | async-done | bytes 131104 | tf_op jit(solution)/shard_map/all_to_all | solution.py:530
  83.0 1.0 %split_grads.1 = (f32[3,3,3,6,32]{4,3,2,1,0:T(8,128)}, f32[3,3,3,32,32]{4,3,2,1,0:T(8,128)}, f32[3,3,5,3,32]{4,3,2,1,0:T(4,128)}) custom-call(bf16[512,128]{1,0:T(8,128)(2,1)S(1)} %bitcast.41), custom_call_target="tpu_custom_call" | custom-call | tf_op jit(solution)/shard_map/split_grads/pallas_call | solution.py:549
  (41 shorter events, 1.5 us)
Async XLA Ops:
  0.6 0.9 %copy-start.1 = (f32[5,4,8,128]{3,2,1,0:T(8,128)S(1)}, f32[5,4,8,128]{3,2,1,0:T(8,128)}, u32[]{:S(2)}) copy-start(f32[5,4,8,128]{3,2,1,0:T(8,128)} %cot.1) | copy-start | bytes 245764
  1.5 0.9 %copy-start.5 = (f32[5,4,8,128]{3,2,1,0:T(8,128)S(1)}, f32[5,4,8,128]{3,2,1,0:T(8,128)}, u32[]{:S(2)}) copy-start(f32[5,4,8,128]{3,2,1,0:T(8,128)} %param.9) | copy-start | bytes 245764
  2.4 0.7 copy-start.6
  3.4 10.9 %copy-start = (bf16[8,128,128]{2,1,0:T(8,128)(2,1)S(1)}, bf16[8,128,128]{2,1,0:T(8,128)(2,1)}, u32[]{:S(2)}) copy-start(bf16[8,128,128]{2,1,0:T(8,128)(2,1)} %prints.3) | copy-start | bytes 786436
  3.4 10.8 %copy-start.3 = (s32[64,128,2]{1,2,0:T(2,128)S(1)}, s32[64,128,2]{1,2,0:T(2,128)}, u32[]{:S(2)}) copy-start(s32[64,128,2]{1,2,0:T(2,128)} %param.12) | copy-start | bytes 196612
  3.4 10.8 %copy-start.4 = (s32[64,128,2]{1,2,0:T(2,128)S(1)}, s32[64,128,2]{1,2,0:T(2,128)}, u32[]{:S(2)}) copy-start(s32[64,128,2]{1,2,0:T(2,128)} %param.13) | copy-start | bytes 196612
  14.2 2.3 %copy-start.7 = (bf16[3,3,3,32,32]{4,3,2,1,0:T(8,128)(2,1)S(1)}, bf16[3,3,3,32,32]{4,3,2,1,0:T(8,128)(2,1)}, u32[]{:S(2)}) copy-start(bf16[3,3,3,32,32]{4,3,2,1,0:T(8,128)(2,1)} %param.15) | copy-start | bytes 165892
  15.5 6.0 %collective-permute-start = (bf16[704,128]{1,0:T(8,128)(2,1)S(1)}, bf16[704,128]{1,0:T(8,128)(2,1)S(1)}, u32[]{:S(2)}, u32[]{:S(2)}) collective-permute-start(bf16[704,128]{1,0:T(8,128)(2,1)S(1)} %box_rows.1.here), channel_id=1, source_target_pairs={{0,4},{4,0},{8,12},{12,8},{16,20},{20,16},{24,28},{28,24},{32,36},... | collective-permute-start | bytes 540680 | tf_op jit(solution)/shard_map/ppermute | solution.py:465
  15.8 5.7 %collective-permute-start.1 = (bf16[704,128]{1,0:T(8,128)(2,1)S(1)}, bf16[704,128]{1,0:T(8,128)(2,1)S(1)}, u32[]{:S(2)}, u32[]{:S(2)}) collective-permute-start(bf16[704,128]{1,0:T(8,128)(2,1)S(1)} %box_rows.1.here), channel_id=1, source_target_pairs={{0,0},{4,8},{8,4},{12,16},{16,12},{20,24},{24,20},{28,32},{32,28},... | collective-permute-start | bytes 540680 | tf_op jit(solution)/shard_map/ppermute | solution.py:466
  16.7 0.8 copy-start.9
  17.7 0.8 copy-start.8
  31.9 30.3 %all-to-all-start = ((bf16[256,2,128]{2,1,0:T(2,128)(2,1)}), bf16[256,2,128]{2,1,0:T(2,128)(2,1)S(1)}, u32[]{:S(2)}, u32[]{:S(2)}) async-start(bf16[256,2,128]{2,1,0:T(2,128)(2,1)} %bitcast.27), calls=%async_computation | async-start | bytes 262144 | tf_op jit(solution)/shard_map/all_to_all | solution.py:502
  49.4 0.9 %copy-start.2 = (f32[5,4,8,128]{3,2,1,0:T(8,128)S(1)}, f32[5,4,8,128]{3,2,1,0:T(8,128)}, u32[]{:S(2)}) copy-start(f32[5,4,8,128]{3,2,1,0:T(8,128)} %cot.1) | copy-start | bytes 245764
  51.6 18.6 %collective-permute-start.2 = (bf16[32,128]{1,0:T(8,128)(2,1)S(1)}, bf16[32,128]{1,0:T(8,128)(2,1)S(1)}, u32[]{:S(2)}, u32[]{:S(2)}) collective-permute-start(bf16[32,128]{1,0:T(8,128)(2,1)S(1)} %get-tuple-element.14), channel_id=1, source_target_pairs={{0,1},{1,2},{2,3},{3,0},{4,5},{5,6},{6,7},{7,4},{8,9},{9,10},{10,1... | collective-permute-start | bytes 24584 | tf_op jit(solution)/shard_map/ppermute | solution.py:519
  54.7 15.5 %collective-permute-start.3 = (bf16[32,128]{1,0:T(8,128)(2,1)S(1)}, bf16[32,128]{1,0:T(8,128)(2,1)S(1)}, u32[]{:S(2)}, u32[]{:S(2)}) collective-permute-start(bf16[32,128]{1,0:T(8,128)(2,1)S(1)} %get-tuple-element.14), channel_id=1, source_target_pairs={{0,2},{1,3},{2,0},{3,1},{4,6},{5,7},{6,4},{7,5},{8,10},{9,11},{10,... | collective-permute-start | bytes 24584 | tf_op jit(solution)/shard_map/ppermute | solution.py:519
  56.6 13.6 %collective-permute-start.4 = (bf16[32,128]{1,0:T(8,128)(2,1)S(1)}, bf16[32,128]{1,0:T(8,128)(2,1)S(1)}, u32[]{:S(2)}, u32[]{:S(2)}) collective-permute-start(bf16[32,128]{1,0:T(8,128)(2,1)S(1)} %get-tuple-element.14), channel_id=1, source_target_pairs={{0,3},{1,0},{2,1},{3,2},{4,7},{5,4},{6,5},{7,6},{8,11},{9,8},{10,9... | collective-permute-start | bytes 24584 | tf_op jit(solution)/shard_map/ppermute | solution.py:519
  62.9 20.1 %all-to-all-start.1 = ((bf16[256,2,128]{2,1,0:T(2,128)(2,1)}), bf16[256,2,128]{2,1,0:T(2,128)(2,1)S(1)}, u32[]{:S(2)}, u32[]{:S(2)}) async-start(bf16[256,2,128]{2,1,0:T(2,128)(2,1)} %bitcast.29), calls=%async_computation.1 | async-start | bytes 262144 | tf_op jit(solution)/shard_map/all_to_all | solution.py:530

commit v5 on v4

--- a/solution.py
+++ b/solution.py
@@ -6,6 +6,7 @@
 from jax.experimental import pallas as pl
 from jax.experimental.pallas import tpu as pltpu
 from jax.sharding import PartitionSpec as P
+
 
 F32 = jnp.float32
 BF16 = jnp.bfloat16
@@ -29,6 +30,10 @@
 
 def vmem_spec():
     return pl.BlockSpec(memory_space=pltpu.VMEM)
+
+
+def in_hbm(array):
+    return array if INTERPRET else pltpu.with_memory_space_constraint(array, pltpu.HBM)
 
 
 def pack_kernel(primal, cotangent, dual, out, primal_in, cotangent_in, dual_in, sems):
@@ -113,12 +118,6 @@
     return lane == 0, lane == LANES - 1
 
 
-def shifted(value, first, last):
-    left = jnp.where(first, 0.0, pltpu.roll(value, 1, 1))
-    right = jnp.where(last, 0.0, pltpu.roll(value, LANES - 1, 1))
-    return left, value, right
-
-
 def shift_sum(taps, first, last):
     step = taps.shape[0] // 3
     left = jnp.where(first, 0.0, pltpu.roll(taps[:step], 1, 1))
@@ -176,20 +175,27 @@
     odd = slab_at % 2 == 1
     has_prev, has_next = slab_at > 0, slab_at < slabs - 1
     for part in range(3):
-        for z in range(CZ):
-            cut = slice(z * WY * SENT, (z + 1) * WY * SENT)
-            if part == 1:
-                rows = here[cut]
-            else:
-                towards, away = paired[cut], crossed[cut]
-                rows = jnp.where(odd, towards, away) if part == 0 else jnp.where(odd, away, towards)
-                rows = jnp.where(has_next if part else has_prev, rows, jnp.zeros_like(rows))
-            rows = jnp.dot(spread, rows, preferred_element_type=F32).astype(BF16)
-            both = jnp.dot(rows, sides, preferred_element_type=F32).astype(BF16)
-            to = slice(part * per + z * WY, part * per + (z + 1) * WY)
-            box[to, 0:SLOT, :] = both[:, :LANES].reshape(WY, SLOT, LANES)
-            box[to, SLOT : 2 * SLOT, :] = rows.reshape(WY, SLOT, LANES)
-            box[to, 2 * SLOT : 3 * SLOT, :] = both[:, LANES:].reshape(WY, SLOT, LANES)
+        for z in range(0, CZ, 2):
+            pair = []
+            for at in range(z, z + 2):
+                cut = slice(at * WY * SENT, (at + 1) * WY * SENT)
+                if part == 1:
+                    rows = here[cut]
+                else:
+                    near, far = paired[cut], crossed[cut]
+                    rows = jnp.where(odd, near, far) if part == 0 else jnp.where(odd, far, near)
+                    rows = jnp.where(has_next if part else has_prev, rows, jnp.zeros_like(rows))
+                pair.append(rows)
+            spaced = jnp.dot(
+                spread, jnp.concatenate(pair, axis=1), preferred_element_type=F32
+            ).astype(BF16)
+            for at in range(2):
+                rows = spaced[:, at * LANES : (at + 1) * LANES]
+                both = jnp.dot(rows, sides, preferred_element_type=F32).astype(BF16)
+                to = slice(part * per + (z + at) * WY, part * per + (z + at + 1) * WY)
+                box[to, 0:SLOT, :] = both[:, :LANES].reshape(WY, SLOT, LANES)
+                box[to, SLOT : 2 * SLOT, :] = rows.reshape(WY, SLOT, LANES)
+                box[to, 2 * SLOT : 3 * SLOT, :] = both[:, LANES:].reshape(WY, SLOT, LANES)
     first, last = lane_masks((HID, LANES))
     z_start, y_start = slab_at * CZ, view_at * RY
     z_end, y_end = slabs * CZ, ranks * RY
@@ -281,7 +287,9 @@
         )
         low = jnp.concatenate([window(box, WY, z + 3, y + 3) for y in range(0, RY, 2)], axis=1)
         mid = jnp.concatenate([window(da_two, rows2, z + 1, y + 1) for y in range(0, RY, 2)], axis=1)
-        ends_grad[...] += lax.dot_general(low, ends, contract, preferred_element_type=F32)
+        ends_grad[0 : 2 * HID, 0 : 27 * SLOT] += lax.dot_general(
+            ends, low, contract, preferred_element_type=F32
+        )
         mid_grad[...] += lax.dot_general(mid, mids, contract, preferred_element_type=F32)
         return carry
 
@@ -289,13 +297,14 @@
 
     grads[...] = jnp.zeros(grads.shape, F32)
     grads[0:288, 0 : 3 * HID] = mid_grad[...]
+    turned = ends_grad[...].T
     for tap in range(9):
         for shift in range(3):
             at = (tap * 3 + shift) * SLOT
             to = 288 + tap * SLOT
             cut = slice(shift * HID, (shift + 1) * HID)
-            grads[to : to + 8, cut] = ends_grad[at : at + 8, 0:HID]
-            grads[to + 8 : to + 16, cut] = ends_grad[at + 8 : at + 16, HID : 2 * HID]
+            grads[to : to + 8, cut] = turned[at : at + 8, 0:HID]
+            grads[to + 8 : to + 16, cut] = turned[at + 8 : at + 16, HID : 2 * HID]
     packed[0 : grads.shape[0], :] = grads[...].astype(BF16)
     packed[grads.shape[0] :, :] = jnp.zeros((packed.shape[0] - grads.shape[0], LANES), BF16)
 
@@ -412,7 +421,7 @@
 def shards(
     primal, dual, footprints, tile_index, footprint_offset, w_first, w_middle, w_last, cotangent
 ):
-    views_here, det_tiles, bins = dual.shape
+    views_here, det_tiles, _ = dual.shape
     all_views, tiles_here, taps = tile_index.shape
     ranks = lax.axis_size("view")
     slabs = lax.axis_size("slab")
@@ -427,7 +436,7 @@
     packed = pl.pallas_call(
         pack_kernel,
         out_shape=jax.ShapeDtypeStruct((320 + views_here * det_tiles, LANES), BF16),
-        in_specs=[pl.BlockSpec(memory_space=pl.ANY)] * 3,
+        in_specs=[pl.BlockSpec(memory_space=pltpu.HBM)] * 3,
         out_specs=vmem_spec(),
         scratch_shapes=[
             pltpu.VMEM((160, LANES), F32),
@@ -439,9 +448,9 @@
         interpret=INTERPRET,
         name="pack_inputs",
     )(
-        primal.reshape(160, LANES),
-        cotangent.reshape(160, LANES),
-        dual.reshape(views_here * det_tiles, LANES),
+        in_hbm(primal.reshape(160, LANES)),
+        in_hbm(cotangent.reshape(160, LANES)),
+        in_hbm(dual.reshape(views_here * det_tiles, LANES)),
     )
     packed = lax.all_gather(packed, "view", axis=0, tiled=False)
 
@@ -462,8 +471,8 @@
     )(meta, packed, tiles, foots, footprints)
 
     inner = lambda i: i if i == 0 or i == slabs - 1 else ((i - 1) ^ 1) + 1
+    crossed = lax.ppermute(here, "slab", [(i, inner(i)) for i in range(slabs)])
     paired = lax.ppermute(here, "slab", [(i, i ^ 1) for i in range(slabs)])
-    crossed = lax.ppermute(here, "slab", [(i, inner(i)) for i in range(slabs)])
 
     w_in = jnp.concatenate([by_taps(w_first, 0), by_taps(flipped(w_last), 8)], axis=0)
     w_mid = by_rows(w_middle, HID, HID)
@@ -481,7 +490,7 @@
         out_specs=(vmem_spec(),) * 2,
         scratch_shapes=[
             pltpu.VMEM((432, LANES), F32),
-            pltpu.VMEM((27 * SLOT, 2 * HID), F32),
+            pltpu.VMEM((LANES, 4 * LANES), F32),
             pltpu.VMEM((288, 3 * HID), F32),
             pltpu.VMEM((7, 3 * HID, 2 * LANES), F32),
             pltpu.VMEM((7, 3 * HID, 2 * LANES), F32),
@@ -527,9 +536,8 @@
         interpret=INTERPRET,
         name="sum_shares",
     )(shares.reshape(grads.shape))
-    whole = lax.all_to_all(
-        summed.reshape(shares.shape), both, 0, 0, tiled=True
-    ).reshape(grads.shape)
+    whole = lax.all_to_all(summed.reshape(shares.shape), both, 0, 0, tiled=True)
+    whole = whole.reshape(grads.shape)
 
     arrived = jnp.stack([strip] + others)
     order = (view_at - jnp.arange(ranks)) % ranks

time: 84.5 us -> 82.9 us (0.981)
  local copies, waits for them, and re-layouts: 6.35 us -> 3.87 us
  Pallas kernels: 16.2 us -> 17.2 us
    unnamed x20 -> x14, local copies, waits for them, and re-layouts: 4.55 us -> 2.07 us
where the time goes in v5:
time: 82.9 us; the launch traced here: 82.5 us
  starting transfers between devices  30.7 us (37%)
  waiting for transfers between devices  18.8 us (23%)
  Pallas kernels  17.2 us (21%)
  blocking collectives  10.8 us (13%)
  local copies, waits for them, and re-layouts  3.87 us (5%)
  between operations  0.89 us (1%)
    all_to_all x1, starting transfers between devices, shards(): lax.all_to_all(grads.reshape(devices, per, LANES), both, 0, 0, tiled=True)  17.5 us
    all_gather x1, blocking collectives, shards(): packed = lax.all_gather(packed, 'view', axis=0, tiled=False)  10.8 us
    all_to_all x1, waiting for transfers between devices, shards(): whole = lax.all_to_all(summed.reshape(shares.shape), both, 0, 0, tiled=True)  10.8 us
    pallas_call x1, Pallas kernels, shards(): pl.pallas_call(net_kernel, out_shape=(jax.ShapeDtypeStruct((rows1, HID, L...  10.7 us
    all_to_all x1, starting transfers between devices, shards(): whole = lax.all_to_all(summed.reshape(shares.shape), both, 0, 0, tiled=True)  7.24 us
    all_to_all x1, waiting for transfers between devices, shards(): lax.all_to_all(grads.reshape(devices, per, LANES), both, 0, 0, tiled=True)  5.6 us
    ppermute x3, starting transfers between devices, shards(): lax.ppermute(strip, 'view', ring(step))  5 us
    ppermute x1, waiting for transfers between devices, shards(): paired = lax.ppermute(here, 'slab', [(i, i ^ 1) for i in range(slabs)])  2.38 us
  transfers between devices with their start and end apart: 7, of which 3 were waited for; matrix products, arithmetic and copies ran while one was open for 2% of the time, Pallas kernels for 4%

profile of v5, /device:TPU:1, one launch (start us, length us, event | category | flops | bytes accessed | tf_op | source)
XLA Modules:
  0.0 82.5 jit_solution(11891878289504878716)
XLA Ops:
  0.6 1.0 %pack_inputs.1 = bf16[384,128]{1,0:T(8,128)(2,1)S(1)} custom-call(f32[160,128]{1,0:T(8,128)} %bitcast.52, f32[160,128]{1,0:T(8,128)} %bitcast.42, bf16[64,128]{1,0:T(8,128)(2,1)} %bitcast.54), custom_call_target="tpu_custom_call" | custom-call | tf_op jit(solution)/shard_map/pack_inputs/pallas_call | solution.py:436
  1.6 10.8 %all-gather = bf16[1536,128]{1,0:T(8,128)(2,1)S(1)} all-gather(bf16[384,128]{1,0:T(8,128)(2,1)S(1)} %pack_inputs.1), channel_id=2, replica_groups=mesh['slab'=64,'view'=4] {'view'}, dimensions={0}, use_global_device_ids=true | all-gather | bytes 491520 | tf_op jit(solution)/shard_map/all_gather | solution.py:455
  12.5 1.2 %box_rows.1.here = bf16[704,128]{1,0:T(8,128)(2,1)S(1)} custom-call(s32[1]{0:T(128)} %bitcast.1.meta, bf16[4,384,128]{2,1,0:T(8,128)(2,1)S(1)} %bitcast.39, s32[128,128]{1,0:T(8,128)S(1)} %bitcast.43, s32[128,128]{1,0:T(8,128)S(1)} %bitcast.45, bf16[8,128,128]{2,1,0:T(8,128)(2,1)S(1)} %copy-done), custom_call_target="tpu_custom_call" | custom-call | tf_op jit(solution)/shard_map/box_rows/pallas_call | solution.py:457
  13.7 0.4 collective-permute-start
  14.1 0.7 collective-permute-start.1
  14.8 0.2 copy.23
  15.0 0.2 reshape.117.w_mid_flip
  15.2 0.6 copy-done.6
  16.0 0.7 copy-done.5
  17.0 0.2 reshape.116.w_mid
  17.4 2.4 %collective-permute-done.paired = bf16[704,128]{1,0:T(8,128)(2,1)S(1)} collective-permute-done((bf16[704,128]{1,0:T(8,128)(2,1)S(1)}, bf16[704,128]{1,0:T(8,128)(2,1)S(1)}, u32[]{:S(2)}, u32[]{:S(2)}) %collective-permute-start) | collective-permute-done | bytes 180256 | tf_op jit(solution)/shard_map/ppermute | solution.py:475
  19.7 10.7 %net_box.1 = (bf16[60,32,128]{2,1,0:T(8,128)(2,1)S(1)}, bf16[512,128]{1,0:T(8,128)(2,1)}) custom-call(s32[4]{0:T(128)S(1)} %pad_add_fusion.meta, bf16[704,128]{1,0:T(8,128)(2,1)S(1)} %collective-permute-done.paired, bf16[704,128]{1,0:T(8,128)(2,1)S(1)} %box_rows.1.here, bf16[704,128]{1,0:T(8,128)(2,1)S(1)} %collective-permute-done.1.crossed, ...), custom_call_target="tpu_custom_call" | custom-call | tf_op jit(solution)/shard_map/net_box/pallas_call | solution.py:483
  30.4 17.5 %all-to-all-start = ((bf16[256,2,128]{2,1,0:T(2,128)(2,1)}), bf16[256,2,128]{2,1,0:T(2,128)(2,1)S(1)}, u32[]{:S(2)}, u32[]{:S(2)}) async-start(bf16[256,2,128]{2,1,0:T(2,128)(2,1)} %bitcast.27), calls=%async_computation | async-start | bytes 262144 | tf_op jit(solution)/shard_map/all_to_all | solution.py:511
  48.1 0.7 copy-done.1
  48.8 1.3 %last_layer.1 = (f32[5,4,8,128]{3,2,1,0:T(8,128)}, bf16[32,128]{1,0:T(8,128)(2,1)S(1)}) custom-call(bf16[60,32,128]{2,1,0:T(8,128)(2,1)S(1)} %get-tuple-element.12.da_one, f32[5,4,8,128]{3,2,1,0:T(8,128)S(1)} %copy-done.1, bf16[24,288]{1,0:T(8,128)(2,1)S(1)} %reshape.118.w_first_flip), custom_call_target="tpu_custom_call" | custom-call | tf_op jit(solution)/shard_map/last_layer/pallas_call | solution.py:513
  50.1 3.1 %collective-permute-start.2 = (bf16[32,128]{1,0:T(8,128)(2,1)S(1)}, bf16[32,128]{1,0:T(8,128)(2,1)S(1)}, u32[]{:S(2)}, u32[]{:S(2)}) collective-permute-start(bf16[32,128]{1,0:T(8,128)(2,1)S(1)} %get-tuple-element.14), channel_id=1, source_target_pairs={{0,1},{1,2},{2,3},{3,0},{4,5},{5,6},{6,7},{7,4},{8,9},{9,10},{10,1... | collective-permute-start | bytes 24584 | tf_op jit(solution)/shard_map/ppermute | solution.py:528
  53.3 1.9 %collective-permute-start.3 = (bf16[32,128]{1,0:T(8,128)(2,1)S(1)}, bf16[32,128]{1,0:T(8,128)(2,1)S(1)}, u32[]{:S(2)}, u32[]{:S(2)}) collective-permute-start(bf16[32,128]{1,0:T(8,128)(2,1)S(1)} %get-tuple-element.14), channel_id=1, source_target_pairs={{0,2},{1,3},{2,0},{3,1},{4,6},{5,7},{6,4},{7,5},{8,10},{9,11},{10,... | collective-permute-start | bytes 24584 | tf_op jit(solution)/shard_map/ppermute | solution.py:528
  55.1 5.6 %all-to-all-done = bf16[256,2,128]{2,1,0:T(2,128)(2,1)S(1)} async-done(((bf16[256,2,128]{2,1,0:T(2,128)(2,1)}), bf16[256,2,128]{2,1,0:T(2,128)(2,1)S(1)}, u32[]{:S(2)}, u32[]{:S(2)}) %all-to-all-start) | async-done | bytes 131104 | tf_op jit(solution)/shard_map/all_to_all | solution.py:511
  60.7 0.7 sum_shares.1
  61.5 7.2 %all-to-all-start.1 = ((bf16[256,2,128]{2,1,0:T(2,128)(2,1)}), bf16[256,2,128]{2,1,0:T(2,128)(2,1)S(1)}, u32[]{:S(2)}, u32[]{:S(2)}) async-start(bf16[256,2,128]{2,1,0:T(2,128)(2,1)} %bitcast.29), calls=%async_computation.1 | async-start | bytes 262144 | tf_op jit(solution)/shard_map/all_to_all | solution.py:539
  68.8 0.6 gather_fusion
  69.4 1.3 %dual_views.1 = f32[64,128]{1,0:T(8,128)} custom-call(s32[1]{0:T(128)} %bitcast.1.meta, bf16[4,32,128]{2,1,0:T(8,128)(2,1)S(1)} %broadcast_select_fusion.strips, s32[128,128]{1,0:T(8,128)S(1)} %bitcast.44, s32[128,128]{1,0:T(8,128)S(1)} %bitcast.46, bf16[8,128,128]{2,1,0:T(8,128)(2,1)S(1)} %copy-done), custom_call_target="tpu_custom_call" | custom-call | tf_op jit(solution)/shard_map/dual_views/pallas_call | solution.py:545
  70.8 10.8 %all-to-all-done.1 = bf16[256,2,128]{2,1,0:T(2,128)(2,1)S(1)} async-done(((bf16[256,2,128]{2,1,0:T(2,128)(2,1)}), bf16[256,2,128]{2,1,0:T(2,128)(2,1)S(1)}, u32[]{:S(2)}, u32[]{:S(2)}) %all-to-all-start.1) | async-done | bytes 131104 | tf_op jit(solution)/shard_map/all_to_all | solution.py:539
  81.5 1.0 %split_grads.1 = (f32[3,3,3,6,32]{4,3,2,1,0:T(8,128)}, f32[3,3,3,32,32]{4,3,2,1,0:T(8,128)}, f32[3,3,5,3,32]{4,3,2,1,0:T(4,128)}) custom-call(bf16[512,128]{1,0:T(8,128)(2,1)S(1)} %bitcast.41), custom_call_target="tpu_custom_call" | custom-call | tf_op jit(solution)/shard_map/split_grads/pallas_call | solution.py:557
  (35 shorter events, 0.9 us)
Async XLA Ops:
  1.6 10.9 %copy-start = (bf16[8,128,128]{2,1,0:T(8,128)(2,1)S(1)}, bf16[8,128,128]{2,1,0:T(8,128)(2,1)}, u32[]{:S(2)}) copy-start(bf16[8,128,128]{2,1,0:T(8,128)(2,1)} %prints.3) | copy-start | bytes 786436
  1.6 10.8 %copy-start.2 = (s32[64,128,2]{1,2,0:T(2,128)S(1)}, s32[64,128,2]{1,2,0:T(2,128)}, u32[]{:S(2)}) copy-start(s32[64,128,2]{1,2,0:T(2,128)} %param.12) | copy-start | bytes 196612
  1.6 10.8 %copy-start.3 = (s32[64,128,2]{1,2,0:T(2,128)S(1)}, s32[64,128,2]{1,2,0:T(2,128)}, u32[]{:S(2)}) copy-start(s32[64,128,2]{1,2,0:T(2,128)} %param.13) | copy-start | bytes 196612
  12.5 2.3 %copy-start.4 = (bf16[3,3,3,32,32]{4,3,2,1,0:T(8,128)(2,1)S(1)}, bf16[3,3,3,32,32]{4,3,2,1,0:T(8,128)(2,1)}, u32[]{:S(2)}) copy-start(bf16[3,3,3,32,32]{4,3,2,1,0:T(8,128)(2,1)} %param.15) | copy-start | bytes 165892
  13.7 6.0 %collective-permute-start = (bf16[704,128]{1,0:T(8,128)(2,1)S(1)}, bf16[704,128]{1,0:T(8,128)(2,1)S(1)}, u32[]{:S(2)}, u32[]{:S(2)}) collective-permute-start(bf16[704,128]{1,0:T(8,128)(2,1)S(1)} %box_rows.1.here), channel_id=1, source_target_pairs={{0,4},{4,0},{8,12},{12,8},{16,20},{20,16},{24,28},{28,24},{32,36},... | collective-permute-start | bytes 540680 | tf_op jit(solution)/shard_map/ppermute | solution.py:475
  14.1 5.7 %collective-permute-start.1 = (bf16[704,128]{1,0:T(8,128)(2,1)S(1)}, bf16[704,128]{1,0:T(8,128)(2,1)S(1)}, u32[]{:S(2)}, u32[]{:S(2)}) collective-permute-start(bf16[704,128]{1,0:T(8,128)(2,1)S(1)} %box_rows.1.here), channel_id=1, source_target_pairs={{0,0},{4,8},{8,4},{12,16},{16,12},{20,24},{24,20},{28,32},{32,28},... | collective-permute-start | bytes 540680 | tf_op jit(solution)/shard_map/ppermute | solution.py:474
  15.0 0.8 copy-start.6
  15.9 0.8 copy-start.5
  30.4 30.3 %all-to-all-start = ((bf16[256,2,128]{2,1,0:T(2,128)(2,1)}), bf16[256,2,128]{2,1,0:T(2,128)(2,1)S(1)}, u32[]{:S(2)}, u32[]{:S(2)}) async-start(bf16[256,2,128]{2,1,0:T(2,128)(2,1)} %bitcast.27), calls=%async_computation | async-start | bytes 262144 | tf_op jit(solution)/shard_map/all_to_all | solution.py:511
  47.9 0.9 %copy-start.1 = (f32[5,4,8,128]{3,2,1,0:T(8,128)S(1)}, f32[5,4,8,128]{3,2,1,0:T(8,128)}, u32[]{:S(2)}) copy-start(f32[5,4,8,128]{3,2,1,0:T(8,128)} %cot.1) | copy-start | bytes 245764
  50.1 18.6 %collective-permute-start.2 = (bf16[32,128]{1,0:T(8,128)(2,1)S(1)}, bf16[32,128]{1,0:T(8,128)(2,1)S(1)}, u32[]{:S(2)}, u32[]{:S(2)}) collective-permute-start(bf16[32,128]{1,0:T(8,128)(2,1)S(1)} %get-tuple-element.14), channel_id=1, source_target_pairs={{0,1},{1,2},{2,3},{3,0},{4,5},{5,6},{6,7},{7,4},{8,9},{9,10},{10,1... | collective-permute-start | bytes 24584 | tf_op jit(solution)/shard_map/ppermute | solution.py:528
  53.3 15.5 %collective-permute-start.3 = (bf16[32,128]{1,0:T(8,128)(2,1)S(1)}, bf16[32,128]{1,0:T(8,128)(2,1)S(1)}, u32[]{:S(2)}, u32[]{:S(2)}) collective-permute-start(bf16[32,128]{1,0:T(8,128)(2,1)S(1)} %get-tuple-element.14), channel_id=1, source_target_pairs={{0,2},{1,3},{2,0},{3,1},{4,6},{5,7},{6,4},{7,5},{8,10},{9,11},{10,... | collective-permute-start | bytes 24584 | tf_op jit(solution)/shard_map/ppermute | solution.py:528
  55.1 13.6 %collective-permute-start.4 = (bf16[32,128]{1,0:T(8,128)(2,1)S(1)}, bf16[32,128]{1,0:T(8,128)(2,1)S(1)}, u32[]{:S(2)}, u32[]{:S(2)}) collective-permute-start(bf16[32,128]{1,0:T(8,128)(2,1)S(1)} %get-tuple-element.14), channel_id=1, source_target_pairs={{0,3},{1,0},{2,1},{3,2},{4,7},{5,4},{6,5},{7,6},{8,11},{9,8},{10,9... | collective-permute-start | bytes 24584 | tf_op jit(solution)/shard_map/ppermute | solution.py:528
  61.5 20.1 %all-to-all-start.1 = ((bf16[256,2,128]{2,1,0:T(2,128)(2,1)}), bf16[256,2,128]{2,1,0:T(2,128)(2,1)S(1)}, u32[]{:S(2)}, u32[]{:S(2)}) async-start(bf16[256,2,128]{2,1,0:T(2,128)(2,1)} %bitcast.29), calls=%async_computation.1 | async-start | bytes 262144 | tf_op jit(solution)/shard_map/all_to_all | solution.py:539

commit v6 on v5

--- a/solution.py
+++ b/solution.py
@@ -125,12 +125,12 @@
     return taps[step : 2 * step] + left + right
 
 
-def window(ref, width, z, y):
+def window(get, width, z, y):
     sides = []
     for ahead in range(2):
         sides.append(
             jnp.concatenate(
-                [ref[(z + a) * width + y + ahead + b] for a in range(3) for b in range(3)], axis=0
+                [get((z + a) * width + y + ahead + b) for a in range(3) for b in range(3)], axis=0
             )
         )
     return jnp.concatenate(sides, axis=1)
@@ -153,84 +153,137 @@
     return jnp.where(col == (row >> 4) * SENT + channel, 1.0, 0.0).astype(BF16)
 
 
-def pipelined(count, multiply, finish, first_buf, second_buf):
-    multiply(0, first_buf)
-
+def pipelined(slices, multiply, finish, first_buf, second_buf):
     bufs = (first_buf, second_buf)
-    for z in range(1, count):
-        multiply(z, bufs[z % 2])
-        finish(z - 1, bufs[1 - z % 2])
-    finish(count - 1, bufs[1 - count % 2])
+    multiply(slices[0], first_buf)
+    for at in range(1, len(slices)):
+        multiply(slices[at], bufs[at % 2])
+        finish(slices[at - 1], bufs[1 - at % 2])
+    finish(slices[-1], bufs[1 - len(slices) % 2])
+
+
+def place_rows(box, to, rows, sides):
+    both = jnp.dot(rows, sides, preferred_element_type=F32).astype(BF16)
+    to = slice(to, to + WY)
+    box[to, 0:SLOT, :] = both[:, :LANES].reshape(WY, SLOT, LANES)
+    box[to, SLOT : 2 * SLOT, :] = rows.reshape(WY, SLOT, LANES)
+    box[to, 2 * SLOT : 3 * SLOT, :] = both[:, LANES:].reshape(WY, SLOT, LANES)
+
+
+def sigmoid(value):
+    return 0.5 * jnp.tanh(0.5 * value) + 0.5
+
+
+def inside_of(slab_at, view_at, slabs, ranks):
+    def inside(z, y, reach):
+        zz, yy = slab_at * CZ - reach + z, view_at * RY - reach + y
+        return (zz >= 0) & (zz < slabs * CZ) & (yy >= 0) & (yy < ranks * RY)
+
+    return inside
+
+
+def times(weights, get, width, rows):
+    def multiply(z, buf):
+        for y in range(0, rows, 2):
+            buf[y // 2, 0 : weights.shape[0], :] = jnp.dot(
+                weights[...], window(get, width, z, y), preferred_element_type=F32
+            )
+
+    return multiply
+
+
+def first_layer(inside, base, z_one, slope, dz_two):
+    rows3 = RY + 6
+
+    def finish(z, buf):
+        for y in range(rows3):
+            half = slice((y % 2) * LANES, (y % 2 + 1) * LANES)
+            value = buf[y // 2, 0:HID, half]
+            sig = sigmoid(value)
+            at = (z - base) * rows3 + y
+            z_one[at] = jnp.where(inside(z, y, 3), value * sig, 0.0).astype(BF16)
+            slope[at] = sig * (1.0 + value * (1.0 - sig))
+            dz_two[at] = buf[y // 2, HID : 2 * HID, half]
+
+    return finish
+
+
+OWN_SLICES = (4, 5)
+
+
+def own_kernel(meta, here, w_in, box, z_one, slope, dz_two, buf_a, buf_b):
+    inside = inside_of(meta[0], meta[1], meta[2], meta[3])
+    sides = side_matrix()
+    spread = spread_matrix()
+    step = WY * SENT
+    for z in range(0, CZ, 2):
+        pair = [here[at * step : (at + 1) * step] for at in (z, z + 1)]
+        spaced = jnp.dot(
+            spread, jnp.concatenate(pair, axis=1), preferred_element_type=F32
+        ).astype(BF16)
+        for at in range(2):
+            place_rows(box, (z + at) * WY, spaced[:, at * LANES : (at + 1) * LANES], sides)
+    pipelined(
+        OWN_SLICES,
+        times(w_in, lambda i: box[i - CZ * WY], WY, RY + 6),
+        first_layer(inside, OWN_SLICES[0], z_one, slope, dz_two),
+        buf_a,
+        buf_b,
+    )
 
 
 def net_kernel(
-    meta, paired, here, crossed, w_in, w_mid, w_mid_flip,
+    meta, paired, crossed, own_box, own_z_one, own_slope, own_dz_two, w_in, w_mid, w_mid_flip,
     da_one, packed,
     grads, ends_grad, mid_grad, buf_a, buf_b, box, slope, dz_two, z_one, z_two, da_two,
 ):
-    slab_at, view_at, slabs, ranks = meta[0], meta[1], meta[2], meta[3]
+    slab_at, slabs = meta[0], meta[2]
+    inside = inside_of(meta[0], meta[1], meta[2], meta[3])
     sides = side_matrix()
     spread = spread_matrix()
     per = CZ * WY
+    step = WY * SENT
     odd = slab_at % 2 == 1
     has_prev, has_next = slab_at > 0, slab_at < slabs - 1
-    for part in range(3):
+    for part in range(2):
         for z in range(0, CZ, 2):
             pair = []
-            for at in range(z, z + 2):
-                cut = slice(at * WY * SENT, (at + 1) * WY * SENT)
-                if part == 1:
-                    rows = here[cut]
-                else:
-                    near, far = paired[cut], crossed[cut]
-                    rows = jnp.where(odd, near, far) if part == 0 else jnp.where(odd, far, near)
-                    rows = jnp.where(has_next if part else has_prev, rows, jnp.zeros_like(rows))
-                pair.append(rows)
+            for at in (z, z + 1):
+                cut = slice(at * step, (at + 1) * step)
+                near, far = paired[cut], crossed[cut]
+                rows = jnp.where(odd, far, near) if part else jnp.where(odd, near, far)
+                pair.append(jnp.where(has_next if part else has_prev, rows, jnp.zeros_like(rows)))
             spaced = jnp.dot(
                 spread, jnp.concatenate(pair, axis=1), preferred_element_type=F32
             ).astype(BF16)
             for at in range(2):
-                rows = spaced[:, at * LANES : (at + 1) * LANES]
-                both = jnp.dot(rows, sides, preferred_element_type=F32).astype(BF16)
-                to = slice(part * per + (z + at) * WY, part * per + (z + at + 1) * WY)
-                box[to, 0:SLOT, :] = both[:, :LANES].reshape(WY, SLOT, LANES)
-                box[to, SLOT : 2 * SLOT, :] = rows.reshape(WY, SLOT, LANES)
-                box[to, 2 * SLOT : 3 * SLOT, :] = both[:, LANES:].reshape(WY, SLOT, LANES)
+                to = part * per + (z + at) * WY
+                place_rows(box, to, spaced[:, at * LANES : (at + 1) * LANES], sides)
     first, last = lane_masks((HID, LANES))
-    z_start, y_start = slab_at * CZ, view_at * RY
-    z_end, y_end = slabs * CZ, ranks * RY
-
-    def inside(z, y, reach):
-        zz, yy = z_start - reach + z, y_start - reach + y
-        return (zz >= 0) & (zz < z_end) & (yy >= 0) & (yy < y_end)
-
-    def sigmoid(value):
-        return 0.5 * jnp.tanh(0.5 * value) + 0.5
-
     depth3, rows3 = CZ + 6, RY + 6
     depth2, rows2 = CZ + 4, RY + 4
     depth1, rows1 = CZ + 2, RY + 2
 
-    def times(weights, source, width, rows):
-        def multiply(z, buf):
-            for y in range(0, rows, 2):
-                buf[y // 2, 0 : weights.shape[0], :] = jnp.dot(
-                    weights[...], window(source, width, z, y), preferred_element_type=F32
-                )
-
-        return multiply
-
-    def finish_one(z, buf):
-        for y in range(rows3):
-            half = slice((y % 2) * LANES, (y % 2 + 1) * LANES)
-            value = buf[y // 2, 0:HID, half]
-            sig = sigmoid(value)
-            at = z * rows3 + y
-            z_one[at] = jnp.where(inside(z, y, 3), value * sig, 0.0).astype(BF16)
-            slope[at] = sig * (1.0 + value * (1.0 - sig))
-            dz_two[at] = buf[y // 2, HID : 2 * HID, half]
-
-    pipelined(depth3, times(w_in, box, WY, rows3), finish_one, buf_a, buf_b)
+    def box_row(i):
+        if per <= i < 2 * per:
+            return own_box[i - per]
+        return box[i if i < per else i - per]
+
+    def from_own(ref, own):
+        low, high = OWN_SLICES[0] * rows3, (OWN_SLICES[-1] + 1) * rows3
+        return lambda i: own[i - low] if low <= i < high else ref[i]
+
+    z_one_row = from_own(z_one, own_z_one)
+    slope_row = from_own(slope, own_slope)
+    dz_two_row = from_own(dz_two, own_dz_two)
+
+    pipelined(
+        [z for z in range(depth3) if z not in OWN_SLICES],
+        times(w_in, box_row, WY, rows3),
+        first_layer(inside, 0, z_one, slope, dz_two),
+        buf_a,
+        buf_b,
+    )
 
     def finish_two(z, buf):
         for y in range(rows2):
@@ -239,28 +292,33 @@
             sig = sigmoid(value)
             at = z * rows2 + y
             z_two[at] = (value * sig).astype(BF16)
-            grad = dz_two[(z + 1) * rows3 + y + 1] * (sig * (1.0 + value * (1.0 - sig)))
+            grad = dz_two_row((z + 1) * rows3 + y + 1) * (sig * (1.0 + value * (1.0 - sig)))
             da_two[at] = jnp.where(inside(z, y, 2), grad, 0.0).astype(BF16)
 
-    pipelined(depth2, times(w_mid, z_one, rows3, rows2), finish_two, buf_a, buf_b)
+    pipelined(
+        range(depth2), times(w_mid, z_one_row, rows3, rows2), finish_two, buf_a, buf_b
+    )
 
     def finish_back(z, buf):
         for y in range(rows1):
             half = slice((y % 2) * LANES, (y % 2 + 1) * LANES)
             value = shift_sum(buf[y // 2, 0 : 3 * HID, half], first, last)
-            grad = value * slope[(z + 2) * rows3 + y + 2]
+            grad = value * slope_row((z + 2) * rows3 + y + 2)
             da_one[z * rows1 + y] = jnp.where(inside(z, y, 1), grad, 0.0).astype(BF16)
 
-    pipelined(depth1, times(w_mid_flip, da_two, rows2, rows1), finish_back, buf_a, buf_b)
+    da_two_row = lambda i: da_two[i]
+    pipelined(
+        range(depth1), times(w_mid_flip, da_two_row, rows2, rows1), finish_back, buf_a, buf_b
+    )
 
     ends_grad[...] = jnp.zeros(ends_grad.shape, F32)
     mid_grad[...] = jnp.zeros(mid_grad.shape, F32)
     contract = (((1,), (1,)), ((), ()))
 
-    def layer_out(z, carry):
-        inner = z_one[pl.ds((z + 3) * rows3 + 3, RY)]
+    for z in range(CZ):
+        inner = [z_one_row((z + 3) * rows3 + 3 + y) for y in range(RY)]
         both = jnp.dot(
-            inner.reshape(RY * HID, LANES), sides, preferred_element_type=F32
+            jnp.concatenate(inner, axis=0), sides, preferred_element_type=F32
         ).astype(BF16)
         ends = jnp.concatenate(
             [
@@ -285,15 +343,12 @@
             ],
             axis=1,
         )
-        low = jnp.concatenate([window(box, WY, z + 3, y + 3) for y in range(0, RY, 2)], axis=1)
-        mid = jnp.concatenate([window(da_two, rows2, z + 1, y + 1) for y in range(0, RY, 2)], axis=1)
+        low = jnp.concatenate([window(box_row, WY, z + 3, y + 3) for y in range(0, RY, 2)], axis=1)
+        mid = jnp.concatenate([window(da_two_row, rows2, z + 1, y + 1) for y in range(0, RY, 2)], axis=1)
         ends_grad[0 : 2 * HID, 0 : 27 * SLOT] += lax.dot_general(
             ends, low, contract, preferred_element_type=F32
         )
         mid_grad[...] += lax.dot_general(mid, mids, contract, preferred_element_type=F32)
-        return carry
-
-    lax.fori_loop(0, CZ, layer_out, 0)
 
     grads[...] = jnp.zeros(grads.shape, F32)
     grads[0:288, 0 : 3 * HID] = mid_grad[...]
@@ -314,7 +369,7 @@
     first, last = lane_masks((8, LANES))
     for z in range(CZ):
         for y in range(0, RY, 2):
-            taps = jnp.dot(w_first_flip[...], window(da_one, rows1, z, y), preferred_element_type=F32)
+            taps = jnp.dot(w_first_flip[...], window(lambda i: da_one[i], rows1, z, y), preferred_element_type=F32)
             for s in range(2):
                 at = (z * RY + y + s) * 8
                 dx[at : at + 8, :] = shift_sum(taps[:, s * LANES : (s + 1) * LANES], first, last)
@@ -479,14 +534,29 @@
     w_mid_flip = by_rows(flipped(w_middle), HID, HID)
     w_first_flip = by_rows(flipped(w_first), HID, 8)
 
-    rows3, rows2, rows1 = 140, 96, 60
+    rows3, rows2, rows1, rows_own = 140, 96, 60, 28
+    own = pl.pallas_call(
+        own_kernel,
+        out_shape=(
+            jax.ShapeDtypeStruct((CZ * WY, 3 * SLOT, LANES), BF16),
+            jax.ShapeDtypeStruct((rows_own, HID, LANES), BF16),
+            jax.ShapeDtypeStruct((rows_own, HID, LANES), F32),
+            jax.ShapeDtypeStruct((rows_own, HID, LANES), F32),
+        ),
+        in_specs=[smem_spec()] + [vmem_spec()] * 2,
+        out_specs=(vmem_spec(),) * 4,
+        scratch_shapes=[pltpu.VMEM((7, 2 * HID, 2 * LANES), F32)] * 2,
+        compiler_params=PARAMS,
+        interpret=INTERPRET,
+        name="own_slab",
+    )(meta_net, here, w_in)
     da_one, grads = pl.pallas_call(
         net_kernel,
         out_shape=(
             jax.ShapeDtypeStruct((rows1, HID, LANES), BF16),
             jax.ShapeDtypeStruct((2 * devices if devices >= 256 else 32 * devices, LANES), BF16),
         ),
-        in_specs=[smem_spec()] + [vmem_spec()] * 6,
+        in_specs=[smem_spec()] + [vmem_spec()] * 9,
         out_specs=(vmem_spec(),) * 2,
         scratch_shapes=[
             pltpu.VMEM((432, LANES), F32),
@@ -494,7 +564,7 @@
             pltpu.VMEM((288, 3 * HID), F32),
             pltpu.VMEM((7, 3 * HID, 2 * LANES), F32),
             pltpu.VMEM((7, 3 * HID, 2 * LANES), F32),
-            pltpu.VMEM((3 * CZ * WY, 3 * SLOT, LANES), BF16),
+            pltpu.VMEM((2 * CZ * WY, 3 * SLOT, LANES), BF16),
             pltpu.VMEM((rows3, HID, LANES), F32),
             pltpu.VMEM((rows3, HID, LANES), F32),
             pltpu.VMEM((rows3, HID, LANES), BF16),
@@ -504,7 +574,7 @@
         compiler_params=PARAMS,
         interpret=INTERPRET,
         name="net_box",
-    )(meta_net, paired, here, crossed, w_in, w_mid, w_mid_flip)
+    )(meta_net, paired, crossed, *own, w_in, w_mid, w_mid_flip)
 
     both = ("slab", "view")
     per = grads.shape[0] // devices

time: 82.9 us -> 81 us (0.977)
  waiting for transfers between devices: 18.8 us -> 17.8 us
    pallas_call x1, Pallas kernels: 10.7 us -> 8.92 us  [shards(): pl.pallas_call(net_kernel, out_shape=(jax.ShapeDtypeStruct((rows1, HID, L...]
    pallas_call x0 -> x1, Pallas kernels: none -> 1.56 us  [shards(): pl.pallas_call(own_kernel, out_shape=(jax.ShapeDtypeStruct((CZ * WY, 3 *...]
    ppermute x1, waiting for transfers between devices: 2.38 us -> 1.4 us  [shards(): paired = lax.ppermute(here, 'slab', [(i, i ^ 1) for i in range(slabs)])]
  transfers between devices with their start and end apart: 7 -> 7, of which waited for: 3 -> 3; matrix products, arithmetic and copies ran while one was open for 2% -> 2% of each run, Pallas kernels for 4% -> 6%
where the time goes in v6:
time: 81 us; the launch traced here: 80.8 us
  starting transfers between devices  30.8 us (38%)
  waiting for transfers between devices  17.8 us (22%)
  Pallas kernels  17 us (21%)
  blocking collectives  10.8 us (13%)
  local copies, waits for them, and re-layouts  3.29 us (4%)
  between operations  0.89 us (1%)
    all_to_all x1, starting transfers between devices, shards(): lax.all_to_all(grads.reshape(devices, per, LANES), both, 0, 0, tiled=True)  17.5 us
    all_gather x1, blocking collectives, shards(): packed = lax.all_gather(packed, 'view', axis=0, tiled=False)  10.8 us
    all_to_all x1, waiting for transfers between devices, shards(): whole = lax.all_to_all(summed.reshape(shares.shape), both, 0, 0, tiled=True)  10.8 us
    pallas_call x1, Pallas kernels, shards(): pl.pallas_call(net_kernel, out_shape=(jax.ShapeDtypeStruct((rows1, HID, L...  8.92 us
    all_to_all x1, starting transfers between devices, shards(): whole = lax.all_to_all(summed.reshape(shares.shape), both, 0, 0, tiled=True)  7.24 us
    all_to_all x1, waiting for transfers between devices, shards(): lax.all_to_all(grads.reshape(devices, per, LANES), both, 0, 0, tiled=True)  5.6 us
    ppermute x3, starting transfers between devices, shards(): lax.ppermute(strip, 'view', ring(step))  5 us
  transfers between devices with their start and end apart: 7, of which 3 were waited for; matrix products, arithmetic and copies ran while one was open for 2% of the time, Pallas kernels for 6%

profile of v6, /device:TPU:1, one launch (start us, length us, event | category | flops | bytes accessed | tf_op | source)
XLA Modules:
  0.0 80.8 jit_solution(9915837991644492393)
XLA Ops:
  0.6 1.0 %pack_inputs.1 = bf16[384,128]{1,0:T(8,128)(2,1)S(1)} custom-call(f32[160,128]{1,0:T(8,128)} %bitcast.52, f32[160,128]{1,0:T(8,128)} %bitcast.42, bf16[64,128]{1,0:T(8,128)(2,1)} %bitcast.54), custom_call_target="tpu_custom_call" | custom-call | tf_op jit(solution)/shard_map/pack_inputs/pallas_call | solution.py:491
  1.6 10.8 %all-gather = bf16[1536,128]{1,0:T(8,128)(2,1)S(1)} all-gather(bf16[384,128]{1,0:T(8,128)(2,1)S(1)} %pack_inputs.1), channel_id=2, replica_groups=mesh['slab'=64,'view'=4] {'view'}, dimensions={0}, use_global_device_ids=true | all-gather | bytes 491520 | tf_op jit(solution)/shard_map/all_gather | solution.py:510
  12.5 1.2 %box_rows.1.here = bf16[704,128]{1,0:T(8,128)(2,1)S(1)} custom-call(s32[1]{0:T(128)} %bitcast.1.meta, bf16[4,384,128]{2,1,0:T(8,128)(2,1)S(1)} %bitcast.39, s32[128,128]{1,0:T(8,128)S(1)} %bitcast.43, s32[128,128]{1,0:T(8,128)S(1)} %bitcast.45, bf16[8,128,128]{2,1,0:T(8,128)(2,1)S(1)} %copy-done), custom_call_target="tpu_custom_call" | custom-call | tf_op jit(solution)/shard_map/box_rows/pallas_call | solution.py:512
  13.7 0.4 collective-permute-start
  14.1 0.7 collective-permute-start.1
  15.0 0.7 copy-done.5
  15.9 0.2 copy.23
  16.1 0.2 reshape.117.w_mid_flip
  16.4 0.2 reshape.116.w_mid
  16.7 1.6 %own_slab.1 = (bf16[64,48,128]{2,1,0:T(8,128)(2,1)S(1)}, bf16[28,32,128]{2,1,0:T(8,128)(2,1)S(1)}, f32[28,32,128]{2,1,0:T(8,128)S(1)}, f32[28,32,128]{2,1,0:T(8,128)S(1)}) custom-call(s32[4]{0:T(128)S(1)} %pad_add_fusion.meta, bf16[704,128]{1,0:T(8,128)(2,1)S(1)} %box_rows.1.here, bf16[64,432]{1,0:T(8,128)(2,1)S(1)} %pad_maximum_fusion.w_in), custom_call_target="tpu_custom_call" | custom-call | tf_op jit(solution)/shard_map/own_slab/pallas_call | solution.py:538
  18.3 1.4 %collective-permute-done.paired = bf16[704,128]{1,0:T(8,128)(2,1)S(1)} collective-permute-done((bf16[704,128]{1,0:T(8,128)(2,1)S(1)}, bf16[704,128]{1,0:T(8,128)(2,1)S(1)}, u32[]{:S(2)}, u32[]{:S(2)}) %collective-permute-start) | collective-permute-done | bytes 180256 | tf_op jit(solution)/shard_map/ppermute | solution.py:530
  19.7 8.9 %net_box.1 = (bf16[60,32,128]{2,1,0:T(8,128)(2,1)S(1)}, bf16[512,128]{1,0:T(8,128)(2,1)}) custom-call(s32[4]{0:T(128)S(1)} %pad_add_fusion.meta, bf16[704,128]{1,0:T(8,128)(2,1)S(1)} %collective-permute-done.paired, bf16[704,128]{1,0:T(8,128)(2,1)S(1)} %collective-permute-done.1.crossed, bf16[64,48,128]{2,1,0:T(8,128)(2,1)S(1)} %get-tuple-element.16.own_box, ...), custom_call_target="tpu_custom_call" | custom-call | tf_op jit(solution)/shard_map/net_box/pallas_call | solution.py:553
  28.7 17.5 %all-to-all-start = ((bf16[256,2,128]{2,1,0:T(2,128)(2,1)}), bf16[256,2,128]{2,1,0:T(2,128)(2,1)S(1)}, u32[]{:S(2)}, u32[]{:S(2)}) async-start(bf16[256,2,128]{2,1,0:T(2,128)(2,1)} %bitcast.27), calls=%async_computation | async-start | bytes 262144 | tf_op jit(solution)/shard_map/all_to_all | solution.py:581
  46.3 0.7 copy-done.1
  47.1 1.3 %last_layer.1 = (f32[5,4,8,128]{3,2,1,0:T(8,128)}, bf16[32,128]{1,0:T(8,128)(2,1)S(1)}) custom-call(bf16[60,32,128]{2,1,0:T(8,128)(2,1)S(1)} %get-tuple-element.20.da_one, f32[5,4,8,128]{3,2,1,0:T(8,128)S(1)} %copy-done.1, bf16[24,288]{1,0:T(8,128)(2,1)S(1)} %reshape.118.w_first_flip), custom_call_target="tpu_custom_call" | custom-call | tf_op jit(solution)/shard_map/last_layer/pallas_call | solution.py:583
  48.3 3.1 %collective-permute-start.2 = (bf16[32,128]{1,0:T(8,128)(2,1)S(1)}, bf16[32,128]{1,0:T(8,128)(2,1)S(1)}, u32[]{:S(2)}, u32[]{:S(2)}) collective-permute-start(bf16[32,128]{1,0:T(8,128)(2,1)S(1)} %get-tuple-element.22), channel_id=1, source_target_pairs={{0,1},{1,2},{2,3},{3,0},{4,5},{5,6},{6,7},{7,4},{8,9},{9,10},{10,1... | collective-permute-start | bytes 24584 | tf_op jit(solution)/shard_map/ppermute | solution.py:598
  51.5 1.9 %collective-permute-start.3 = (bf16[32,128]{1,0:T(8,128)(2,1)S(1)}, bf16[32,128]{1,0:T(8,128)(2,1)S(1)}, u32[]{:S(2)}, u32[]{:S(2)}) collective-permute-start(bf16[32,128]{1,0:T(8,128)(2,1)S(1)} %get-tuple-element.22), channel_id=1, source_target_pairs={{0,2},{1,3},{2,0},{3,1},{4,6},{5,7},{6,4},{7,5},{8,10},{9,11},{10,... | collective-permute-start | bytes 24584 | tf_op jit(solution)/shard_map/ppermute | solution.py:598
  53.4 5.6 %all-to-all-done = bf16[256,2,128]{2,1,0:T(2,128)(2,1)S(1)} async-done(((bf16[256,2,128]{2,1,0:T(2,128)(2,1)}), bf16[256,2,128]{2,1,0:T(2,128)(2,1)S(1)}, u32[]{:S(2)}, u32[]{:S(2)}) %all-to-all-start) | async-done | bytes 131104 | tf_op jit(solution)/shard_map/all_to_all | solution.py:581
  59.0 0.7 sum_shares.1
  59.7 7.2 %all-to-all-start.1 = ((bf16[256,2,128]{2,1,0:T(2,128)(2,1)}), bf16[256,2,128]{2,1,0:T(2,128)(2,1)S(1)}, u32[]{:S(2)}, u32[]{:S(2)}) async-start(bf16[256,2,128]{2,1,0:T(2,128)(2,1)} %bitcast.29), calls=%async_computation.1 | async-start | bytes 262144 | tf_op jit(solution)/shard_map/all_to_all | solution.py:609
  67.0 0.6 gather_fusion
  67.6 1.3 %dual_views.1 = f32[64,128]{1,0:T(8,128)} custom-call(s32[1]{0:T(128)} %bitcast.1.meta, bf16[4,32,128]{2,1,0:T(8,128)(2,1)S(1)} %broadcast_select_fusion.strips, s32[128,128]{1,0:T(8,128)S(1)} %bitcast.44, s32[128,128]{1,0:T(8,128)S(1)} %bitcast.46, bf16[8,128,128]{2,1,0:T(8,128)(2,1)S(1)} %copy-done), custom_call_target="tpu_custom_call" | custom-call | tf_op jit(solution)/shard_map/dual_views/pallas_call | solution.py:615
  69.0 10.8 %all-to-all-done.1 = bf16[256,2,128]{2,1,0:T(2,128)(2,1)S(1)} async-done(((bf16[256,2,128]{2,1,0:T(2,128)(2,1)}), bf16[256,2,128]{2,1,0:T(2,128)(2,1)S(1)}, u32[]{:S(2)}, u32[]{:S(2)}) %all-to-all-start.1) | async-done | bytes 131104 | tf_op jit(solution)/shard_map/all_to_all | solution.py:609
  79.8 1.0 %split_grads.1 = (f32[3,3,3,6,32]{4,3,2,1,0:T(8,128)}, f32[3,3,3,32,32]{4,3,2,1,0:T(8,128)}, f32[3,3,5,3,32]{4,3,2,1,0:T(4,128)}) custom-call(bf16[512,128]{1,0:T(8,128)(2,1)S(1)} %bitcast.41), custom_call_target="tpu_custom_call" | custom-call | tf_op jit(solution)/shard_map/split_grads/pallas_call | solution.py:627
  (36 shorter events, 1.0 us)
Async XLA Ops:
  1.6 10.9 %copy-start = (bf16[8,128,128]{2,1,0:T(8,128)(2,1)S(1)}, bf16[8,128,128]{2,1,0:T(8,128)(2,1)}, u32[]{:S(2)}) copy-start(bf16[8,128,128]{2,1,0:T(8,128)(2,1)} %prints.3) | copy-start | bytes 786436
  1.6 10.8 %copy-start.2 = (s32[64,128,2]{1,2,0:T(2,128)S(1)}, s32[64,128,2]{1,2,0:T(2,128)}, u32[]{:S(2)}) copy-start(s32[64,128,2]{1,2,0:T(2,128)} %param.12) | copy-start | bytes 196612
  1.6 10.8 %copy-start.3 = (s32[64,128,2]{1,2,0:T(2,128)S(1)}, s32[64,128,2]{1,2,0:T(2,128)}, u32[]{:S(2)}) copy-start(s32[64,128,2]{1,2,0:T(2,128)} %param.13) | copy-start | bytes 196612
  12.5 2.3 %copy-start.6 = (bf16[3,3,3,5,32]{4,2,3,1,0:T(4,128)(2,1)S(1)}, bf16[3,3,3,5,32]{4,2,3,1,0:T(4,128)(2,1)}, u32[]{:S(2)}) copy-start(bf16[3,3,3,5,32]{4,2,3,1,0:T(4,128)(2,1)} %param.16) | copy-start | bytes 25924
  13.7 6.0 %collective-permute-start = (bf16[704,128]{1,0:T(8,128)(2,1)S(1)}, bf16[704,128]{1,0:T(8,128)(2,1)S(1)}, u32[]{:S(2)}, u32[]{:S(2)}) collective-permute-start(bf16[704,128]{1,0:T(8,128)(2,1)S(1)} %box_rows.1.here), channel_id=1, source_target_pairs={{0,4},{4,0},{8,12},{12,8},{16,20},{20,16},{24,28},{28,24},{32,36},... | collective-permute-start | bytes 540680 | tf_op jit(solution)/shard_map/ppermute | solution.py:530
  14.1 5.7 %collective-permute-start.1 = (bf16[704,128]{1,0:T(8,128)(2,1)S(1)}, bf16[704,128]{1,0:T(8,128)(2,1)S(1)}, u32[]{:S(2)}, u32[]{:S(2)}) collective-permute-start(bf16[704,128]{1,0:T(8,128)(2,1)S(1)} %box_rows.1.here), channel_id=1, source_target_pairs={{0,0},{4,8},{8,4},{12,16},{16,12},{20,24},{24,20},{28,32},{32,28},... | collective-permute-start | bytes 540680 | tf_op jit(solution)/shard_map/ppermute | solution.py:529
  14.9 0.8 %copy-start.5 = (bf16[3,3,3,32,6]{3,4,2,1,0:T(8,128)(2,1)S(1)}, bf16[3,3,3,32,6]{3,4,2,1,0:T(8,128)(2,1)}, u32[]{:S(2)}) copy-start(bf16[3,3,3,32,6]{3,4,2,1,0:T(8,128)(2,1)} %param.14) | copy-start | bytes 31108
  14.9 0.9 %copy-start.4 = (bf16[3,3,3,32,32]{4,3,2,1,0:T(8,128)(2,1)S(1)}, bf16[3,3,3,32,32]{4,3,2,1,0:T(8,128)(2,1)}, u32[]{:S(2)}) copy-start(bf16[3,3,3,32,32]{4,3,2,1,0:T(8,128)(2,1)} %param.15) | copy-start | bytes 165892
  28.7 30.3 %all-to-all-start = ((bf16[256,2,128]{2,1,0:T(2,128)(2,1)}), bf16[256,2,128]{2,1,0:T(2,128)(2,1)S(1)}, u32[]{:S(2)}, u32[]{:S(2)}) async-start(bf16[256,2,128]{2,1,0:T(2,128)(2,1)} %bitcast.27), calls=%async_computation | async-start | bytes 262144 | tf_op jit(solution)/shard_map/all_to_all | solution.py:581
  46.2 0.9 %copy-start.1 = (f32[5,4,8,128]{3,2,1,0:T(8,128)S(1)}, f32[5,4,8,128]{3,2,1,0:T(8,128)}, u32[]{:S(2)}) copy-start(f32[5,4,8,128]{3,2,1,0:T(8,128)} %cot.1) | copy-start | bytes 245764
  48.3 18.6 %collective-permute-start.2 = (bf16[32,128]{1,0:T(8,128)(2,1)S(1)}, bf16[32,128]{1,0:T(8,128)(2,1)S(1)}, u32[]{:S(2)}, u32[]{:S(2)}) collective-permute-start(bf16[32,128]{1,0:T(8,128)(2,1)S(1)} %get-tuple-element.22), channel_id=1, source_target_pairs={{0,1},{1,2},{2,3},{3,0},{4,5},{5,6},{6,7},{7,4},{8,9},{9,10},{10,1... | collective-permute-start | bytes 24584 | tf_op jit(solution)/shard_map/ppermute | solution.py:598
  51.5 15.5 %collective-permute-start.3 = (bf16[32,128]{1,0:T(8,128)(2,1)S(1)}, bf16[32,128]{1,0:T(8,128)(2,1)S(1)}, u32[]{:S(2)}, u32[]{:S(2)}) collective-permute-start(bf16[32,128]{1,0:T(8,128)(2,1)S(1)} %get-tuple-element.22), channel_id=1, source_target_pairs={{0,2},{1,3},{2,0},{3,1},{4,6},{5,7},{6,4},{7,5},{8,10},{9,11},{10,... | collective-permute-start | bytes 24584 | tf_op jit(solution)/shard_map/ppermute | solution.py:598
  53.4 13.6 %collective-permute-start.4 = (bf16[32,128]{1,0:T(8,128)(2,1)S(1)}, bf16[32,128]{1,0:T(8,128)(2,1)S(1)}, u32[]{:S(2)}, u32[]{:S(2)}) collective-permute-start(bf16[32,128]{1,0:T(8,128)(2,1)S(1)} %get-tuple-element.22), channel_id=1, source_target_pairs={{0,3},{1,0},{2,1},{3,2},{4,7},{5,4},{6,5},{7,6},{8,11},{9,8},{10,9... | collective-permute-start | bytes 24584 | tf_op jit(solution)/shard_map/ppermute | solution.py:598
  59.7 20.1 %all-to-all-start.1 = ((bf16[256,2,128]{2,1,0:T(2,128)(2,1)}), bf16[256,2,128]{2,1,0:T(2,128)(2,1)S(1)}, u32[]{:S(2)}, u32[]{:S(2)}) async-start(bf16[256,2,128]{2,1,0:T(2,128)(2,1)} %bitcast.29), calls=%async_computation.1 | async-start | bytes 262144 | tf_op jit(solution)/shard_map/all_to_all | solution.py:609

commit v7 on v6

--- a/solution.py
+++ b/solution.py
@@ -21,7 +21,9 @@
 HID = 32
 SLOT = 16
 DTL = 4
-SENT = 11
+XS, GS = 6, 5
+XR, GR = WY * XS, WY * GS
+SENT = XR + GR
 
 
 def smem_spec():
@@ -51,8 +53,10 @@
     out[320:, :] = dual_in[...]
 
 
-def gather_kernel(meta, packed, tiles, foots, prints, out, codes, duals, field, rows):
-    view_at = meta[0]
+def gather_kernel(
+    meta, packed, tiles, foots, prints, out, to_pair, to_cross, codes, duals, field, rows_x, rows_g
+):
+    odd, view_at = meta[0] % 2, meta[1]
     foot_count = prints.shape[0]
     views = tiles.shape[0] // 2
     codes[...] = (tiles[...] * foot_count + foots[...]).astype(F32)
@@ -81,8 +85,11 @@
         part = jnp.dot(counts, dual_rows, preferred_element_type=F32)
         high = part.astype(BF16)
         low = (part - high.astype(F32)).astype(BF16)
-        back = back + jnp.dot(high, prints[o], preferred_element_type=F32)
-        back = back + jnp.dot(low, prints[o], preferred_element_type=F32)
+        back = back + jnp.dot(
+            jnp.concatenate([high, low], axis=1),
+            jnp.concatenate([prints[o], prints[o]], axis=0),
+            preferred_element_type=F32,
+        )
     field[...] = back
 
     before = jnp.maximum(view_at - 1, 0)
@@ -92,10 +99,11 @@
     full_y = RY * ranks
 
     def place(z, slot, mid, low_side, high_side):
-        base = z * WY * SENT + slot
-        rows[pl.ds(base, REACH, stride=SENT), :] = jnp.where(has_before, low_side[RY - REACH :], 0.0)
-        rows[pl.ds(base + REACH * SENT, RY, stride=SENT), :] = mid
-        rows[pl.ds(base + (REACH + RY) * SENT, REACH, stride=SENT), :] = jnp.where(
+        rows, count = (rows_x, XS) if slot < XS else (rows_g, GS)
+        base = z * WY * count + slot % XS
+        rows[pl.ds(base, REACH, stride=count), :] = jnp.where(has_before, low_side[RY - REACH :], 0.0)
+        rows[pl.ds(base + REACH * count, RY, stride=count), :] = mid
+        rows[pl.ds(base + (REACH + RY) * count, REACH, stride=count), :] = jnp.where(
             has_after, high_side[:REACH], 0.0
         )
 
@@ -110,7 +118,14 @@
     for z in range(CZ):
         at = lambda rank: field[pl.ds(pl.multiple_of(z * full_y + rank * RY, RY), RY), :]
         place(z, 5, at(view_at), at(before), at(after))
-    out[...] = rows[...].astype(BF16)
+    for z in range(CZ):
+        out[z * SENT : z * SENT + XR, :] = rows_x[z * XR : (z + 1) * XR, :].astype(BF16)
+        out[z * SENT + XR : (z + 1) * SENT, :] = rows_g[z * GR : (z + 1) * GR, :].astype(BF16)
+    for message, start in ((to_pair, 1 - odd), (to_cross, odd)):
+        message[0 : CZ * XR, :] = rows_x[...].astype(BF16)
+        message[CZ * XR :, :] = rows_g[
+            pl.ds(pl.multiple_of(start * GR, GR), (CZ - 1) * GR), :
+        ].astype(BF16)
 
 
 def lane_masks(shape):
@@ -145,12 +160,14 @@
 
 
 def spread_matrix():
-    shape = (WY * SLOT, WY * SENT)
+    shape = (WY * SLOT, SENT)
     row = lax.broadcasted_iota(jnp.int32, shape, 0)
     col = lax.broadcasted_iota(jnp.int32, shape, 1)
-    slot = row & (SLOT - 1)
-    channel = jnp.where(slot < 6, slot, jnp.where((slot >= 8) & (slot < 13), slot - 2, -WY * SENT))
-    return jnp.where(col == (row >> 4) * SENT + channel, 1.0, 0.0).astype(BF16)
+    slot, y = row & (SLOT - 1), row >> 4
+    source = jnp.where(
+        slot < XS, y * XS + slot, jnp.where((slot >= 8) & (slot < 13), XR + y * GS + slot - 8, -1)
+    )
+    return jnp.where(col == source, 1.0, 0.0).astype(BF16)
 
 
 def pipelined(slices, multiply, finish, first_buf, second_buf):
@@ -215,9 +232,8 @@
     inside = inside_of(meta[0], meta[1], meta[2], meta[3])
     sides = side_matrix()
     spread = spread_matrix()
-    step = WY * SENT
     for z in range(0, CZ, 2):
-        pair = [here[at * step : (at + 1) * step] for at in (z, z + 1)]
+        pair = [here[at * SENT : (at + 1) * SENT] for at in (z, z + 1)]
         spaced = jnp.dot(
             spread, jnp.concatenate(pair, axis=1), preferred_element_type=F32
         ).astype(BF16)
@@ -242,17 +258,26 @@
     sides = side_matrix()
     spread = spread_matrix()
     per = CZ * WY
-    step = WY * SENT
     odd = slab_at % 2 == 1
     has_prev, has_next = slab_at > 0, slab_at < slabs - 1
     for part in range(2):
         for z in range(0, CZ, 2):
             pair = []
             for at in (z, z + 1):
-                cut = slice(at * step, (at + 1) * step)
-                near, far = paired[cut], crossed[cut]
-                rows = jnp.where(odd, far, near) if part else jnp.where(odd, near, far)
-                pair.append(jnp.where(has_next if part else has_prev, rows, jnp.zeros_like(rows)))
+                first_g = 0 if part else 1
+                cuts = [slice(at * XR, (at + 1) * XR)]
+                if 0 <= at - first_g < CZ - 1:
+                    g_at = CZ * XR + (at - first_g) * GR
+                    cuts.append(slice(g_at, g_at + GR))
+                pieces = []
+                for cut in cuts:
+                    near, far = paired[cut], crossed[cut]
+                    rows = jnp.where(odd, far, near) if part else jnp.where(odd, near, far)
+                    has = has_next if part else has_prev
+                    pieces.append(jnp.where(has, rows, jnp.zeros_like(rows)))
+                if len(cuts) == 1:
+                    pieces.append(jnp.zeros((GR, LANES), BF16))
+                pair.append(jnp.concatenate(pieces, axis=0))
             spaced = jnp.dot(
                 spread, jnp.concatenate(pair, axis=1), preferred_element_type=F32
             ).astype(BF16)
@@ -509,25 +534,31 @@
     )
     packed = lax.all_gather(packed, "view", axis=0, tiled=False)
 
-    here = pl.pallas_call(
+    sent = (CZ * XR + (CZ - 1) * GR, LANES)
+    here, to_pair, to_cross = pl.pallas_call(
         gather_kernel,
-        out_shape=jax.ShapeDtypeStruct((CZ * WY * SENT, LANES), BF16),
+        out_shape=(
+            jax.ShapeDtypeStruct((CZ * SENT, LANES), BF16),
+            jax.ShapeDtypeStruct(sent, BF16),
+            jax.ShapeDtypeStruct(sent, BF16),
+        ),
         in_specs=[smem_spec()] + [vmem_spec()] * 4,
-        out_specs=vmem_spec(),
+        out_specs=(vmem_spec(),) * 3,
         scratch_shapes=[
             pltpu.VMEM((all_views * taps, tiles_here), F32),
             pltpu.VMEM((all_views * det_tiles, LANES), F32),
             pltpu.VMEM((tiles_here, LANES), F32),
-            pltpu.VMEM((CZ * WY * SENT, LANES), F32),
+            pltpu.VMEM((CZ * XR, LANES), F32),
+            pltpu.VMEM((CZ * GR, LANES), F32),
         ],
         compiler_params=PARAMS,
         interpret=INTERPRET,
         name="box_rows",
-    )(meta, packed, tiles, foots, footprints)
+    )(meta_net, packed, tiles, foots, footprints)
 
     inner = lambda i: i if i == 0 or i == slabs - 1 else ((i - 1) ^ 1) + 1
-    crossed = lax.ppermute(here, "slab", [(i, inner(i)) for i in range(slabs)])
-    paired = lax.ppermute(here, "slab", [(i, i ^ 1) for i in range(slabs)])
+    crossed = lax.ppermute(to_cross, "slab", [(i, inner(i)) for i in range(slabs)])
+    paired = lax.ppermute(to_pair, "slab", [(i, i ^ 1) for i in range(slabs)])
 
     w_in = jnp.concatenate([by_taps(w_first, 0), by_taps(flipped(w_last), 8)], axis=0)
     w_mid = by_rows(w_middle, HID, HID)

time: 81 us -> 81.4 us (level)
  no operation moved by 1% of the time
where the time goes in v7:
time: 81.4 us; the launch traced here: 81.1 us
  starting transfers between devices  30.8 us (38%)
  Pallas kernels  17.8 us (22%)
  waiting for transfers between devices  17.4 us (21%)
  blocking collectives  10.8 us (13%)
  local copies, waits for them, and re-layouts  3.29 us (4%)
  between operations  0.89 us (1%)
    all_to_all x1, starting transfers between devices, shards(): lax.all_to_all(grads.reshape(devices, per, LANES), both, 0, 0, tiled=True)  17.5 us
    all_gather x1, blocking collectives, shards(): packed = lax.all_gather(packed, 'view', axis=0, tiled=False)  10.8 us
    all_to_all x1, waiting for transfers between devices, shards(): whole = lax.all_to_all(summed.reshape(shares.shape), both, 0, 0, tiled=True)  10.8 us
    pallas_call x1, Pallas kernels, shards(): pl.pallas_call(net_kernel, out_shape=(jax.ShapeDtypeStruct((rows1, HID, L...  8.92 us
    all_to_all x1, starting transfers between devices, shards(): whole = lax.all_to_all(summed.reshape(shares.shape), both, 0, 0, tiled=True)  7.24 us
    all_to_all x1, waiting for transfers between devices, shards(): lax.all_to_all(grads.reshape(devices, per, LANES), both, 0, 0, tiled=True)  5.6 us
    ppermute x3, starting transfers between devices, shards(): lax.ppermute(strip, 'view', ring(step))  5 us
    pallas_call x1, Pallas kernels, shards(): pl.pallas_call(gather_kernel, out_shape=(jax.ShapeDtypeStruct((CZ * SENT,...  1.95 us
  transfers between devices with their start and end apart: 7, of which 3 were waited for; matrix products, arithmetic and copies ran while one was open for 2% of the time, Pallas kernels for 6%

profile of v7, /device:TPU:1, one launch (start us, length us, event | category | flops | bytes accessed | tf_op | source)
XLA Modules:
  0.0 81.1 jit_solution(1927458932630324408)
XLA Ops:
  0.6 1.0 %pack_inputs.1 = bf16[384,128]{1,0:T(8,128)(2,1)S(1)} custom-call(f32[160,128]{1,0:T(8,128)} %bitcast.52, f32[160,128]{1,0:T(8,128)} %bitcast.42, bf16[64,128]{1,0:T(8,128)(2,1)} %bitcast.54), custom_call_target="tpu_custom_call" | custom-call | tf_op jit(solution)/shard_map/pack_inputs/pallas_call | solution.py:516
  1.6 10.8 %all-gather = bf16[1536,128]{1,0:T(8,128)(2,1)S(1)} all-gather(bf16[384,128]{1,0:T(8,128)(2,1)S(1)} %pack_inputs.1), channel_id=2, replica_groups=mesh['slab'=64,'view'=4] {'view'}, dimensions={0}, use_global_device_ids=true | all-gather | bytes 491520 | tf_op jit(solution)/shard_map/all_gather | solution.py:535
  12.6 2.0 %box_rows.1 = (bf16[704,128]{1,0:T(8,128)(2,1)S(1)}, bf16[624,128]{1,0:T(8,128)(2,1)S(1)}, bf16[624,128]{1,0:T(8,128)(2,1)S(1)}) custom-call(s32[4]{0:T(128)S(1)} %pad_add_fusion.meta, bf16[4,384,128]{2,1,0:T(8,128)(2,1)S(1)} %bitcast.39, s32[128,128]{1,0:T(8,128)S(1)} %bitcast.43, s32[128,128]{1,0:T(8,128)S(1)} %bitcast.45, bf16[8,128,128]{2,1,0:T(8,128)(2,1)S(1)} %copy-done), custom_call_target="tpu_custom_call" | custom-call | tf_op jit(solution)/shard_map/box_rows/pallas_call | solution.py:538
  14.5 0.4 collective-permute-start
  14.9 0.7 collective-permute-start.1
  15.8 0.7 copy-done.5
  16.7 0.2 copy.23
  16.9 0.2 reshape.117.w_mid_flip
  17.3 0.2 reshape.116.w_mid
  17.5 1.6 %own_slab.1 = (bf16[64,48,128]{2,1,0:T(8,128)(2,1)S(1)}, bf16[28,32,128]{2,1,0:T(8,128)(2,1)S(1)}, f32[28,32,128]{2,1,0:T(8,128)S(1)}, f32[28,32,128]{2,1,0:T(8,128)S(1)}) custom-call(s32[4]{0:T(128)S(1)} %pad_add_fusion.meta, bf16[704,128]{1,0:T(8,128)(2,1)S(1)} %get-tuple-element.21.here, bf16[64,432]{1,0:T(8,128)(2,1)S(1)} %pad_maximum_fusion.w_in), custom_call_target="tpu_custom_call" | custom-call | tf_op jit(solution)/shard_map/own_slab/pallas_call | solution.py:569
  19.1 1.0 %collective-permute-done.paired = bf16[624,128]{1,0:T(8,128)(2,1)S(1)} collective-permute-done((bf16[624,128]{1,0:T(8,128)(2,1)S(1)}, bf16[624,128]{1,0:T(8,128)(2,1)S(1)}, u32[]{:S(2)}, u32[]{:S(2)}) %collective-permute-start) | collective-permute-done | bytes 159776 | tf_op jit(solution)/shard_map/ppermute | solution.py:561
  20.1 8.9 %net_box.1 = (bf16[60,32,128]{2,1,0:T(8,128)(2,1)S(1)}, bf16[512,128]{1,0:T(8,128)(2,1)}) custom-call(s32[4]{0:T(128)S(1)} %pad_add_fusion.meta, bf16[624,128]{1,0:T(8,128)(2,1)S(1)} %collective-permute-done.paired, bf16[624,128]{1,0:T(8,128)(2,1)S(1)} %collective-permute-done.1.crossed, bf16[64,48,128]{2,1,0:T(8,128)(2,1)S(1)} %get-tuple-element.22.own_box, ...), custom_call_target="tpu_custom_call" | custom-call | tf_op jit(solution)/shard_map/net_box/pallas_call | solution.py:584
  29.0 17.5 %all-to-all-start = ((bf16[256,2,128]{2,1,0:T(2,128)(2,1)}), bf16[256,2,128]{2,1,0:T(2,128)(2,1)S(1)}, u32[]{:S(2)}, u32[]{:S(2)}) async-start(bf16[256,2,128]{2,1,0:T(2,128)(2,1)} %bitcast.27), calls=%async_computation | async-start | bytes 262144 | tf_op jit(solution)/shard_map/all_to_all | solution.py:612
  46.7 0.7 copy-done.1
  47.4 1.3 %last_layer.1 = (f32[5,4,8,128]{3,2,1,0:T(8,128)}, bf16[32,128]{1,0:T(8,128)(2,1)S(1)}) custom-call(bf16[60,32,128]{2,1,0:T(8,128)(2,1)S(1)} %get-tuple-element.26.da_one, f32[5,4,8,128]{3,2,1,0:T(8,128)S(1)} %copy-done.1, bf16[24,288]{1,0:T(8,128)(2,1)S(1)} %reshape.118.w_first_flip), custom_call_target="tpu_custom_call" | custom-call | tf_op jit(solution)/shard_map/last_layer/pallas_call | solution.py:614
  48.7 3.1 %collective-permute-start.2 = (bf16[32,128]{1,0:T(8,128)(2,1)S(1)}, bf16[32,128]{1,0:T(8,128)(2,1)S(1)}, u32[]{:S(2)}, u32[]{:S(2)}) collective-permute-start(bf16[32,128]{1,0:T(8,128)(2,1)S(1)} %get-tuple-element.28), channel_id=1, source_target_pairs={{0,1},{1,2},{2,3},{3,0},{4,5},{5,6},{6,7},{7,4},{8,9},{9,10},{10,1... | collective-permute-start | bytes 24584 | tf_op jit(solution)/shard_map/ppermute | solution.py:629
  51.9 1.9 %collective-permute-start.3 = (bf16[32,128]{1,0:T(8,128)(2,1)S(1)}, bf16[32,128]{1,0:T(8,128)(2,1)S(1)}, u32[]{:S(2)}, u32[]{:S(2)}) collective-permute-start(bf16[32,128]{1,0:T(8,128)(2,1)S(1)} %get-tuple-element.28), channel_id=1, source_target_pairs={{0,2},{1,3},{2,0},{3,1},{4,6},{5,7},{6,4},{7,5},{8,10},{9,11},{10,... | collective-permute-start | bytes 24584 | tf_op jit(solution)/shard_map/ppermute | solution.py:629
  53.7 5.6 %all-to-all-done = bf16[256,2,128]{2,1,0:T(2,128)(2,1)S(1)} async-done(((bf16[256,2,128]{2,1,0:T(2,128)(2,1)}), bf16[256,2,128]{2,1,0:T(2,128)(2,1)S(1)}, u32[]{:S(2)}, u32[]{:S(2)}) %all-to-all-start) | async-done | bytes 131104 | tf_op jit(solution)/shard_map/all_to_all | solution.py:612
  59.3 0.7 sum_shares.1
  60.1 7.2 %all-to-all-start.1 = ((bf16[256,2,128]{2,1,0:T(2,128)(2,1)}), bf16[256,2,128]{2,1,0:T(2,128)(2,1)S(1)}, u32[]{:S(2)}, u32[]{:S(2)}) async-start(bf16[256,2,128]{2,1,0:T(2,128)(2,1)} %bitcast.29), calls=%async_computation.1 | async-start | bytes 262144 | tf_op jit(solution)/shard_map/all_to_all | solution.py:640
  67.4 0.6 gather_fusion
  68.0 1.3 %dual_views.1 = f32[64,128]{1,0:T(8,128)} custom-call(s32[1]{0:T(128)} %bitcast.1.meta, bf16[4,32,128]{2,1,0:T(8,128)(2,1)S(1)} %broadcast_select_fusion.strips, s32[128,128]{1,0:T(8,128)S(1)} %bitcast.44, s32[128,128]{1,0:T(8,128)S(1)} %bitcast.46, bf16[8,128,128]{2,1,0:T(8,128)(2,1)S(1)} %copy-done), custom_call_target="tpu_custom_call" | custom-call | tf_op jit(solution)/shard_map/dual_views/pallas_call | solution.py:646
  69.4 10.8 %all-to-all-done.1 = bf16[256,2,128]{2,1,0:T(2,128)(2,1)S(1)} async-done(((bf16[256,2,128]{2,1,0:T(2,128)(2,1)}), bf16[256,2,128]{2,1,0:T(2,128)(2,1)S(1)}, u32[]{:S(2)}, u32[]{:S(2)}) %all-to-all-start.1) | async-done | bytes 131104 | tf_op jit(solution)/shard_map/all_to_all | solution.py:640
  80.1 1.0 %split_grads.1 = (f32[3,3,3,6,32]{4,3,2,1,0:T(8,128)}, f32[3,3,3,32,32]{4,3,2,1,0:T(8,128)}, f32[3,3,5,3,32]{4,3,2,1,0:T(4,128)}) custom-call(bf16[512,128]{1,0:T(8,128)(2,1)S(1)} %bitcast.41), custom_call_target="tpu_custom_call" | custom-call | tf_op jit(solution)/shard_map/split_grads/pallas_call | solution.py:658
  (36 shorter events, 1.0 us)
Async XLA Ops:
  1.6 10.9 %copy-start = (bf16[8,128,128]{2,1,0:T(8,128)(2,1)S(1)}, bf16[8,128,128]{2,1,0:T(8,128)(2,1)}, u32[]{:S(2)}) copy-start(bf16[8,128,128]{2,1,0:T(8,128)(2,1)} %prints.3) | copy-start | bytes 786436
  1.6 10.9 %copy-start.2 = (s32[64,128,2]{1,2,0:T(2,128)S(1)}, s32[64,128,2]{1,2,0:T(2,128)}, u32[]{:S(2)}) copy-start(s32[64,128,2]{1,2,0:T(2,128)} %param.12) | copy-start | bytes 196612
  1.6 10.9 %copy-start.3 = (s32[64,128,2]{1,2,0:T(2,128)S(1)}, s32[64,128,2]{1,2,0:T(2,128)}, u32[]{:S(2)}) copy-start(s32[64,128,2]{1,2,0:T(2,128)} %param.13) | copy-start | bytes 196612
  12.5 3.0 %copy-start.6 = (bf16[3,3,3,5,32]{4,2,3,1,0:T(4,128)(2,1)S(1)}, bf16[3,3,3,5,32]{4,2,3,1,0:T(4,128)(2,1)}, u32[]{:S(2)}) copy-start(bf16[3,3,3,5,32]{4,2,3,1,0:T(4,128)(2,1)} %param.16) | copy-start | bytes 25924
  14.5 5.6 %collective-permute-start = (bf16[624,128]{1,0:T(8,128)(2,1)S(1)}, bf16[624,128]{1,0:T(8,128)(2,1)S(1)}, u32[]{:S(2)}, u32[]{:S(2)}) collective-permute-start(bf16[624,128]{1,0:T(8,128)(2,1)S(1)} %get-tuple-element.19), channel_id=1, source_target_pairs={{0,4},{4,0},{8,12},{12,8},{16,20},{20,16},{24,28},{28,24},{32,36},... | collective-permute-start | bytes 479240 | tf_op jit(solution)/shard_map/ppermute | solution.py:561
  14.9 5.2 %collective-permute-start.1 = (bf16[624,128]{1,0:T(8,128)(2,1)S(1)}, bf16[624,128]{1,0:T(8,128)(2,1)S(1)}, u32[]{:S(2)}, u32[]{:S(2)}) collective-permute-start(bf16[624,128]{1,0:T(8,128)(2,1)S(1)} %get-tuple-element.20), channel_id=1, source_target_pairs={{0,0},{4,8},{8,4},{12,16},{16,12},{20,24},{24,20},{28,32},{32,28},... | collective-permute-start | bytes 479240 | tf_op jit(solution)/shard_map/ppermute | solution.py:560
  15.7 0.8 %copy-start.5 = (bf16[3,3,3,32,6]{3,4,2,1,0:T(8,128)(2,1)S(1)}, bf16[3,3,3,32,6]{3,4,2,1,0:T(8,128)(2,1)}, u32[]{:S(2)}) copy-start(bf16[3,3,3,32,6]{3,4,2,1,0:T(8,128)(2,1)} %param.14) | copy-start | bytes 31108
  15.7 0.9 %copy-start.4 = (bf16[3,3,3,32,32]{4,3,2,1,0:T(8,128)(2,1)S(1)}, bf16[3,3,3,32,32]{4,3,2,1,0:T(8,128)(2,1)}, u32[]{:S(2)}) copy-start(bf16[3,3,3,32,32]{4,3,2,1,0:T(8,128)(2,1)} %param.15) | copy-start | bytes 165892
  29.0 30.3 %all-to-all-start = ((bf16[256,2,128]{2,1,0:T(2,128)(2,1)}), bf16[256,2,128]{2,1,0:T(2,128)(2,1)S(1)}, u32[]{:S(2)}, u32[]{:S(2)}) async-start(bf16[256,2,128]{2,1,0:T(2,128)(2,1)} %bitcast.27), calls=%async_computation | async-start | bytes 262144 | tf_op jit(solution)/shard_map/all_to_all | solution.py:612
  46.5 0.9 %copy-start.1 = (f32[5,4,8,128]{3,2,1,0:T(8,128)S(1)}, f32[5,4,8,128]{3,2,1,0:T(8,128)}, u32[]{:S(2)}) copy-start(f32[5,4,8,128]{3,2,1,0:T(8,128)} %cot.1) | copy-start | bytes 245764
  48.7 18.6 %collective-permute-start.2 = (bf16[32,128]{1,0:T(8,128)(2,1)S(1)}, bf16[32,128]{1,0:T(8,128)(2,1)S(1)}, u32[]{:S(2)}, u32[]{:S(2)}) collective-permute-start(bf16[32,128]{1,0:T(8,128)(2,1)S(1)} %get-tuple-element.28), channel_id=1, source_target_pairs={{0,1},{1,2},{2,3},{3,0},{4,5},{5,6},{6,7},{7,4},{8,9},{9,10},{10,1... | collective-permute-start | bytes 24584 | tf_op jit(solution)/shard_map/ppermute | solution.py:629
  51.9 15.5 %collective-permute-start.3 = (bf16[32,128]{1,0:T(8,128)(2,1)S(1)}, bf16[32,128]{1,0:T(8,128)(2,1)S(1)}, u32[]{:S(2)}, u32[]{:S(2)}) collective-permute-start(bf16[32,128]{1,0:T(8,128)(2,1)S(1)} %get-tuple-element.28), channel_id=1, source_target_pairs={{0,2},{1,3},{2,0},{3,1},{4,6},{5,7},{6,4},{7,5},{8,10},{9,11},{10,... | collective-permute-start | bytes 24584 | tf_op jit(solution)/shard_map/ppermute | solution.py:629
  53.7 13.6 %collective-permute-start.4 = (bf16[32,128]{1,0:T(8,128)(2,1)S(1)}, bf16[32,128]{1,0:T(8,128)(2,1)S(1)}, u32[]{:S(2)}, u32[]{:S(2)}) collective-permute-start(bf16[32,128]{1,0:T(8,128)(2,1)S(1)} %get-tuple-element.28), channel_id=1, source_target_pairs={{0,3},{1,0},{2,1},{3,2},{4,7},{5,4},{6,5},{7,6},{8,11},{9,8},{10,9... | collective-permute-start | bytes 24584 | tf_op jit(solution)/shard_map/ppermute | solution.py:629
  60.1 20.1 %all-to-all-start.1 = ((bf16[256,2,128]{2,1,0:T(2,128)(2,1)}), bf16[256,2,128]{2,1,0:T(2,128)(2,1)S(1)}, u32[]{:S(2)}, u32[]{:S(2)}) async-start(bf16[256,2,128]{2,1,0:T(2,128)(2,1)} %bitcast.29), calls=%async_computation.1 | async-start | bytes 262144 | tf_op jit(solution)/shard_map/all_to_all | solution.py:640
